TPU v7x, 32 devices: a whole 2x2x4 slice. The times are simulated.
32 devices in a mesh: dp: 2 (over y), row: 4 (over z), col: 4 (over x, core).
Axes of the slice: x: 2, y: 2, z: 4, core: 2. Of those that a mesh axis runs over, the one named last changes fastest.
Arguments:
- tokens_in: bfloat16 [2, 4096, 1024], P(None, ('dp', 'row'), 'col'), may hold values from -6 to 6
- segments: int32 [2, 2, 2048], P(None, 'dp'), may hold values from 0 to 31, never falling along the last dimension, each value on 1 to 1024 neighbouring positions
- gain_attn: float32 [1024], P('col'), may hold values from 0.25 to 1.75
- gain_ffn: float32 [1024], P('col'), may hold values from 0.25 to 1.75
- w_heads: bfloat16 [1024, 160], P('col', 'row'), may hold values from -0.4375 to 0.4375
- w_ranks: bfloat16 [1024, 640], P('col', 'row'), may hold values from -0.1875 to 0.1875
- w_out: bfloat16 [1024, 1024], P('row', 'col'), may hold values from -0.75 to 0.75
- w_gate: bfloat16 [1024, 2816], P('col', 'row'), may hold values from -0.1875 to 0.1875
- w_up: bfloat16 [1024, 2816], P('col', 'row'), may hold values from -0.1875 to 0.1875
- w_down: bfloat16 [2816, 1024], P('row', 'col'), may hold values from -0.21875 to 0.21875
- cotangent: bfloat16 [2, 4096, 1024], P(None, ('dp', 'row'), 'col'), may hold values from -6 to 6
Outputs:
- output: bfloat16 [2, 4096, 1024], P(None, ('dp', 'row'), 'col')
- grad_input: float32 [2, 4096, 1024], P(None, ('dp', 'row'), 'col')
- grad_gain_attn: float32 [1024], P('col')
- grad_gain_ffn: float32 [1024], P('col')
- grad_w_heads: float32 [1024, 160], P('col', 'row')
- grad_w_ranks: float32 [1024, 640], P('col', 'row')
- grad_w_out: float32 [1024, 1024], P('row', 'col')
- grad_w_gate: float32 [1024, 2816], P('col', 'row')
- grad_w_up: float32 [1024, 2816], P('col', 'row')
- grad_w_down: float32 [2816, 1024], P('row', 'col')
Inputs may be any that keep to these rules, and one draw needn't show every extreme that they name: `segments`: document numbers count from 0 within each sequence of 2048 tokens, never fall, and a document holds 1 to 1024 tokens.
All inputs are finite; a program needn't handle non-finite values.
Results may differ from a plain program's by a relative error of at most 0.019.
The roundings to bfloat16 on the way count: a program that leaves them out, or rounds other values in their place, can miss the bound.
Values may be sent and summed in bfloat16 or wider, within the bound.
A program may use at most 128 MiB of HBM per device.

v0:
```python
import functools

import jax
import jax.numpy as jnp
from jax import lax
from jax.experimental import pallas as pl
from jax.experimental.pallas import tpu as pltpu
from jax.sharding import PartitionSpec as P

D = 1024
H = 16
HD = 64
RQ = 6
RK = 2
FAC = 10
MAX_DOC = 1024

EPS = 1e-06
ROPE = 10000.0
NEG = -1e30
BF = jnp.bfloat16
F32 = jnp.float32
LANES = 128
PAIRS = H // 2
FAC_ORDER = (6, 7, 8, 9, 0, 1, 2, 3, 4, 5)
FAC_BACK = (4, 5, 6, 7, 8, 9, 0, 1, 2, 3)
VMEM = pl.BlockSpec(memory_space=pltpu.VMEM)


def nn(a, b):
    return jnp.dot(a, b, preferred_element_type=F32)


def nt(a, b):
    return lax.dot_general(a, b, (((1,), (1,)), ((), ())), preferred_element_type=F32)


def tn(a, b):
    return lax.dot_general(a, b, (((0,), (0,)), ((), ())), preferred_element_type=F32)


def two_pass(a, b):
    high = a.astype(BF)
    low = (a - high.astype(F32)).astype(BF)
    return nn(high, b) + nn(low, b)


def lane_iota(shape):
    return lax.broadcasted_iota(jnp.int32, shape, len(shape) - 1)


def spread(rows, first, width):
    row = lax.broadcasted_iota(jnp.int32, (rows, width), 0)
    head = lax.broadcasted_iota(jnp.int32, (rows, width), 1) // HD
    return (row == head + first).astype(F32).astype(BF)


def collect(rows, width, first):
    head = lax.broadcasted_iota(jnp.int32, (rows, width), 0) // HD
    lane = lax.broadcasted_iota(jnp.int32, (rows, width), 1)
    return (lane == head + first).astype(F32).astype(BF)


GROUP = 4
GROUP_COLS = 48
RANK_COLS = FAC * HD
HEAD_COLS = H // GROUP * GROUP_COLS
ALL_COLS = RANK_COLS + HEAD_COLS


def factor_place(head, j):
    return head // GROUP * GROUP_COLS + j * GROUP + head % GROUP


def head_spread(j, first_head, width):
    row = lax.broadcasted_iota(jnp.int32, (HEAD_COLS, width), 0)
    head = lax.broadcasted_iota(jnp.int32, (HEAD_COLS, width), 1) // HD + first_head
    return (row == factor_place(head, j)).astype(F32).astype(BF)


def head_collect(j):
    head = lax.broadcasted_iota(jnp.int32, (D, HEAD_COLS), 0) // HD
    lane = lax.broadcasted_iota(jnp.int32, (D, HEAD_COLS), 1)
    return (lane == factor_place(head, j)).astype(F32).astype(BF)


def key_columns():
    row = lax.broadcasted_iota(jnp.int32, (HEAD_COLS, LANES), 0)
    lane = lax.broadcasted_iota(jnp.int32, (HEAD_COLS, LANES), 1)
    taken = (row == factor_place(lane % H, lane // H)) & (lane < 2 * RK * H)
    return taken.astype(F32).astype(BF)


def swap_halves(tile):
    lane = lane_iota(tile.shape)
    ahead = pltpu.roll(tile, LANES - HD // 2, 1)
    behind = pltpu.roll(tile, HD // 2, 1)
    return jnp.where(lane % HD < HD // 2, ahead, behind)


def double_left(tile):
    return jnp.where(lane_iota(tile.shape) < HD, tile, pltpu.roll(tile, HD, 1))


def double_right(tile):
    return jnp.where(lane_iota(tile.shape) < HD, pltpu.roll(tile, HD, 1), tile)


def params(**more):
    return pltpu.CompilerParams(vmem_limit_bytes=60 << 20, **more)


def call(body, outs, scratch=(), cost=None):
    return pl.pallas_call(
        body,
        out_shape=outs,
        scratch_shapes=scratch,
        compiler_params=params(),
        cost_estimate=cost,
    )


def cost_of(flops, moved):
    return pl.CostEstimate(flops=int(flops), bytes_accessed=int(moved), transcendentals=0)


MESH = pl.DeviceIdType.MESH
ANY = pl.BlockSpec(memory_space=pl.ANY)


class Mover:
    def __init__(self, send_sem, recv_sem):
        self.send_sem = send_sem
        self.recv_sem = recv_sem
        self.used = 0

    def copy(self, source, target, **place):
        index = self.used
        self.used += 1
        return pltpu.make_async_remote_copy(
            src_ref=source,
            dst_ref=target,
            send_sem=self.send_sem.at[index],
            recv_sem=self.recv_sem.at[index],
            device_id=place,
            device_id_type=MESH,
        )


def greet(partners):
    barrier = pltpu.get_barrier_semaphore()
    count = 0
    for present, place in partners:
        if present is None:
            pl.semaphore_signal(barrier, inc=1, device_id=place, device_id_type=MESH)
            count = count + 1
        else:

            @pl.when(present)
            def _():
                pl.semaphore_signal(barrier, inc=1, device_id=place, device_id_type=MESH)

            count = count + present.astype(jnp.int32)
    pl.semaphore_wait(barrier, count)


def neighbours():
    col = lax.axis_index("col")
    core = col + 1 - 2 * lax.rem(col, 2)
    across = lax.rem(col + 2, 4)
    return col, core, across


def square():
    dp = lax.axis_index("dp")
    x = lax.axis_index("col") // 2
    return dp, (dp * 2 + x, dp * 2 + 1 - x, (1 - dp) * 2 + x, (1 - dp) * 2 + 1 - x)


def comm_params(ident):
    return params(collective_id=ident, has_side_effects=True)


class AttendCopies:
    def __init__(self, w_ref, cot_ref, rows_ref, near_ref, mixes_ref, send_sem, recv_sem):
        row = lax.axis_index("row")
        col, core, across = neighbours()
        dp, (me, on_x, on_y, _) = square()
        mover = Mover(send_sem, recv_sem)
        self.left = row >= 1
        self.right = row <= 2
        self.both = jnp.logical_and(self.left, self.right)
        self.from_left = row >= 2
        self.from_right = row <= 1
        self.partners = [
            (self.right, {"row": row + 1}),
            (self.left, {"row": row - 1}),
            (None, {"col": across}),
            (None, {"col": core}),
            (None, {"dp": 1 - dp}),
        ]
        self.to_right = mover.copy(w_ref, rows_ref.at[row], row=row + 1)
        self.to_left = mover.copy(w_ref, rows_ref.at[row], row=row - 1)
        self.pass_right = mover.copy(rows_ref.at[row - 1], rows_ref.at[row - 1], row=row + 1)
        self.pass_left = mover.copy(rows_ref.at[row + 1], rows_ref.at[row + 1], row=row - 1)
        half = cot_ref.shape[0] // 2
        top, low = pl.ds(0, half), pl.ds(half, half)
        self.cots = [
            mover.copy(cot_ref.at[low], near_ref.at[me, low], col=across),
            mover.copy(cot_ref.at[top], near_ref.at[me, top], dp=1 - dp),
            mover.copy(cot_ref.at[top], near_ref.at[me, top], col=across),
            mover.copy(cot_ref.at[low], near_ref.at[me, low], dp=1 - dp),
        ]
        self.relays = [
            mover.copy(near_ref.at[on_x, low], near_ref.at[on_x, low], dp=1 - dp),
            mover.copy(near_ref.at[on_y, top], near_ref.at[on_y, top], col=across),
        ]
        self.mixes = []
        for r in range(4):
            for c in (col, across):
                self.mixes.append(mover.copy(mixes_ref.at[r, c], mixes_ref.at[r, c], col=core))

    def first(self):
        greet(self.partners)
        pl.when(self.right)(self.to_right.start)
        pl.when(self.left)(self.to_left.start)
        for c in self.cots + self.mixes:
            c.start()

    def second(self):
        for c in self.cots[:2]:
            c.wait_recv()
        for c in self.relays:
            c.start()
        pl.when(self.left)(self.to_right.wait_recv)
        pl.when(self.right)(self.to_left.wait_recv)
        pl.when(self.both)(self.pass_right.start)
        pl.when(self.both)(self.pass_left.start)

    def last(self):
        pl.when(self.right)(self.to_right.wait_send)
        pl.when(self.left)(self.to_left.wait_send)
        pl.when(self.both)(self.pass_right.wait_send)
        pl.when(self.both)(self.pass_left.wait_send)
        pl.when(self.from_left)(self.pass_right.wait_recv)
        pl.when(self.from_right)(self.pass_left.wait_recv)
        for c in self.cots[:2]:
            c.wait_send()
        for c in self.cots[2:] + self.relays + self.mixes:
            c.wait()


class BackCopies:
    def __init__(self, refs, sems):
        (
            self.pair_ref, self.mixed_ref, self.rows_ref, self.g_out_ref,
            self.out_ref, self.ends_ref, self.part_ref,
            self.relay_ref, self.diag_ref, self.far_ref, self.send_ref,
            self.right_ref, self.left_ref, self.got_ref,
            self.near_ref, self.side_ref, self.across_ref,
            self.pieces_ref, self.mine_ref, self.rows_in_ref, self.g_in_ref,
        ) = refs
        send_sem, recv_sem, local_sem = sems
        self.row = row = lax.axis_index("row")
        self.col, core, across = col, _, _ = neighbours()
        cross = lax.rem(core + 2, 4)
        self.dp, self.spots = dp, (me, on_x, on_y, on_both) = square()
        mover = Mover(send_sem, recv_sem)
        self.x, self.mine = x, mine = col // 2, lax.rem(col, 2)
        self.partners = [(None, {"col": c}) for c in (core, across, cross)]
        self.partners += [(None, {"dp": 1 - dp}), (row <= 2, {"row": row + 1}), (row >= 1, {"row": row - 1})]
        half = self.pair_ref.shape[1] // 2
        top, low = pl.ds(0, half), pl.ds(half, half)
        y = 1 - dp
        self.diag = [
            mover.copy(self.pair_ref.at[on_both, top], self.diag_ref.at[0], col=across),
            mover.copy(self.pair_ref.at[on_both, low], self.diag_ref.at[1], dp=y),
        ]
        self.far = [
            mover.copy(self.pair_ref.at[on_x, top], self.far_ref.at[0, top], col=across),
            mover.copy(self.pair_ref.at[on_y, low], self.far_ref.at[1, low], dp=y),
            mover.copy(self.relay_ref.at[0], self.far_ref.at[1, top], dp=y),
            mover.copy(self.relay_ref.at[1], self.far_ref.at[0, low], col=across),
        ]
        self.out = [mover.copy(self.send_ref.at[c], self.out_ref.at[col], col=c) for c in (across, cross, core)]
        self.own = pltpu.make_async_copy(self.send_ref.at[col], self.out_ref.at[col], local_sem.at[0])
        self.hop_right = [
            mover.copy(self.rows_ref.at[3], self.got_ref.at[0], row=row + 1),
            mover.copy(self.right_ref.at[0], self.got_ref.at[1], row=row + 1),
            mover.copy(self.right_ref.at[1], self.ends_ref.at[0], row=row + 1),
        ]
        self.hop_left = [
            mover.copy(self.rows_ref.at[0], self.got_ref.at[0], row=row - 1),
            mover.copy(self.left_ref.at[0], self.got_ref.at[2], row=row - 1),
            mover.copy(self.left_ref.at[1], self.ends_ref.at[1], row=row - 1),
        ]
        self.cores = [
            mover.copy(self.g_out_ref.at[r, k * 2 + 1 - mine], self.near_ref.at[k, r], col=core)
            for k in range(2)
            for r in range(4)
        ]
        self.sides = [mover.copy(self.side_ref.at[r], self.across_ref.at[r], col=across) for r in range(4)]
        self.loads = [
            pltpu.make_async_copy(self.pair_ref.at[on_y, top], self.pieces_ref.at[0], local_sem.at[1]),
            pltpu.make_async_copy(self.pair_ref.at[on_x, low], self.pieces_ref.at[1], local_sem.at[2]),
            pltpu.make_async_copy(self.pair_ref.at[me], self.mine_ref, local_sem.at[3]),
            pltpu.make_async_copy(self.rows_ref, self.rows_in_ref, local_sem.at[4]),
        ]
        self.g_loads = [
            pltpu.make_async_copy(
                self.g_out_ref.at[r, lax.rem(x + k, 2) * 2 + mine], self.g_in_ref.at[k, r], local_sem.at[5 + 4 * k + r]
            )
            for k in range(2)
            for r in range(4)
        ]

    def first(self):
        row = self.row
        greet(self.partners)
        for c in self.diag + self.far[:2] + self.cores:
            c.start()
        pl.when(row == 0)(self.hop_right[0].start)
        pl.when(row == 3)(self.hop_left[0].start)
        for c in self.loads + self.g_loads:
            c.start()

    def cross_x(self):
        for c in self.g_loads:
            c.wait()
        for c in self.cores:
            c.wait_recv()
        for r in range(4):
            self.side_ref[r] = (
                self.g_in_ref[1, r].astype(F32) + self.near_ref[1 - self.x, r].astype(F32)
            ).astype(BF)
            self.sides[r].start()

    def second(self):
        row = self.row
        for c in self.loads:
            c.wait()
        pl.when(row == 1)(self.hop_right[0].wait_recv)
        pl.when(row == 2)(self.hop_left[0].wait_recv)
        hop = self.got_ref[0].astype(F32)
        ahead = self.rows_in_ref[jnp.minimum(row + 2, 3)].astype(F32)
        self.right_ref[0] = jnp.where(row == 1, ahead + hop, ahead).astype(BF)
        behind = self.rows_in_ref[jnp.maximum(row - 2, 0)].astype(F32)
        self.left_ref[0] = jnp.where(row == 2, behind + hop, behind).astype(BF)
        pl.when(row <= 1)(self.hop_right[1].start)
        pl.when(row >= 2)(self.hop_left[1].start)
        for k in range(2):
            self.diag[k].wait_recv()
            self.relay_ref[k] = (self.pieces_ref[k].astype(F32) + self.diag_ref[k].astype(F32)).astype(BF)
            self.far[2 + k].start()

    def third(self):
        row = self.row
        middle = jnp.logical_and(row >= 1, row <= 2)
        pl.when(middle)(self.hop_right[1].wait_recv)
        pl.when(middle)(self.hop_left[1].wait_recv)
        ahead = self.rows_in_ref[jnp.minimum(row + 1, 3)].astype(F32)
        behind = self.rows_in_ref[jnp.maximum(row - 1, 0)].astype(F32)
        self.right_ref[1] = jnp.where(row >= 1, ahead + self.got_ref[1].astype(F32), ahead).astype(BF)
        self.left_ref[1] = jnp.where(row <= 2, behind + self.got_ref[2].astype(F32), behind).astype(BF)
        pl.when(row <= 2)(self.hop_right[2].start)
        pl.when(row >= 1)(self.hop_left[2].start)
        for c in self.far:
            c.wait_recv()
        feat = self.send_ref.shape[2]
        for c in range(4):
            lanes = slice(c * feat, (c + 1) * feat)
            self.send_ref[c] = (
                self.mixed_ref[:, lanes]
                + self.mine_ref[:, lanes].astype(F32)
                + self.far_ref[0, :, lanes].astype(F32)
                + self.far_ref[1, :, lanes].astype(F32)
            ).astype(BF)
        for c in self.out:
            c.start()
        self.own.start()

    def last(self):
        row = self.row
        for r in range(4):
            self.sides[r].wait_recv()
            self.part_ref[r] = (
                self.g_in_ref[0, r].astype(F32)
                + self.near_ref[self.x, r].astype(F32)
                + self.across_ref[r].astype(F32)
            ).astype(BF)
        for c in self.out:
            c.wait()
        self.own.wait()
        for c in self.diag + self.far + self.cores + self.sides:
            c.wait_send()
        pl.when(row == 0)(self.hop_right[0].wait_send)
        pl.when(row == 3)(self.hop_left[0].wait_send)
        pl.when(row <= 1)(self.hop_right[1].wait_send)
        pl.when(row >= 2)(self.hop_left[1].wait_send)
        pl.when(row <= 2)(self.hop_right[2].wait_send)
        pl.when(row >= 1)(self.hop_left[2].wait_send)
        pl.when(row >= 1)(self.hop_right[2].wait_recv)
        pl.when(row <= 2)(self.hop_left[2].wait_recv)


def first_norm(x_ref, gain_ref, h_ref):
    parts = x_ref.shape[0]
    feat = x_ref.shape[2]
    xs = [x_ref[c].astype(F32) for c in range(parts)]
    total = sum(jnp.sum(v * v, axis=1, keepdims=True) for v in xs)
    scale = lax.rsqrt(total / D + EPS)
    for c in range(parts):
        lanes = slice(c * feat, (c + 1) * feat)
        h_ref[:, lanes] = (xs[c] * scale * gain_ref[c, :1]).astype(BF)


def place_factor_weights(blocks_ref, w_ref):
    n_row, parts, _, feat = blocks_ref.shape
    ranks_each = RANK_COLS // n_row
    for c in range(parts):
        lanes = slice(c * feat, (c + 1) * feat)
        for r in range(n_row):
            w_ref[r * ranks_each : (r + 1) * ranks_each, lanes] = blocks_ref[r, c, :ranks_each]
            w_ref[RANK_COLS + r * GROUP_COLS : RANK_COLS + (r + 1) * GROUP_COLS, lanes] = blocks_ref[
                r, c, ranks_each:
            ]


def make_factors(h_ref, w_ref, turn_ref, hf_ref, bq_ref, kf_ref):
    both = nt(h_ref[...], w_ref[...])
    heads = both[:, RANK_COLS:]
    hf_ref[...] = heads
    cosine = turn_ref[:, :LANES]
    sine = turn_ref[:, LANES:]
    for tile in range(RANK_COLS // LANES):
        lanes = slice(tile * LANES, (tile + 1) * LANES)
        part = both[:, lanes]
        if tile < 4:
            part = part * cosine + swap_halves(part) * sine
        if tile < 3:
            bq_ref[:, lanes] = part
        else:
            kf_ref[:, (tile - 3) * LANES : (tile - 2) * LANES] = part.astype(BF)
    kf_ref[:, 2 * LANES :] = nn(heads.astype(BF), key_columns()).astype(BF)


def make_queries(hf_ref, bq_ref, q_ref):
    heads = hf_ref[...]
    high = heads.astype(BF)
    low = (heads - high.astype(F32)).astype(BF)
    ranks = []
    for r in range(RQ):
        tile = bq_ref[:, (r // 2) * LANES : (r // 2 + 1) * LANES]
        ranks.append(double_left(tile) if r % 2 == 0 else double_right(tile))
    width = 2 * LANES
    for p in range(D // width):
        lanes = slice(p * width, (p + 1) * width)
        acc = None
        for r in range(RQ):
            pick = head_spread(2 * RK + r, p * (width // HD), width)
            term = (nn(high, pick) + nn(low, pick)) * jnp.concatenate([ranks[r]] * 2, axis=1)
            acc = term if acc is None else acc + term
        q_ref[:, lanes] = (acc / RQ).astype(BF)


def front_body(x_ref, gain_ref, blocks_ref, turn_ref, h_ref, hf_ref, bq_ref, kf_ref, q_ref, w_ref):
    first_norm(x_ref, gain_ref, h_ref)
    place_factor_weights(blocks_ref, w_ref)
    make_factors(h_ref, w_ref, turn_ref, hf_ref, bq_ref, kf_ref)
    make_queries(hf_ref, bq_ref, q_ref)


def head_body(
    tok_ref, w_own_ref, gain_ref, ffn_ref, mix_ref, turn_ref,
    x_ref, gains_ref, parts_ref, mixes_ref, h_ref, hf_ref, bq_ref, q_ref, w_ref, win_ref,
    blocks_ref, send_sem, recv_sem,
):
    row = lax.axis_index("row")
    col, core, across = neighbours()
    cross = lax.rem(core + 2, 4)
    side = lax.rem(col, 2)
    rows = [lax.rem(row + k, 4) for k in range(4)]
    back = [lax.rem(row + 4 - k, 4) for k in range(4)]
    greet([(None, {"col": c}) for c in (core, across, cross)] + [(None, {"row": r}) for r in rows[1:]])
    mover = Mover(send_sem, recv_sem)
    started = []

    def go(source, target, **place):
        c = mover.copy(source, target, **place)
        c.start()
        started.append(c)
        return c

    down = [None] + [go(w_own_ref, blocks_ref.at[row, col], row=rows[k]) for k in range(1, 4)]
    sides = [go(w_own_ref, blocks_ref.at[row, col], col=across)]
    cores = [go(w_own_ref, blocks_ref.at[row, col], col=core)]
    toks = []
    rest = []
    for c in (across, cross, core):
        toks.append(go(gain_ref, gains_ref.at[col], col=c))
        toks.append(go(tok_ref.at[c], x_ref.at[col], col=c))
    mix_down = [None] + [go(mix_ref, mixes_ref.at[row, col], row=rows[k]) for k in range(1, 4)]
    blocks_ref[row, col] = w_own_ref[...]
    gains_ref[col] = gain_ref[...]
    x_ref[col] = tok_ref[col]
    parts_ref[col] = ffn_ref[col]
    mixes_ref[row, col] = mix_ref[...]
    zero = jnp.zeros(win_ref.shape[1:], BF)
    has_one = row >= 1
    has_two = row >= 2
    for absent, slot in (
        (jnp.logical_not(has_two), 0),
        (jnp.logical_and(jnp.logical_not(has_two), side == 0), 1),
        (jnp.logical_and(jnp.logical_not(has_one), side == 1), 1),
        (jnp.logical_not(has_one), 2),
        (jnp.logical_and(jnp.logical_not(has_one), side == 0), 3),
    ):

        @pl.when(absent)
        def _():
            win_ref[slot] = zero

    for k in range(1, 4):
        down[k].wait_recv()
        block = blocks_ref.at[back[k], col]
        sides.append(go(block, block, col=across))
        cores.append(go(block, block, col=core))
    for c in (across, cross, core):
        rest.append(go(ffn_ref.at[c], parts_ref.at[col], col=c))
    for c in toks:
        c.wait_recv()
    first_norm(x_ref, gains_ref, h_ref)
    passed = []
    for k in range(4):
        sides[k].wait_recv()
        block = blocks_ref.at[back[k], across]
        passed.append(go(block, block, col=core))
    for c in cores + passed:
        c.wait_recv()
    for k in range(4):
        if k > 0:
            mix_down[k].wait_recv()
        block = mixes_ref.at[back[k], col]
        rest.append(go(block, block, col=across))
    place_factor_weights(blocks_ref, w_ref)
    make_factors(h_ref, w_ref, turn_ref, hf_ref, bq_ref, win_ref.at[4])

    own = win_ref.at[4]
    one = mover.copy(own, win_ref.at[2], row=row + 1)
    two = mover.copy(win_ref.at[2], win_ref.at[0], row=row + 1)
    near = mover.copy(own, win_ref.at[3], col=core)
    pass_one = mover.copy(win_ref.at[2], win_ref.at[1 + 2 * side], col=core)
    pass_two = mover.copy(win_ref.at[0], win_ref.at[1], col=core)
    hands_on = jnp.logical_and(has_one, row <= 2)
    sends_two = jnp.logical_and(has_two, side == 1)
    takes_two = jnp.logical_and(has_two, side == 0)
    pl.when(row <= 2)(one.start)
    pl.when(side == 0)(near.start)

    @pl.when(has_one)
    def _():
        one.wait_recv()
        pass_one.start()

    pl.when(hands_on)(two.start)
    make_queries(hf_ref, bq_ref, q_ref)

    @pl.when(has_two)
    def _():
        two.wait_recv()

    pl.when(sends_two)(pass_two.start)

    @pl.when(has_one)
    def _():
        pass_one.wait_recv()
        pass_one.wait_send()

    pl.when(takes_two)(pass_two.wait_recv)
    pl.when(sends_two)(pass_two.wait_send)
    pl.when(side == 1)(near.wait_recv)
    pl.when(side == 0)(near.wait_send)
    pl.when(row <= 2)(one.wait_send)
    pl.when(hands_on)(two.wait_send)
    for c in rest:
        c.wait_recv()
    for c in started:
        c.wait_send()


def head(tok, w_own, gains, ffn_own, w_out, turn):
    rows, feat = tok.shape[1:]
    count = 3 + 4 + 4 + 6 + 3 + 3 + 4 + 4 + 5
    return pl.pallas_call(
        head_body,
        out_shape=(
            jax.ShapeDtypeStruct(tok.shape, BF),
            jax.ShapeDtypeStruct((4,) + gains.shape, F32),
            jax.ShapeDtypeStruct(ffn_own.shape, BF),
            jax.ShapeDtypeStruct((4, 4) + w_out.shape, BF),
            jax.ShapeDtypeStruct((rows, D), BF),
            jax.ShapeDtypeStruct((rows, HEAD_COLS), F32),
            jax.ShapeDtypeStruct((rows, RQ * HD), F32),
            jax.ShapeDtypeStruct((rows, D), BF),
            jax.ShapeDtypeStruct((ALL_COLS, D), BF),
            jax.ShapeDtypeStruct((5, rows, 3 * LANES), BF),
        ),
        in_specs=[VMEM] * 6,
        out_specs=(VMEM,) * 10,
        scratch_shapes=[
            pltpu.VMEM((4, 4) + w_own.shape, BF),
            pltpu.SemaphoreType.DMA((count,)),
            pltpu.SemaphoreType.DMA((count,)),
        ],
        compiler_params=comm_params(1),
        cost_estimate=cost_of(2 * rows * D * 800 * 3, 14 << 20),
    )(tok, w_own, gains, ffn_own, w_out, turn)


def front(x_parts, gains, blocks, turn):
    rows = x_parts.shape[1]
    return call(
        front_body,
        (
            jax.ShapeDtypeStruct((rows, D), BF),
            jax.ShapeDtypeStruct((rows, HEAD_COLS), F32),
            jax.ShapeDtypeStruct((rows, RQ * HD), F32),
            jax.ShapeDtypeStruct((rows, 3 * LANES), BF),
            jax.ShapeDtypeStruct((rows, D), BF),
            jax.ShapeDtypeStruct((ALL_COLS, D), BF),
        ),
        cost=cost_of(2 * rows * D * 800 * 3, 6 << 20),
    )(x_parts, gains, blocks, turn)


def mask_bias(seg_ref, keys, rows):
    seg_row = seg_ref[...].astype(F32)
    wide = jnp.broadcast_to(seg_row, (LANES, keys))
    column = wide.T
    column = jnp.concatenate([column] * (rows // LANES), axis=1)
    key_idx = lax.broadcasted_iota(jnp.int32, (keys, rows), 0)
    query_idx = lax.broadcasted_iota(jnp.int32, (keys, rows), 1) + (keys - rows)
    same = column == seg_row[:, keys - rows :]
    return jnp.where(same & (key_idx <= query_idx), 0.0, NEG)


def attend_body(fast, q_ref, kf_ref, seg_ref, *refs):
    if fast:
        w_ref, cot_ref, _, o_ref, lse_ref, k_ref, v_ref, w_rows_ref, cot_near_ref, mixes_ref = refs[:10]
        bias_ref, dup_ref, send_sem, recv_sem = refs[10:]
        side_work = AttendCopies(w_ref, cot_ref, w_rows_ref, cot_near_ref, mixes_ref, send_sem, recv_sem)
        side_work.first()
    else:
        o_ref, lse_ref, k_ref, v_ref, bias_ref, dup_ref = refs
    rows = q_ref.shape[0]
    keys = kf_ref.shape[0]
    bias_ref[...] = mask_bias(seg_ref, keys, rows)
    for s in range(2 * RK):
        tile = kf_ref[:, (s // 2) * LANES : (s // 2 + 1) * LANES].astype(F32)
        dup_ref[s] = double_left(tile) if s % 2 == 0 else double_right(tile)

    def pair(p, carried):
        if fast:
            pl.when(p == 4)(side_work.second)
        lanes = pl.ds(pl.multiple_of(p * LANES, LANES), LANES)
        weights = kf_ref[:, 2 * LANES :]
        made = []
        for kind in range(2):
            acc = None
            for s in range(RK):
                pick = spread(LANES, (kind * RK + s) * H + 2 * p, LANES)
                term = nn(weights, pick) * dup_ref[kind * RK + s]
                acc = term if acc is None else acc + term
            made.append((acc / RK).astype(BF))
        k_tile, v_tile = made
        k_ref[:, lanes] = k_tile
        v_ref[:, lanes] = v_tile
        v_turned = v_tile.astype(F32).T.astype(BF)
        q_turned = (q_ref[:, lanes].astype(F32) * HD**-0.5).T
        half = lax.broadcasted_iota(jnp.int32, q_turned.shape, 0) // HD
        outs = []
        for side in range(2):
            q_side = jnp.where(half == side, q_turned, 0.0).astype(BF)
            scores = nn(k_tile, q_side) + bias_ref[...]
            peak = jnp.max(scores, axis=0, keepdims=True)
            weight = jnp.exp(scores - peak)
            total = jnp.sum(weight, axis=0, keepdims=True)
            probs = (weight * (1.0 / total)).astype(BF)
            outs.append(nn(v_turned[side * HD : (side + 1) * HD], probs))
            lse_ref[2 * p + side] = jnp.broadcast_to(peak + jnp.log(total), (8, rows))
        o_ref[:, lanes] = jnp.concatenate(outs, axis=0).T.astype(BF)
        return carried

    lax.fori_loop(0, PAIRS, pair, 0)
    if fast:
        side_work.last()


def attend(q, kf_window, seg_window, w_own=None, cot=None, mixes=None):
    rows = q.shape[0]
    keys = kf_window.shape[0]
    fast = w_own is not None
    outs = [
        jax.ShapeDtypeStruct((rows, D), BF),
        jax.ShapeDtypeStruct((H, 8, rows), F32),
        jax.ShapeDtypeStruct((keys, D), BF),
        jax.ShapeDtypeStruct((keys, D), BF),
    ]
    scratch = [pltpu.VMEM((keys, rows), F32), pltpu.VMEM((2 * RK, keys, LANES), F32)]
    in_specs, out_specs, more = [VMEM] * 3, [VMEM] * 4, []
    if fast:
        outs += [
            jax.ShapeDtypeStruct((4,) + w_own.shape, BF),
            jax.ShapeDtypeStruct((4,) + cot.shape, BF),
            jax.ShapeDtypeStruct(mixes.shape, BF),
        ]
        in_specs += [ANY] * 3
        out_specs += [ANY] * 3
        more = [w_own, cot, mixes]
        scratch += [
            pltpu.SemaphoreType.DMA((18,)),
            pltpu.SemaphoreType.DMA((18,)),
        ]
    return pl.pallas_call(
        functools.partial(attend_body, fast),
        out_shape=tuple(outs),
        in_specs=in_specs,
        out_specs=tuple(out_specs),
        scratch_shapes=scratch,
        input_output_aliases={5: 6} if fast else {},
        compiler_params=comm_params(3) if fast else params(),
        cost_estimate=cost_of(2 * rows * keys * D * 16, 16 << 20),
    )(q, kf_window, seg_window, *more)


def attend_back_body(fast, q_ref, k_ref, v_ref, do_ref, lse_ref, kf_ref, seg_ref, *refs):
    if fast:
        dq_ref, dkf_ref = refs[4:6]
        bias_ref, dup_ref, sum_ref, fac_ref = refs[9:13]
        side_work = BackCopies(refs[:4] + refs[6:9] + refs[13:27], refs[27:])
        side_work.first()
    else:
        dq_ref, dkf_ref, bias_ref, dup_ref, sum_ref, fac_ref = refs
    rows = q_ref.shape[0]
    keys = kf_ref.shape[0]
    bias_ref[...] = mask_bias(seg_ref, keys, rows)
    for s in range(2 * RK):
        tile = kf_ref[:, (s // 2) * LANES : (s // 2 + 1) * LANES].astype(F32)
        dup_ref[s] = double_left(tile) if s % 2 == 0 else double_right(tile)
    sum_ref[...] = jnp.zeros_like(sum_ref)
    fac_ref[...] = jnp.zeros_like(fac_ref)

    def pair(p, carried):
        if fast:
            pl.when(p == 1)(side_work.cross_x)
            pl.when(p == 3)(side_work.second)
            pl.when(p == 6)(side_work.third)
        lanes = pl.ds(pl.multiple_of(p * LANES, LANES), LANES)
        k_tile = k_ref[:, lanes]
        v_tile = v_ref[:, lanes]
        k_turned = k_tile.astype(F32).T.astype(BF)
        q_tile = q_ref[:, lanes].astype(F32) * HD**-0.5
        do_tile = do_ref[:, lanes].astype(F32)
        q_turned = q_tile.T
        do_turned = do_tile.T
        half = lax.broadcasted_iota(jnp.int32, q_turned.shape, 0) // HD
        lane_half = lax.broadcasted_iota(jnp.int32, q_tile.shape, 1) // HD
        d_k = None
        d_v = None
        d_q = []
        for side in range(2):
            q_side = jnp.where(half == side, q_turned, 0.0).astype(BF)
            do_side = jnp.where(half == side, do_turned, 0.0).astype(BF)
            scores = nn(k_tile, q_side) + bias_ref[...]
            probs = jnp.exp(scores - lse_ref[2 * p + side][:1])
            d_prob = nn(v_tile, do_side)
            delta = jnp.sum(probs * d_prob, axis=0, keepdims=True)
            d_score = (probs * (d_prob - delta)).astype(BF)
            d_q.append(nn(k_turned[side * HD : (side + 1) * HD], d_score))
            q_back = jnp.where(lane_half == side, q_tile, 0.0).astype(BF)
            do_back = jnp.where(lane_half == side, do_tile, 0.0).astype(BF)
            part_k = nn(d_score, q_back)
            part_v = nn(probs.astype(BF), do_back)
            d_k = part_k if d_k is None else d_k + part_k
            d_v = part_v if d_v is None else d_v + part_v
        dq_ref[:, lanes] = jnp.concatenate(d_q, axis=0).T * HD**-0.5
        weights = kf_ref[:, 2 * LANES :]
        for kind, grad in ((0, d_k), (1, d_v)):
            for s in range(RK):
                slot = kind * RK + s
                pick = spread(LANES, slot * H + 2 * p, LANES)
                sum_ref[slot] += nn(weights, pick) * grad
                fac_ref[...] += two_pass(grad * dup_ref[slot], collect(LANES, LANES, slot * H + 2 * p))
        return carried

    lax.fori_loop(0, PAIRS, pair, 0)
    for tile in range(2):
        first = sum_ref[2 * tile]
        second = sum_ref[2 * tile + 1]
        first = first + pltpu.roll(first, HD, 1)
        second = second + pltpu.roll(second, HD, 1)
        merged = jnp.where(lane_iota(first.shape) < HD, first, second)
        dkf_ref[:, tile * LANES : (tile + 1) * LANES] = (merged / RK).astype(BF)
    dkf_ref[:, 2 * LANES :] = (fac_ref[...] / RK).astype(BF)
    if fast:
        side_work.last()


def attend_back(q, k, v, d_heads, lse, kf_window, seg_window, *more):
    rows = q.shape[0]
    keys = kf_window.shape[0]
    fast = len(more) > 0
    outs = [jax.ShapeDtypeStruct((rows, D), F32), jax.ShapeDtypeStruct(kf_window.shape, BF)]
    scratch = [
        pltpu.VMEM((keys, rows), F32),
        pltpu.VMEM((2 * RK, keys, LANES), F32),
        pltpu.VMEM((2 * RK, keys, LANES), F32),
        pltpu.VMEM((keys, LANES), F32),
    ]
    in_specs, out_specs = [VMEM] * 7, [VMEM] * 2
    if fast:
        in_specs += [ANY, VMEM, ANY, ANY]
        grads, g_out = more[2], more[3]
        parts, feat = g_out.shape[1], g_out.shape[3]
        block, hop = g_out.shape[2:], grads.shape[1:]
        outs += [
            jax.ShapeDtypeStruct((parts, rows, feat), BF),
            jax.ShapeDtypeStruct((2,) + hop, BF),
            jax.ShapeDtypeStruct((4,) + block, BF),
        ]
        out_specs += [ANY, ANY, VMEM]
        scratch += [
            pltpu.VMEM((2, rows // 2, D), BF),
            pltpu.VMEM((2, rows // 2, D), BF),
            pltpu.VMEM((2, rows, D), BF),
            pltpu.VMEM((parts, rows, feat), BF),
            pltpu.VMEM((2,) + hop, BF),
            pltpu.VMEM((2,) + hop, BF),
            pltpu.VMEM((3,) + hop, BF),
            pltpu.VMEM((2, 4) + block, BF),
            pltpu.VMEM((4,) + block, BF),
            pltpu.VMEM((4,) + block, BF),
            pltpu.VMEM((2, rows // 2, D), BF),
            pltpu.VMEM((rows, D), BF),
            pltpu.VMEM(grads.shape, BF),
            pltpu.VMEM((2, 4) + block, BF),
            pltpu.SemaphoreType.DMA((27,)),
            pltpu.SemaphoreType.DMA((27,)),
            pltpu.SemaphoreType.DMA((13,)),
        ]
    return pl.pallas_call(
        functools.partial(attend_back_body, fast),
        out_shape=tuple(outs),
        in_specs=in_specs,
        out_specs=tuple(out_specs),
        scratch_shapes=scratch,
        compiler_params=comm_params(6) if fast else params(),
        cost_estimate=cost_of(2 * rows * keys * D * 40, 16 << 20),
    )(q, k, v, d_heads, lse, kf_window, seg_window, *more)


def mixing_body(x_ref, heads_ref, w_out_ref, gain_ref, mixed_ref, h_ref):
    parts, _, feat = x_ref.shape
    rows_of = w_out_ref.shape[0]
    head_rows = w_out_ref.shape[2]
    total = None
    for c in range(parts):
        lanes = slice(c * feat, (c + 1) * feat)
        acc = x_ref[c].astype(F32)
        for r in range(rows_of):
            acc = acc + nn(heads_ref[:, r * head_rows : (r + 1) * head_rows], w_out_ref[r, c])
        mixed_ref[:, lanes] = acc
        part = jnp.sum(acc * acc, axis=1, keepdims=True)
        total = part if total is None else total + part
    scale = lax.rsqrt(total / D + EPS)
    for c in range(parts):
        lanes = slice(c * feat, (c + 1) * feat)
        h_ref[:, lanes] = (mixed_ref[:, lanes] * scale * gain_ref[c, 1:2]).astype(BF)


def mixing(x_parts, heads, w_out, gains):
    rows = heads.shape[0]
    return call(
        mixing_body,
        (jax.ShapeDtypeStruct((rows, D), F32), jax.ShapeDtypeStruct((rows, D), BF)),
        cost=cost_of(2 * rows * D * D, 5 << 20),
    )(x_parts, heads, w_out, gains)


def ffn_steps(blocks, h_at, cot_at, w_ref, hid_ref, dg_ref, du_ref, out_at, back_at):
    def block(t, carried):
        h = h_at(t)[...]
        gate = nt(h, w_ref[0])
        up = nt(h, w_ref[1])
        d_hidden = nt(cot_at(t)[...], w_ref[2])
        sig = 1.0 / (1.0 + jnp.exp(-gate))
        silu = gate * sig
        hidden = (silu * up).astype(BF)
        d_gate = (d_hidden * up * sig * (1.0 + gate * (1.0 - sig))).astype(BF)
        d_up = (d_hidden * silu).astype(BF)
        rows = h.shape[0]
        place = pl.ds(pl.multiple_of(t * rows, rows), rows)
        hid_ref[place] = hidden
        dg_ref[place] = d_gate
        du_ref[place] = d_up
        out_at(t)[...] = nn(hidden, w_ref[2]).astype(BF)
        back_at(t)[...] = (nn(d_gate, w_ref[0]) + nn(d_up, w_ref[1])).astype(BF)
        return carried

    lax.fori_loop(0, blocks, block, 0)


def ffn_body(h_ref, cot_ref, w_ref, out_ref, back_ref, g_ref, hid_ref, dg_ref, du_ref):
    parts, rows, _ = h_ref.shape
    ffn_steps(
        parts, lambda t: h_ref.at[t], lambda t: cot_ref.at[t], w_ref, hid_ref, dg_ref, du_ref,
        lambda t: out_ref.at[t], lambda t: back_ref.at[t],
    )
    h_all = h_ref[...].reshape(parts * rows, D)
    cot_all = cot_ref[...].reshape(parts * rows, D)
    for place, (left, right) in enumerate(((dg_ref, h_all), (du_ref, h_all), (hid_ref, cot_all))):
        g_ref[place] = tn(left[...], right).astype(BF)


def ffn(h_all, cot_all, w):
    parts, rows, _ = h_all.shape
    units = w.shape[1]
    return call(
        ffn_body,
        (
            jax.ShapeDtypeStruct(h_all.shape, BF),
            jax.ShapeDtypeStruct(h_all.shape, BF),
            jax.ShapeDtypeStruct(w.shape, BF),
        ),
        scratch=[pltpu.VMEM((parts * rows, units), BF)] * 3,
        cost=cost_of(2 * parts * rows * 9 * D * units, 20 << 20),
    )(h_all, cot_all, w)


def unmix_math(
    mixed_ref, cot_ref, d_h, heads_ref, w_out_ref, gain_ref, d_mixed_ref, d_heads_ref, g_out_ref, g_gain_ref
):
    rows_of, parts, head_rows, feat = w_out_ref.shape
    mixed = mixed_ref[...]
    scale = lax.rsqrt(jnp.sum(mixed * mixed, axis=1, keepdims=True) / D + EPS)
    normed = mixed * scale
    g_gain_ref[...] = jnp.sum(d_h * normed, axis=0, keepdims=True)
    gain = jnp.concatenate([gain_ref[c, 1:2] for c in range(parts)], axis=1)
    inner = d_h * gain
    dot = jnp.sum(inner * normed, axis=1, keepdims=True) / D
    d_mixed = cot_ref[...].astype(F32) + scale * (inner - normed * dot)
    d_mixed_ref[...] = d_mixed
    low = d_mixed.astype(BF)
    grad = tn(heads_ref[...], low)
    for r in range(rows_of):
        acc = None
        for c in range(parts):
            lanes = slice(c * feat, (c + 1) * feat)
            term = nt(low[:, lanes], w_out_ref[r, c])
            acc = term if acc is None else acc + term
            g_out_ref[r, c] = grad[r * head_rows : (r + 1) * head_rows, lanes].astype(BF)
        d_heads_ref[:, r * head_rows : (r + 1) * head_rows] = acc.astype(BF)


def write_output(mixed_ref, total, out_ref):
    parts, _, feat = out_ref.shape
    for c in range(parts):
        lanes = slice(c * feat, (c + 1) * feat)
        out_ref[c] = (mixed_ref[:, lanes] + total[:, lanes]).astype(BF)


def unmix_body(
    dh_ref, sum_ref, mixed_ref, cot_ref, heads_ref, w_out_ref, gain_ref,
    out_ref, d_mixed_ref, d_heads_ref, g_out_ref, g_gain_ref,
):
    unmix_math(
        mixed_ref, cot_ref, dh_ref[...], heads_ref, w_out_ref, gain_ref,
        d_mixed_ref, d_heads_ref, g_out_ref, g_gain_ref,
    )
    write_output(mixed_ref, sum_ref[...], out_ref)


def middle_body(
    x_ref, heads_ref, w_out_ref, gain_ref, cot_own_ref, cot_in_ref, w_own_ref, rows_ref,
    mixed_ref, d_mixed_ref, d_heads_ref, g_out_ref, g_gain_ref, g_ref, out_pair_ref,
    w_ref, h_ref, cot_ref, hid_ref, dg_ref, du_ref, back_ref, fwd_ref, back_got_ref, fwd_got_ref,
    pair_ref, diag_ref, far_ref, send_sem, recv_sem, w_sem, cot_sem,
):
    row = lax.axis_index("row")
    col, core, across = neighbours()
    dp, (me, on_x, on_y, on_both) = square()
    x, mine = col // 2, lax.rem(col, 2)
    y = 1 - dp
    parts, rows, feat = x_ref.shape
    units = rows_ref.shape[3]
    greet(
        [
            (None, {"col": core}),
            (None, {"col": across}),
            (None, {"dp": y}),
            (row <= 2, {"row": row + 1}),
            (row >= 1, {"row": row - 1}),
        ]
    )
    mover = Mover(send_sem, recv_sem)

    def w_place(r, c):
        return w_ref.at[:, pl.ds(pl.multiple_of(r * units, units), units), pl.ds(c * feat, feat)]

    last = []
    for c in range(4):
        right = mover.copy(rows_ref.at[0, c], w_place(0, c), row=row + 1)
        left = mover.copy(rows_ref.at[3, c], w_place(3, c), row=row - 1)
        pl.when(row == 2)(right.start)
        pl.when(row == 1)(left.start)
        last.append((right, left))
    local = []
    for k in range(4):
        r = lax.rem(row + k, 4)
        here = {1: row != 3, 3: row != 0}.get(k)
        for c in range(4):
            source = w_own_ref.at[c] if k == 0 else rows_ref.at[r, c]
            copy = pltpu.make_async_copy(source, w_place(r, c), w_sem.at[k, c])
            if here is None:
                copy.start()
            else:
                pl.when(here)(copy.start)
            local.append((here, copy))
    cots = []
    for k in range(4):
        from_x = lax.rem(x + k % 2, 2)
        from_dp = lax.rem(dp + k // 2, 2)
        lanes = pl.ds(pl.multiple_of((from_x * 2 + mine) * feat, feat), feat)
        for c in range(4):
            part = pl.ds(c * rows, rows)
            source = cot_own_ref.at[part] if k == 0 else cot_in_ref.at[from_dp * 2 + from_x, part]
            spot = from_dp * 2 + c // 2
            copy = pltpu.make_async_copy(source, cot_ref.at[lax.rem(mine + c, 2), spot, :, lanes], cot_sem.at[k, c])
            copy.start()
            local.append((None, copy))
            sent = mover.copy(source, cot_ref.at[lax.rem(mine + c + 1, 2), spot, :, lanes], col=core)
            sent.start()
            cots.append(sent)

    total = None
    for c in range(parts):
        lanes = slice(c * feat, (c + 1) * feat)
        acc = x_ref[c].astype(F32)
        for r in range(4):
            acc = acc + nn(heads_ref[:, r * feat : (r + 1) * feat], w_out_ref[r, c])
        mixed_ref[:, lanes] = acc
        part = jnp.sum(acc * acc, axis=1, keepdims=True)
        total = part if total is None else total + part
    scale = lax.rsqrt(total / D + EPS)
    for c in range(parts):
        lanes = slice(c * feat, (c + 1) * feat)
        h_ref[0, me, :, lanes] = (mixed_ref[:, lanes] * scale * gain_ref[c, 1:2]).astype(BF)

    half = rows // 2
    top, low = pl.ds(0, half), pl.ds(half, half)

    def h_copy(spot, part=None, side=0, **place):
        source = h_ref.at[0, spot] if part is None else h_ref.at[0, spot, part]
        target = h_ref.at[side, spot] if part is None else h_ref.at[side, spot, part]
        return mover.copy(source, target, **place)

    x_low = h_copy(me, low, col=across)
    y_top = h_copy(me, top, dp=y)
    x_top = h_copy(me, top, col=across)
    y_low = h_copy(me, low, dp=y)
    near = h_copy(me, None, 1, col=core)
    both_low = h_copy(on_x, low, dp=y)
    both_top = h_copy(on_y, top, col=across)
    near_first = [h_copy(on_x, low, 1, col=core), h_copy(on_y, top, 1, col=core)]
    near_second = [h_copy(on_x, top, 1, col=core), h_copy(on_y, low, 1, col=core)]
    near_both = h_copy(on_both, None, 1, col=core)
    for c in (x_low, y_top, near, x_top, y_low):
        c.start()
    steps = (
        ((me, top), (me, low)),
        ((on_x, low), (on_y, top)),
        ((on_x, top), (on_y, low)),
        ((on_both, top), (on_both, low)),
    )
    back_near = [[mover.copy(back_ref.at[1, s, p], back_got_ref.at[s, p], col=core) for s, p in two] for two in steps]
    fwd_near = [[mover.copy(fwd_ref.at[1, s, p], fwd_got_ref.at[s, p], col=core) for s, p in two] for two in steps]
    diag = [
        mover.copy(pair_ref.at[on_both, top], diag_ref.at[0], col=across),
        mover.copy(pair_ref.at[on_both, low], diag_ref.at[1], dp=y),
    ]
    far = [
        mover.copy(pair_ref.at[on_x, top], far_ref.at[0, top], col=across),
        mover.copy(pair_ref.at[on_y, low], far_ref.at[1, low], dp=y),
        mover.copy(pair_ref.at[on_y, top], far_ref.at[1, top], dp=y),
        mover.copy(pair_ref.at[on_x, low], far_ref.at[0, low], col=across),
    ]

    def add_pair(k):
        for (s, p), c in zip(steps[k], back_near[k]):
            c.wait_recv()
            pair_ref[s, p] = (back_ref[0, s, p].astype(F32) + back_got_ref[s, p].astype(F32)).astype(BF)

    for here, copy in local:
        if here is None:
            copy.wait()
        else:
            pl.when(here)(copy.wait)
    for c in cots:
        c.wait_recv()
    for right, left in last:
        pl.when(row == 3)(right.wait_recv)
        pl.when(row == 0)(left.wait_recv)

    def block(t, carried):
        @pl.when(t == 1)
        def _():
            near.wait_recv()

        @pl.when(t == 2)
        def _():
            x_low.wait_recv()
            both_low.start()
            near_first[0].start()
            y_top.wait_recv()
            both_top.start()
            near_first[1].start()

        @pl.when(t == 3)
        def _():
            for c in near_first:
                c.wait_recv()

        @pl.when(t == 4)
        def _():
            x_top.wait_recv()
            near_second[0].start()
            y_low.wait_recv()
            near_second[1].start()

        @pl.when(t == 5)
        def _():
            for c in near_second:
                c.wait_recv()
            add_pair(1)

        @pl.when(t == 6)
        def _():
            both_low.wait_recv()
            both_top.wait_recv()
            near_both.start()

        @pl.when(t == 7)
        def _():
            near_both.wait_recv()
            add_pair(2)
            far[0].start()
            far[1].start()

        name, side = t // 2, lax.rem(t, 2)
        first_dp = lax.rem(dp + jnp.where(name == 3, 1, 0), 2)
        first_x = lax.rem(x + jnp.where(name >= 1, 1, 0), 2)
        first = first_dp * 2 + first_x
        other_dp = lax.rem(dp + jnp.where(name >= 1, 1, 0), 2)
        other_x = lax.rem(x + jnp.where(name == 3, 1, 0), 2)
        other = other_dp * 2 + other_x
        first_rows = pl.ds(pl.multiple_of(jnp.where(name == 1, half, 0), half), half)
        other_rows = pl.ds(pl.multiple_of(jnp.where(name == 1, 0, half), half), half)
        h = jnp.concatenate([h_ref[side, first, first_rows], h_ref[side, other, other_rows]], axis=0)
        cot = jnp.concatenate([cot_ref[side, first, first_rows], cot_ref[side, other, other_rows]], axis=0)
        gate = nt(h, w_ref[0])
        up = nt(h, w_ref[1])
        d_hidden = nt(cot, w_ref[2])
        sig = 1.0 / (1.0 + jnp.exp(-gate))
        silu = gate * sig
        hidden = (silu * up).astype(BF)
        d_gate = (d_hidden * up * sig * (1.0 + gate * (1.0 - sig))).astype(BF)
        d_up = (d_hidden * silu).astype(BF)
        back = (nn(d_gate, w_ref[0]) + nn(d_up, w_ref[1])).astype(BF)
        fwd = nn(hidden, w_ref[2]).astype(BF)
        for spot, part, cut in ((first, first_rows, slice(0, half)), (other, other_rows, slice(half, rows))):
            start = jnp.where(part.start == 0, 0, half)
            place = pl.ds(pl.multiple_of((side * 4 + spot) * rows + start, half), half)
            hid_ref[place] = hidden[cut]
            dg_ref[place] = d_gate[cut]
            du_ref[place] = d_up[cut]
            back_ref[side, spot, part] = back[cut]
            fwd_ref[side, spot, part] = fwd[cut]
        for k in range(4):

            @pl.when(t == 2 * k + 1)
            def _():
                for c in back_near[k] + fwd_near[k]:
                    c.start()

        return carried

    lax.fori_loop(0, 8, block, 0)
    add_pair(3)
    for c in diag:
        c.start()

    def gradient(place, left, right):
        grad = tn(left[...], right[...].reshape(8 * rows, D))
        for r in range(4):
            g_ref[r, place] = grad[r * units : (r + 1) * units].astype(BF)

    gradient(0, dg_ref, h_ref)
    gradient(1, du_ref, h_ref)
    for k, (s, part) in enumerate(((on_y, top), (on_x, low))):
        if k == 1:
            far[0].wait_send()
        else:
            far[1].wait_send()
        diag[k].wait_recv()
        pair_ref[s, part] = (pair_ref[s, part].astype(F32) + diag_ref[k].astype(F32)).astype(BF)
        far[2 + k].start()
    gradient(2, hid_ref, cot_ref)
    for two, copies in zip(steps, fwd_near):
        for (s, p), c in zip(two, copies):
            c.wait_recv()
            out_pair_ref[s, p] = (fwd_ref[0, s, p].astype(F32) + fwd_got_ref[s, p].astype(F32)).astype(BF)
    add_pair(0)
    for c in far:
        c.wait_recv()
    d_h = pair_ref[me].astype(F32) + far_ref[0].astype(F32) + far_ref[1].astype(F32)
    unmix_math(
        mixed_ref, cot_ref.at[0, me], d_h, heads_ref, w_out_ref, gain_ref,
        d_mixed_ref, d_heads_ref, g_out_ref, g_gain_ref,
    )
    for c in cots + [x_low, y_top, x_top, y_low, near, both_low, both_top, near_both] + near_first + near_second:
        c.wait_send()
    for two in back_near + fwd_near:
        for c in two:
            c.wait_send()
    for c in diag + far[2:]:
        c.wait_send()
    for right, left in last:
        pl.when(row == 2)(right.wait_send)
        pl.when(row == 1)(left.wait_send)


def middle(x_parts, heads, w_out, gains, cot_own, cot_near, w_own, w_rows):
    parts, rows, feat = x_parts.shape
    units = w_rows.shape[3]
    count = 8 + 16 + 12 + 16 + 6
    square_of = pltpu.VMEM((2, 4, rows, D), BF)
    hidden_of = pltpu.VMEM((8 * rows, 4 * units), BF)
    quarter = pltpu.VMEM((4, rows, D), BF)
    return pl.pallas_call(
        middle_body,
        out_shape=(
            jax.ShapeDtypeStruct((rows, D), F32),
            jax.ShapeDtypeStruct((rows, D), F32),
            jax.ShapeDtypeStruct((rows, D), BF),
            jax.ShapeDtypeStruct(w_out.shape, BF),
            jax.ShapeDtypeStruct((1, D), F32),
            jax.ShapeDtypeStruct((4, 3, units, D), BF),
            jax.ShapeDtypeStruct((4, rows, D), BF),
        ),
        in_specs=[VMEM] * 4 + [ANY] * 4,
        out_specs=(VMEM,) * 7,
        scratch_shapes=[pltpu.VMEM((3, 4 * units, D), BF), square_of, square_of]
        + [hidden_of] * 3
        + [square_of, square_of, quarter, quarter, quarter]
        + [
            pltpu.VMEM((2, rows // 2, D), BF),
            pltpu.VMEM((2, rows, D), BF),
            pltpu.SemaphoreType.DMA((count,)),
            pltpu.SemaphoreType.DMA((count,)),
            pltpu.SemaphoreType.DMA((4, 4)),
            pltpu.SemaphoreType.DMA((4, 4)),
        ],
        compiler_params=comm_params(4),
        cost_estimate=cost_of(2 * 8 * rows * 9 * D * 4 * units, 24 << 20),
    )(x_parts, heads, w_out, gains, cot_own, cot_near, w_own, w_rows)


def unmix(dh, out_sum, mixed, cot_own, heads, w_out, gains):
    rows = heads.shape[0]
    parts, feat = w_out.shape[1], w_out.shape[3]
    outs = (
        jax.ShapeDtypeStruct((parts, rows, feat), BF),
        jax.ShapeDtypeStruct((rows, D), F32),
        jax.ShapeDtypeStruct((rows, D), BF),
        jax.ShapeDtypeStruct(w_out.shape, BF),
        jax.ShapeDtypeStruct((1, D), F32),
    )
    return call(unmix_body, outs, cost=cost_of(4 * rows * D * D, 18 << 20))(
        dh, out_sum, mixed, cot_own, heads, w_out, gains
    )


def query_grads(ranks_taken, dq, high, low, bq_ref):
    fac = None
    folded = []
    for r in ranks_taken:
        tile = bq_ref[:, (r // 2) * LANES : (r // 2 + 1) * LANES]
        rank = double_left(tile) if r % 2 == 0 else double_right(tile)
        product = dq * jnp.concatenate([rank] * PAIRS, axis=1)
        term = two_pass(product, head_collect(2 * RK + r))
        fac = term if fac is None else fac + term
        pick = head_spread(2 * RK + r, 0, D)
        terms = (nn(high, pick) + nn(low, pick)) * dq
        acc = terms[:, :LANES]
        for p in range(1, PAIRS):
            acc = acc + terms[:, p * LANES : (p + 1) * LANES]
        folded.append(acc + pltpu.roll(acc, HD, 1))
    return fac, folded


def turned_back(part, turn_ref):
    return part * turn_ref[:, :LANES] - swap_halves(part) * turn_ref[:, LANES:]


def put_query_grads(folded, first, turn_ref, d_ref):
    lane = lane_iota(folded[0].shape)
    for k in range(len(folded) // 2):
        merged = jnp.where(lane < HD, folded[2 * k], folded[2 * k + 1])
        tile = first // 2 + k
        d_ref[:, tile * LANES : (tile + 1) * LANES] = turned_back(merged, turn_ref).astype(BF)


def put_key_grads(dkf, fac, turn_ref, d_ref):
    d_ref[:, 3 * LANES : 4 * LANES] = turned_back(dkf[:, :LANES], turn_ref).astype(BF)
    d_ref[:, 4 * LANES : 5 * LANES] = dkf[:, LANES : 2 * LANES].astype(BF)
    fac = fac.astype(BF).astype(F32) + nt(dkf[:, 2 * LANES :].astype(BF), key_columns())
    d_ref[:, RANK_COLS:] = fac.astype(BF)


def factor_weight_grads(d_ref, h_ref, gains, g_two_ref, g_ref):
    n_row, parts, _, feat = g_ref.shape
    grad = tn(d_ref[...], h_ref[...])
    ranks_each = RANK_COLS // n_row
    used = FAC * GROUP
    for c in range(parts):
        lanes = slice(c * feat, (c + 1) * feat)
        tail = jnp.concatenate(
            [gains[c], g_two_ref[:, lanes], jnp.zeros((GROUP_COLS - used - 2, feat), F32)], axis=0
        )
        for r in range(n_row):
            first = RANK_COLS + r * GROUP_COLS
            g_ref[r, c, :ranks_each] = grad[r * ranks_each : (r + 1) * ranks_each, lanes].astype(BF)
            g_ref[r, c, ranks_each:] = jnp.concatenate([grad[first : first + used, lanes], tail], axis=0).astype(BF)


def first_norm_back(d_h, x_ref, gain_ref, d_mixed_ref, gi_ref):
    parts, _, feat = x_ref.shape
    xs = [x_ref[c].astype(F32) for c in range(parts)]
    total = sum(jnp.sum(v * v, axis=1, keepdims=True) for v in xs)
    scale = lax.rsqrt(total / D + EPS)
    dot = None
    gains = []
    for c in range(parts):
        normed = xs[c] * scale
        grad = d_h[:, c * feat : (c + 1) * feat]
        gains.append(jnp.sum(grad * normed, axis=0, keepdims=True))
        part = jnp.sum(grad * gain_ref[c, :1] * normed, axis=1, keepdims=True)
        dot = part if dot is None else dot + part
    for c in range(parts):
        lanes = slice(c * feat, (c + 1) * feat)
        normed = xs[c] * scale
        total = d_mixed_ref[:, lanes] + scale * (d_h[:, lanes] * gain_ref[c, :1] - normed * (dot / D))
        gi_ref[c] = total.astype(gi_ref.dtype)
    return gains


def back_body(
    dq_ref, dkf_ref, hf_ref, bq_ref, turn_ref, w_ref, h_ref, x_ref, gain_ref, d_mixed_ref, g_two_ref,
    gi_ref, g_ref, d_ref,
):
    heads = hf_ref[...]
    high = heads.astype(BF)
    low = (heads - high.astype(F32)).astype(BF)
    fac, folded = query_grads(range(RQ), dq_ref[...] * (1.0 / RQ), high, low, bq_ref)
    put_query_grads(folded, 0, turn_ref, d_ref)
    put_key_grads(dkf_ref[...].astype(F32), fac, turn_ref, d_ref)
    gains = first_norm_back(nn(d_ref[...], w_ref[...]), x_ref, gain_ref, d_mixed_ref, gi_ref)
    factor_weight_grads(d_ref, h_ref, gains, g_two_ref, g_ref)


def back(dq, dkf, hf, bq, turn, w_rh, h, x_parts, gains, d_mixed, g_two, n_row):
    rows = dq.shape[0]
    parts, _, feat = x_parts.shape
    each = RANK_COLS // n_row + GROUP_COLS
    return call(
        back_body,
        (jax.ShapeDtypeStruct(x_parts.shape, F32), jax.ShapeDtypeStruct((n_row, parts, each, feat), BF)),
        scratch=[pltpu.VMEM((rows, ALL_COLS), BF)],
        cost=cost_of(2 * rows * D * 800 * 6, 12 << 20),
    )(dq, dkf, hf, bq, turn, w_rh, h, x_parts, gains, d_mixed, g_two)


def tail_body(
    win_ref, dq_ref, hf_ref, bq_ref, turn_ref, w_ref, h_ref, x_ref, gain_ref, d_mixed_ref, g_two_ref,
    rows_ref, ends_ref, part_ref,
    grad_ref, gi_all_ref, cols_ref, cols_other_ref, mix_ref, mix_other_ref,
    d_ref, gi_ref, wnear_ref, wsend_ref, wfar_ref, rows_own_ref, cols_send_ref, mix_got_ref,
    g_ref, near_ref, pair_ref, far_ref, side_ref, down_ref, last_ref, end_ref,
    send_sem, recv_sem, local_sem,
):
    row = lax.axis_index("row")
    col, core, across = neighbours()
    cross = lax.rem(core + 2, 4)
    dp = lax.axis_index("dp")
    x, mine = col // 2, lax.rem(col, 2)
    y = 1 - dp
    order = [lax.rem(row + k, 4) for k in (1, 2, 3, 0)]
    greet(
        [(None, {"col": c}) for c in (core, across, cross)]
        + [(None, {"row": r}) for r in order[:3]]
        + [(None, {"dp": y})]
    )
    mover = Mover(send_sem, recv_sem)
    started = []

    def go(source, target, **place):
        c = mover.copy(source, target, **place)
        c.start()
        started.append(c)
        return c

    rows_own = pltpu.make_async_copy(rows_ref.at[row], rows_own_ref, local_sem.at[1])
    rows_own.start()

    near_one = go(win_ref.at[1], wnear_ref.at[0], col=core)
    near_two = go(win_ref.at[3], wnear_ref.at[1], col=core)
    one = mover.copy(wsend_ref.at[0], wfar_ref.at[0], row=row - 1)
    two = mover.copy(wsend_ref.at[1], wfar_ref.at[1], row=row - 1)
    hands_on = jnp.logical_and(row >= 1, row <= 2)
    left = mine == 0
    heads = hf_ref[...]
    high = heads.astype(BF)
    low = (heads - high.astype(F32)).astype(BF)
    dq = dq_ref[...] * (1.0 / RQ)
    near_one.wait_recv()
    near_two.wait_recv()
    zero = jnp.zeros(wnear_ref.shape[1:], F32)
    from_low = wnear_ref[0].astype(F32)
    from_high = wnear_ref[1].astype(F32)
    wsend_ref[1] = (win_ref[0].astype(F32) + jnp.where(left, zero, from_low)).astype(BF)
    pl.when(row >= 2)(two.start)

    width = x_ref.shape[2]
    rows_own.wait()
    for place in range(3):
        total = rows_own_ref[place].astype(F32)
        total = total + jnp.where(row >= 1, ends_ref[0, place].astype(F32), 0.0)
        total = (total + jnp.where(row <= 2, ends_ref[1, place].astype(F32), 0.0)).astype(BF)
        for c in range(4):
            cols_send_ref[c, place] = total[:, c * width : (c + 1) * width]
    columns = [go(cols_send_ref.at[c], cols_ref.at[col], col=c) for c in (across, cross, core)]
    cols_ref[col] = cols_send_ref[col]
    rest = [go(cols_ref.at[col], cols_other_ref.at[col], dp=y)]

    fac, folded = query_grads(range(0, 4), dq, high, low, bq_ref)
    put_query_grads(folded, 0, turn_ref, d_ref)
    sent_on = win_ref[2].astype(F32) + jnp.where(left, from_low, from_high)
    pl.when(hands_on)(two.wait_recv)
    wsend_ref[0] = jnp.where(hands_on, sent_on + wfar_ref[1].astype(F32), sent_on).astype(BF)
    pl.when(row >= 1)(one.start)

    mixes = [go(part_ref.at[order[k]], mix_got_ref.at[k], row=order[k]) for k in range(3)]

    fac_more, folded = query_grads(range(4, RQ), dq, high, low, bq_ref)
    put_query_grads(folded, 4, turn_ref, d_ref)
    for c, source in zip(columns, (across, cross, core)):
        c.wait_recv()
        rest.append(go(cols_ref.at[source], cols_other_ref.at[source], dp=y))
    d_kf = win_ref[4].astype(F32) + jnp.where(left, from_high, zero)
    pl.when(row <= 2)(one.wait_recv)
    d_kf = jnp.where(row <= 2, d_kf + wfar_ref[0].astype(F32), d_kf)
    put_key_grads(d_kf, fac + fac_more, turn_ref, d_ref)
    d_h = nn(d_ref[...], w_ref[...])
    gains = first_norm_back(d_h, x_ref, gain_ref, d_mixed_ref, gi_ref)
    factor_weight_grads(d_ref, h_ref, gains, g_two_ref, g_ref)

    first = [go(g_ref.at[r, (1 - x) * 2 + 1 - mine], near_ref.at[0, k], col=core) for k, r in enumerate(order)]
    second = [go(g_ref.at[r, x * 2 + 1 - mine], near_ref.at[1, k], col=core) for k, r in enumerate(order)]
    sides = []
    for k, r in enumerate(order):
        first[k].wait_recv()
        pair_ref[k] = (g_ref[r, (1 - x) * 2 + mine].astype(F32) + near_ref[0, k].astype(F32)).astype(BF)
        sides.append(go(pair_ref.at[k], side_ref.at[k], col=across))

    total = part_ref[row].astype(F32)
    for k, c in enumerate(mixes):
        c.wait_recv()
        total = total + mix_got_ref[k].astype(F32)
    mix_ref[...] = total.astype(BF)
    rest.append(go(mix_ref, mix_other_ref, dp=y))
    for c in (across, cross, core):
        rest.append(go(gi_ref.at[c], gi_all_ref.at[col], col=c))
    own = pltpu.make_async_copy(gi_ref.at[col], gi_all_ref.at[col], local_sem.at[0])
    own.start()

    downs = []
    for k, r in enumerate(order):
        second[k].wait_recv()
        sides[k].wait_recv()
        far_ref[k] = (
            g_ref[r, x * 2 + mine].astype(F32) + near_ref[1, k].astype(F32) + side_ref[k].astype(F32)
        ).astype(BF)
        if k < 3:
            downs.append(go(far_ref.at[k], down_ref.at[k], row=r))
    total = far_ref[3].astype(F32)
    for k in range(3):
        downs[k].wait_recv()
        total = total + down_ref[k].astype(F32)
    last_ref[...] = total.astype(BF)
    end = go(last_ref, end_ref, dp=y)
    end.wait_recv()
    grad_ref[...] = last_ref[...].astype(F32) + end_ref[...].astype(F32)
    for c in rest:
        c.wait_recv()
    for c in started:
        c.wait_send()
    pl.when(row >= 1)(one.wait_send)
    pl.when(row >= 2)(two.wait_send)
    own.wait()


def tail(win, dq, hf, bq, turn, w_rh, h, x_parts, gains, d_mixed, g_two, g_rows, ends, part):
    rows = dq.shape[0]
    parts, _, feat = x_parts.shape
    units = g_rows.shape[2]
    block = (RANK_COLS // 4 + GROUP_COLS, feat)
    cols = (parts, 3, units, feat)
    mix = part.shape[1:]
    wide = g_rows.shape[1:]
    slot = win.shape[1:]
    count = 2 + 2 + 3 + 8 + 4 + 3 + 1 + 1 + 3 + 3 + 3 + 1
    return pl.pallas_call(
        tail_body,
        out_shape=(
            jax.ShapeDtypeStruct(block, F32),
            jax.ShapeDtypeStruct(x_parts.shape, BF),
            jax.ShapeDtypeStruct(cols, BF),
            jax.ShapeDtypeStruct(cols, BF),
            jax.ShapeDtypeStruct(mix, BF),
            jax.ShapeDtypeStruct(mix, BF),
        ),
        in_specs=[VMEM] * 11 + [ANY, VMEM, VMEM],
        out_specs=(VMEM, ANY, VMEM, ANY, VMEM, ANY),
        scratch_shapes=[
            pltpu.VMEM((rows, ALL_COLS), BF),
            pltpu.VMEM(x_parts.shape, BF),
            pltpu.VMEM((2,) + slot, BF),
            pltpu.VMEM((2,) + slot, BF),
            pltpu.VMEM((2,) + slot, BF),
            pltpu.VMEM(wide, BF),
            pltpu.VMEM(cols, BF),
            pltpu.VMEM((3,) + mix, BF),
            pltpu.VMEM((4, parts) + block, BF),
            pltpu.VMEM((2, 4) + block, BF),
            pltpu.VMEM((4,) + block, BF),
            pltpu.VMEM((4,) + block, BF),
            pltpu.VMEM((4,) + block, BF),
            pltpu.VMEM((3,) + block, BF),
            pltpu.VMEM(block, BF),
            pltpu.VMEM(block, BF),
            pltpu.SemaphoreType.DMA((count,)),
            pltpu.SemaphoreType.DMA((count,)),
            pltpu.SemaphoreType.DMA((2,)),
        ],
        compiler_params=comm_params(7),
        cost_estimate=cost_of(2 * rows * D * 800 * 6, 24 << 20),
    )(win, dq, hf, bq, turn, w_rh, h, x_parts, gains, d_mixed, g_two, g_rows, ends, part)


def local(
    tokens_in, segments, gain_attn, gain_ffn, w_heads, w_ranks, w_out, w_gate, w_up, w_down, cotangent
):
    n_row = lax.axis_size("row")
    n_col = lax.axis_size("col")
    row = lax.axis_index("row")
    col = lax.axis_index("col")
    micro, row_tokens, feat = tokens_in.shape
    subs = n_col // micro
    rows = row_tokens // subs
    length = row_tokens * n_row
    head_local = w_heads.shape[1] // FAC
    rank_local = w_ranks.shape[1]
    ffn_local = w_gate.shape[1]
    out_local = w_out.shape[0]
    block = row * subs + col % subs
    past = min(-(-(MAX_DOC - 1) // rows), n_row * subs - 1)
    keys = (past + 1) * rows

    dp_count = lax.axis_size("dp")
    fast = n_col == 4 and n_row == 4 and dp_count == 2 and micro == 2 and past == 4

    heads_t = jnp.transpose(w_heads.reshape(feat, head_local, FAC), (2, 1, 0))
    heads_t = heads_t[jnp.array(FAC_ORDER)].reshape(FAC * head_local, feat)
    pad = jnp.zeros((GROUP_COLS - FAC * head_local, feat), BF)
    w_own = jnp.concatenate([w_ranks.T, heads_t, pad], axis=0)
    gains_own = jnp.concatenate([gain_attn[None], gain_ffn[None], jnp.zeros((6, feat), F32)], axis=0)
    tokens = tokens_in.reshape(n_col, rows, feat)
    if fast:
        dp = lax.axis_index("dp")
        part = ffn_local // (2 * n_col)
        units = -(-part // 16) * 16
        ffn_own = jnp.stack([w_gate.T, w_up.T, w_down]).reshape(3, 2, n_col, part, feat)
        ffn_own = jnp.transpose(lax.dynamic_index_in_dim(ffn_own, dp, 1, False), (1, 0, 2, 3))
        ffn_own = jnp.pad(ffn_own, ((0, 0), (0, 0), (0, units - part), (0, 0)))
    else:
        part = ffn_local // n_col
        units = part * n_row
        w_ffn = jnp.stack([w_gate.T, w_up.T, w_down]).reshape(3, n_col, part, feat)
        w_ffn = lax.all_to_all(jnp.transpose(w_ffn, (1, 0, 2, 3)), "col", 0, 0, tiled=True)
        w_ffn = jnp.transpose(w_ffn, (1, 2, 0, 3)).reshape(3, part, D)
        w_ffn = jnp.transpose(lax.all_gather(w_ffn, "row", axis=0), (1, 0, 2, 3)).reshape(3, units, D)
        w_blocks = lax.all_gather(w_own, ("row", "col"), axis=0).reshape((n_row, n_col) + w_own.shape)
        gains = lax.all_gather(gains_own, "col", axis=0)
        x_parts = lax.all_to_all(tokens, "col", 0, 0, tiled=True)
        w_out_all = lax.all_gather(w_out, ("row", "col"), axis=0).reshape((n_row, n_col) + w_out.shape)

    seg_row = lax.dynamic_index_in_dim(segments, col // subs, 0, keepdims=False)
    padded = jnp.concatenate([jnp.full((1, past * rows), -1, jnp.int32), seg_row], axis=1)
    seg_window = lax.dynamic_slice_in_dim(padded, block * rows, keys, 1)
    own_seg = seg_window[0, past * rows :]
    key_idx = jnp.arange(keys, dtype=jnp.int32)
    query_idx = jnp.arange(rows, dtype=jnp.int32) + past * rows
    before = (own_seg[:, None] == seg_window) & (key_idx[None, :] < query_idx[:, None])
    places = jnp.sum(before.astype(jnp.int32), axis=1)
    inverse = ROPE ** (-(jnp.arange(HD // 2, dtype=F32) * 2.0 / HD))
    angles = places.astype(F32)[:, None] * inverse[None, :]
    cosine = jnp.cos(angles)
    sine = jnp.sin(angles)
    turn = jnp.concatenate([cosine] * 4 + [-sine, sine, -sine, sine], axis=1)

    groups = [[m * subs + s for s in range(subs)] for m in range(micro)]
    if fast:
        x_parts, gains, ffn_parts, mixes, h_one, head_fac, bq_rot, queries, w_rh, kf_window = head(
            tokens, w_own, gains_own, ffn_own, w_out, turn
        )
        kf_window = kf_window.reshape(keys, -1)
        cot_rows = cotangent.reshape(micro * row_tokens, feat)
        heads_out, lse, key_all, value_all, w_rows, cot_near, mixes = attend(
            queries, kf_window, seg_window, ffn_parts, cot_rows, mixes
        )
        mixed, d_mixed, d_heads, g_out, g_gain_two, g_rows, out_pair = middle(
            x_parts, heads_out, mixes, gains, cot_rows, cot_near, ffn_parts, w_rows
        )
        d_q, d_kf, output, g_ends, g_part = attend_back(
            queries, key_all, value_all, d_heads, lse, kf_window, seg_window, out_pair, mixed, g_rows, g_out
        )
        g_rh, grad_input, g_cols, cols_other, g_out, out_other = tail(
            d_kf.reshape(past + 1, rows, -1), d_q, head_fac, bq_rot, turn, w_rh, h_one, x_parts, gains, d_mixed,
            g_gain_two, g_rows, g_ends, g_part,
        )
        grad_input = grad_input.astype(F32)
        g_out = g_out.astype(F32) + out_other.astype(F32)
        g_ffn = jnp.where(dp == 0, jnp.stack([g_cols, cols_other]), jnp.stack([cols_other, g_cols]))
        g_ffn = jnp.transpose(g_ffn[:, :, :, :part], (2, 0, 1, 3, 4)).reshape(3, ffn_local, feat).astype(F32)
    else:
        h_one, head_fac, bq_rot, key_fac, queries, w_rh = front(x_parts, gains, w_blocks, turn)
        gathered = lax.all_gather(key_fac, "row", axis=0)
        gathered = lax.all_gather(gathered, "col", axis=1, axis_index_groups=groups)
        gathered = gathered.reshape(length, key_fac.shape[1])
        padded_kf = jnp.concatenate([jnp.zeros((past * rows, key_fac.shape[1]), BF), gathered], axis=0)
        kf_window = lax.dynamic_slice_in_dim(padded_kf, block * rows, keys, 0)
        heads_out, lse, key_all, value_all = attend(queries, kf_window, seg_window)
        mixed, h_two = mixing(x_parts, heads_out, w_out_all, gains)
        cot_own = lax.all_to_all(cotangent.reshape(n_col, rows, feat), "col", 0, 0, tiled=True)
        cot_own = jnp.transpose(cot_own, (1, 0, 2)).reshape(rows, D)
        cot_all = lax.all_gather(cot_own, "col", axis=0)
        h_all = lax.all_gather(h_two, "col", axis=0)
        out_part, dh_part, g_ffn = ffn(h_all, cot_all, w_ffn)
        dh_sum = lax.psum_scatter(dh_part, "col", scatter_dimension=0, tiled=False).astype(F32)
        out_sum = lax.psum_scatter(out_part, "col", scatter_dimension=0, tiled=False).astype(F32)
        out_parts, d_mixed, d_heads, g_out, g_gain_two = unmix(
            dh_sum, out_sum, mixed, cot_own, heads_out, w_out_all, gains
        )
        d_q, d_kf = attend_back(queries, key_all, value_all, d_heads, lse, kf_window, seg_window)
        spread_kf = jnp.zeros((past * rows + length, d_kf.shape[1]), BF)
        spread_kf = lax.dynamic_update_slice_in_dim(spread_kf, d_kf, block * rows, 0)[past * rows :]
        spread_kf = spread_kf.reshape(n_row, subs, rows, -1)
        own_kf = lax.psum_scatter(spread_kf, "row", scatter_dimension=0, tiled=False)
        own_kf = lax.psum_scatter(own_kf, "col", scatter_dimension=0, tiled=False, axis_index_groups=groups)
        gi_parts, g_rh = back(
            d_q, own_kf, head_fac, bq_rot, turn, w_rh, h_one, x_parts, gains, d_mixed, g_gain_two, n_row
        )
        output = lax.all_to_all(out_parts, "col", 0, 0, tiled=True)
        grad_input = lax.all_to_all(gi_parts, "col", 0, 0, tiled=True)
        g_ffn = lax.psum_scatter(g_ffn.reshape(3, n_row, part, D), "row", scatter_dimension=1, tiled=False)
        g_ffn = jnp.transpose(lax.psum(g_ffn, "dp").reshape(3, part, n_col, feat), (2, 0, 1, 3))
        g_ffn = lax.all_to_all(g_ffn, "col", 0, 0, tiled=True)
        g_ffn = jnp.transpose(g_ffn, (1, 0, 2, 3)).reshape(3, ffn_local, feat).astype(F32)

        def total(values):
            values = values.reshape((n_row * n_col,) + values.shape[2:])
            values = lax.psum_scatter(values, ("row", "col"), scatter_dimension=0, tiled=False)
            return lax.psum(values, "dp").astype(F32)

        g_out = total(g_out)
        g_rh = total(g_rh)

    used = rank_local + FAC * head_local
    own_heads = g_rh[rank_local:used].reshape(FAC, head_local, feat)
    own_heads = jnp.transpose(own_heads[jnp.array(FAC_BACK)], (2, 1, 0)).reshape(w_heads.shape)
    return (
        output.reshape(tokens_in.shape),
        grad_input.reshape(tokens_in.shape),
        g_rh[used],
        g_rh[used + 1],
        own_heads,
        g_rh[:rank_local].T,
        g_out,
        g_ffn[0].T,
        g_ffn[1].T,
        g_ffn[2],
    )


def solution(mesh):
    tokens = P(None, ("dp", "row"), "col")
    both = P("col", "row")
    turned = P("row", "col")
    gain = P("col")
    return jax.shard_map(
        local,
        mesh=mesh,
        in_specs=(tokens, P(None, "dp", None), gain, gain, both, both, turned, both, both, turned, tokens),
        out_specs=(tokens, tokens, gain, gain, both, both, turned, both, both, turned),
        check_vma=False,
    )
```

profile of v0, /device:TPU:0, one launch (start us, length us, event | category | flops | bytes accessed | tf_op | source)
XLA Modules:
  0.0 255.2 jit_solution(11692349082617151213)
XLA Ops:
  0.6 0.0 copy-start
  0.7 0.0 copy-start.4
  0.7 0.0 copy-start.5
  0.7 0.0 copy-start.3
  0.7 0.6 copy-done
  1.4 0.6 fusion.6
  2.0 0.4 convert_reduce_fusion
  2.4 0.5 multiply_sine_fusion
  3.0 0.0 copy-start.10
  3.0 0.0 copy-start.14
  3.0 0.0 copy-start.9
  3.0 0.0 copy-start.11
  3.0 0.0 copy-start.12
  3.0 1.0 concatenate.16.turn_ref
  4.0 0.0 copy-done.4
  4.0 0.0 copy-done.5
  4.0 0.0 copy-done.3
  4.0 0.1 fusion.4
  4.1 0.9 pad.5.ffn_ref
  5.0 0.0 copy-done.10
  5.0 0.0 copy-done.14
  5.0 0.6 gather_fusion
  5.6 0.1 pad.18.clone
  5.7 0.0 copy-done.9
  5.7 0.7 maximum_maximum_fusion.w_own_ref
  6.5 0.1 pad.15.clone
  6.5 0.0 copy-done.11
  6.5 0.0 copy-done.12
  6.5 0.7 maximum_maximum_fusion.1.gain_ref
  7.2 44.7 %shard_map.204 = (bf16[4,256,256]{2,1,0:T(8,128)(2,1)}, f32[4,8,256]{2,1,0:T(8,128)}, bf16[4,3,96,256]{3,2,1,0:T(8,128)(2,1)}, bf16[4,4,256,256]{3,2,1,0:T(8,128...) custom-call(bf16[4,256,256]{2,1,0:T(8,128)(2,1)} %bitcast.74, ...), custom_call_target="tpu_custom_call" | custom-call | flops 1258291200 | bytes 14680064 | tf_op jit(solution)/shard_map/pallas_call | solution.py:594
  51.9 35.3 %shard_map.205 = (bf16[256,1024]{1,0:T(8,128)(2,1)}, f32[16,8,256]{2,1,0:T(8,128)}, bf16[1280,1024]{1,0:T(8,128)(2,1)}, bf16[1280,1024]{1,0:T(8,128)(2,1)}, bf16...) custom-call(bf16[256,1024]{1,0:T(8,128)(2,1)} %get-tuple-element.45., ...), custom_call_target="tpu_custom_call", output_to_operand_aliasing={{6}: (5, {})} | custom-call | flops 10737418240 | bytes 16777216 | tf_op jit(solution)/shard_map/pallas_call | solution.py:724
  87.2 63.2 %shard_map.206 = (f32[256,1024]{1,0:T(8,128)}, f32[256,1024]{1,0:T(8,128)}, bf16[256,1024]{1,0:T(8,128)(2,1)}, bf16[4,4,256,256]{3,2,1,0:T(8,128)(2,1)}, f32[1,1...) custom-call(bf16[4,256,256]{2,1,0:T(8,128)(2,1)} %get-tuple-element.51.x_ref, ...), custom_call_target="tpu_custom_call" | custom-call | flops 14495514624 | bytes 25165824 | tf_op jit(solution)/shard_map/pallas_call | solution.py:1249
  150.4 49.4 %shard_map.207 = (f32[256,1024]{1,0:T(8,128)}, bf16[1280,384]{1,0:T(8,128)(2,1)}, bf16[4,256,256]{2,1,0:T(8,128)(2,1)}, bf16[2,3,96,1024]{3,2,1,0:T(8,128)(2,1)}, bf16[4,256,256]{2,1,0:T(8,128)(2,1)}) custom-call(bf16[256,1024]{1,0:T(8,128)(2,1)} %get-tuple-element.45.q_ref, bf16[1280,1024]{1,0:T(8,128)(2,1)} %get-tuple-element.49.k_ref, ...), custom_call_target="tpu_custom_call" | custom-call | flops 26843545600 | bytes 16777216 | tf_op jit(solution)/shard_map/pallas_call | solution.py:851
  199.8 47.1 %shard_map.208 = (f32[208,256]{1,0:T(8,128)}, bf16[4,256,256]{2,1,0:T(8,128)(2,1)}, bf16[4,3,96,256]{3,2,1,0:T(8,128)(2,1)}, bf16[4,3,96,256]{3,2,1,0:T(8,128)(2...) custom-call(bf16[5,256,384]{2,1,0:T(8,128)(2,1)} %bitcast.55, f32[256,1024]{1,0:T(8,128)} %get-tuple-element.65.dq_ref, ...), custom_call_target="tpu_custom_call" | custom-call | flops 2516582400 | bytes 25165824 | tf_op jit(solution)/shard_map/pallas_call | solution.py:1532
  246.9 1.8 convert_bitcast_fusion
  248.7 0.0 copy-start.7
  248.7 0.0 copy-start.8
  248.7 0.0 copy-start.1
  248.7 1.4 fusion.7
  250.1 0.0 copy-done.8
  250.1 0.7 convert_add_fusion
  250.8 1.0 bitcast_convert_fusion
  251.9 0.0 copy-done.13
  251.9 0.6 gather_fusion.1
  252.5 0.6 reshape.92
  253.2 0.7 slice_bitcast_fusion
  253.8 0.6 fusion.8
  254.4 0.8 copy.52
  (22 shorter events, 0.1 us)
Async XLA Ops:
  0.6 0.7 copy-start
  0.7 3.4 %copy-start.4 = (bf16[256,704]{0,1:T(8,128)(2,1)S(1)}, bf16[256,704]{0,1:T(8,128)(2,1)}, u32[]{:S(2)}) copy-start(bf16[256,704]{0,1:T(8,128)(2,1)} %param.21) | copy-start | bytes 1081348
  0.7 3.3 %copy-start.5 = (bf16[704,256]{1,0:T(8,128)(2,1)S(1)}, bf16[704,256]{1,0:T(8,128)(2,1)}, u32[]{:S(2)}) copy-start(bf16[704,256]{1,0:T(8,128)(2,1)} %param.22) | copy-start | bytes 1081348
  0.7 3.3 %copy-start.3 = (bf16[256,704]{0,1:T(8,128)(2,1)S(1)}, bf16[256,704]{0,1:T(8,128)(2,1)}, u32[]{:S(2)}) copy-start(bf16[256,704]{0,1:T(8,128)(2,1)} %param.20) | copy-start | bytes 1081348
  3.0 2.0 copy-start.10
  3.0 2.0 copy-start.14
  3.0 2.7 %copy-start.9 = (bf16[256,160]{0,1:T(8,128)(2,1)S(1)}, bf16[256,160]{0,1:T(8,128)(2,1)}, u32[]{:S(2)}) copy-start(bf16[256,160]{0,1:T(8,128)(2,1)} %param.18) | copy-start | bytes 245764
  3.0 3.5 %copy-start.11 = (f32[256]{0:T(256)S(1)}, f32[256]{0:T(256)}, u32[]{:S(2)}) copy-start(f32[256]{0:T(256)} %param.16) | copy-start | bytes 3076
  3.0 3.5 %copy-start.12 = (f32[256]{0:T(256)S(1)}, f32[256]{0:T(256)}, u32[]{:S(2)}) copy-start(f32[256]{0:T(256)} %param.15) | copy-start | bytes 3076
  248.7 1.4 copy-start.7
  248.7 1.4 copy-start.8
  248.7 2.1 copy-start.1
  250.1 1.8 copy-start.6
  250.1 1.8 copy-start.13
  250.1 4.3 %copy-start.2 = (bf16[4,256,256]{2,1,0:T(8,128)(2,1)S(1)}, bf16[4,256,256]{2,1,0:T(8,128)(2,1)}, u32[]{:S(2)}) copy-start(bf16[4,256,256]{2,1,0:T(8,128)(2,1)} %get-tuple-element.63) | copy-start | bytes 1572868
where the time goes:
time: 255 us
  Pallas kernels  240 us (94%)
  local copies, waits for them, and re-layouts  8.63 us (3%)
  other arithmetic  5.98 us (2%)
    pallas_call x1, Pallas kernels, middle(): pl.pallas_call(middle_body, out_shape=(jax.ShapeDtypeStruct((rows, D), F3...  63.2 us
    pallas_call x1, Pallas kernels, attend_back(): pl.pallas_call(functools.partial(attend_back_body, fast), out_shape=tuple...  49.4 us
    pallas_call x1, Pallas kernels, tail(): pl.pallas_call(tail_body, out_shape=(jax.ShapeDtypeStruct(block, F32), ja...  47.1 us
    pallas_call x1, Pallas kernels, head(): pl.pallas_call(head_body, out_shape=(jax.ShapeDtypeStruct(tok.shape, BF),...  44.7 us
    pallas_call x1, Pallas kernels, attend(): pl.pallas_call(functools.partial(attend_body, fast), out_shape=tuple(outs...  35.3 us

commit v1 on v0

--- a/solution.py
+++ b/solution.py
@@ -182,7 +182,7 @@
 
 
 class AttendCopies:
-    def __init__(self, w_ref, cot_ref, rows_ref, near_ref, mixes_ref, send_sem, recv_sem):
+    def __init__(self, cot_ref, rows_ref, near_ref, mixes_ref, send_sem, recv_sem):
         row = lax.axis_index("row")
         col, core, across = neighbours()
         dp, (me, on_x, on_y, _) = square()
@@ -199,10 +199,13 @@
             (None, {"col": core}),
             (None, {"dp": 1 - dp}),
         ]
-        self.to_right = mover.copy(w_ref, rows_ref.at[row], row=row + 1)
-        self.to_left = mover.copy(w_ref, rows_ref.at[row], row=row - 1)
-        self.pass_right = mover.copy(rows_ref.at[row - 1], rows_ref.at[row - 1], row=row + 1)
-        self.pass_left = mover.copy(rows_ref.at[row + 1], rows_ref.at[row + 1], row=row - 1)
+        self.row = row
+        cuts = [pl.ds(0, 2), pl.ds(2, 2)]
+        lower, upper = rows_ref.at[row - 1], rows_ref.at[row + 1]
+        self.pass_right = [mover.copy(lower.at[c], lower.at[c], row=row + 1) for c in cuts]
+        self.pass_left = [mover.copy(upper.at[c], upper.at[c], row=row - 1) for c in cuts]
+        self.last_right = [mover.copy(rows_ref.at[0, c], rows_ref.at[0, c], row=row + 1) for c in cuts]
+        self.last_left = [mover.copy(rows_ref.at[3, c], rows_ref.at[3, c], row=row - 1) for c in cuts]
         half = cot_ref.shape[0] // 2
         top, low = pl.ds(0, half), pl.ds(half, half)
         self.cots = [
@@ -222,28 +225,33 @@
 
     def first(self):
         greet(self.partners)
-        pl.when(self.right)(self.to_right.start)
-        pl.when(self.left)(self.to_left.start)
+        for k in range(2):
+            pl.when(self.both)(self.pass_right[k].start)
+            pl.when(self.both)(self.pass_left[k].start)
         for c in self.cots + self.mixes:
             c.start()
+
+    def hand_on(self, k):
+        pl.when(self.from_left)(self.pass_right[k].wait_recv)
+        pl.when(self.from_right)(self.pass_left[k].wait_recv)
+        pl.when(self.row == 2)(self.last_right[k].start)
+        pl.when(self.row == 1)(self.last_left[k].start)
 
     def second(self):
         for c in self.cots[:2]:
             c.wait_recv()
         for c in self.relays:
             c.start()
-        pl.when(self.left)(self.to_right.wait_recv)
-        pl.when(self.right)(self.to_left.wait_recv)
-        pl.when(self.both)(self.pass_right.start)
-        pl.when(self.both)(self.pass_left.start)
+        self.hand_on(1)
 
     def last(self):
-        pl.when(self.right)(self.to_right.wait_send)
-        pl.when(self.left)(self.to_left.wait_send)
-        pl.when(self.both)(self.pass_right.wait_send)
-        pl.when(self.both)(self.pass_left.wait_send)
-        pl.when(self.from_left)(self.pass_right.wait_recv)
-        pl.when(self.from_right)(self.pass_left.wait_recv)
+        for k in range(2):
+            pl.when(self.both)(self.pass_right[k].wait_send)
+            pl.when(self.both)(self.pass_left[k].wait_send)
+            pl.when(self.row == 2)(self.last_right[k].wait_send)
+            pl.when(self.row == 1)(self.last_left[k].wait_send)
+            pl.when(self.row == 3)(self.last_right[k].wait_recv)
+            pl.when(self.row == 0)(self.last_left[k].wait_recv)
         for c in self.cots[:2]:
             c.wait_send()
         for c in self.cots[2:] + self.relays + self.mixes:
@@ -253,7 +261,7 @@
 class BackCopies:
     def __init__(self, refs, sems):
         (
-            self.pair_ref, self.mixed_ref, self.rows_ref, self.g_out_ref,
+            self.pair_ref, self.mixed_ref, self.rows_ref, self.g_out_ref, self.hop_ref,
             self.out_ref, self.ends_ref, self.part_ref,
             self.relay_ref, self.diag_ref, self.far_ref, self.send_ref,
             self.right_ref, self.left_ref, self.got_ref,
@@ -285,13 +293,11 @@
         self.out = [mover.copy(self.send_ref.at[c], self.out_ref.at[col], col=c) for c in (across, cross, core)]
         self.own = pltpu.make_async_copy(self.send_ref.at[col], self.out_ref.at[col], local_sem.at[0])
         self.hop_right = [
-            mover.copy(self.rows_ref.at[3], self.got_ref.at[0], row=row + 1),
-            mover.copy(self.right_ref.at[0], self.got_ref.at[1], row=row + 1),
+            mover.copy(self.right_ref.at[0], self.got_ref.at[0], row=row + 1),
             mover.copy(self.right_ref.at[1], self.ends_ref.at[0], row=row + 1),
         ]
         self.hop_left = [
-            mover.copy(self.rows_ref.at[0], self.got_ref.at[0], row=row - 1),
-            mover.copy(self.left_ref.at[0], self.got_ref.at[2], row=row - 1),
+            mover.copy(self.left_ref.at[0], self.got_ref.at[1], row=row - 1),
             mover.copy(self.left_ref.at[1], self.ends_ref.at[1], row=row - 1),
         ]
         self.cores = [
@@ -304,8 +310,8 @@
             pltpu.make_async_copy(self.pair_ref.at[on_y, top], self.pieces_ref.at[0], local_sem.at[1]),
             pltpu.make_async_copy(self.pair_ref.at[on_x, low], self.pieces_ref.at[1], local_sem.at[2]),
             pltpu.make_async_copy(self.pair_ref.at[me], self.mine_ref, local_sem.at[3]),
-            pltpu.make_async_copy(self.rows_ref, self.rows_in_ref, local_sem.at[4]),
         ]
+        self.rows_load = pltpu.make_async_copy(self.rows_ref, self.rows_in_ref, local_sem.at[4])
         self.g_loads = [
             pltpu.make_async_copy(
                 self.g_out_ref.at[r, lax.rem(x + k, 2) * 2 + mine], self.g_in_ref.at[k, r], local_sem.at[5 + 4 * k + r]
@@ -316,13 +322,20 @@
 
     def first(self):
         row = self.row
+        self.rows_load.start()
+        for c in self.loads + self.g_loads:
+            c.start()
         greet(self.partners)
         for c in self.diag + self.far[:2] + self.cores:
             c.start()
-        pl.when(row == 0)(self.hop_right[0].start)
-        pl.when(row == 3)(self.hop_left[0].start)
-        for c in self.loads + self.g_loads:
-            c.start()
+        self.rows_load.wait()
+        hop = self.hop_ref[...].astype(F32)
+        ahead = self.rows_in_ref[jnp.minimum(row + 2, 3)].astype(F32)
+        self.right_ref[0] = jnp.where(row == 1, ahead + hop, ahead).astype(BF)
+        behind = self.rows_in_ref[jnp.maximum(row - 2, 0)].astype(F32)
+        self.left_ref[0] = jnp.where(row == 2, behind + hop, behind).astype(BF)
+        pl.when(row <= 1)(self.hop_right[0].start)
+        pl.when(row >= 2)(self.hop_left[0].start)
 
     def cross_x(self):
         for c in self.g_loads:
@@ -339,31 +352,25 @@
         row = self.row
         for c in self.loads:
             c.wait()
-        pl.when(row == 1)(self.hop_right[0].wait_recv)
-        pl.when(row == 2)(self.hop_left[0].wait_recv)
-        hop = self.got_ref[0].astype(F32)
-        ahead = self.rows_in_ref[jnp.minimum(row + 2, 3)].astype(F32)
-        self.right_ref[0] = jnp.where(row == 1, ahead + hop, ahead).astype(BF)
-        behind = self.rows_in_ref[jnp.maximum(row - 2, 0)].astype(F32)
-        self.left_ref[0] = jnp.where(row == 2, behind + hop, behind).astype(BF)
-        pl.when(row <= 1)(self.hop_right[1].start)
-        pl.when(row >= 2)(self.hop_left[1].start)
         for k in range(2):
             self.diag[k].wait_recv()
             self.relay_ref[k] = (self.pieces_ref[k].astype(F32) + self.diag_ref[k].astype(F32)).astype(BF)
             self.far[2 + k].start()
 
+    def last_hop(self):
+        row = self.row
+        middle = jnp.logical_and(row >= 1, row <= 2)
+        pl.when(middle)(self.hop_right[0].wait_recv)
+        pl.when(middle)(self.hop_left[0].wait_recv)
+        ahead = self.rows_in_ref[jnp.minimum(row + 1, 3)].astype(F32)
+        behind = self.rows_in_ref[jnp.maximum(row - 1, 0)].astype(F32)
+        self.right_ref[1] = jnp.where(row >= 1, ahead + self.got_ref[0].astype(F32), ahead).astype(BF)
+        self.left_ref[1] = jnp.where(row <= 2, behind + self.got_ref[1].astype(F32), behind).astype(BF)
+        pl.when(row <= 2)(self.hop_right[1].start)
+        pl.when(row >= 1)(self.hop_left[1].start)
+
     def third(self):
         row = self.row
-        middle = jnp.logical_and(row >= 1, row <= 2)
-        pl.when(middle)(self.hop_right[1].wait_recv)
-        pl.when(middle)(self.hop_left[1].wait_recv)
-        ahead = self.rows_in_ref[jnp.minimum(row + 1, 3)].astype(F32)
-        behind = self.rows_in_ref[jnp.maximum(row - 1, 0)].astype(F32)
-        self.right_ref[1] = jnp.where(row >= 1, ahead + self.got_ref[1].astype(F32), ahead).astype(BF)
-        self.left_ref[1] = jnp.where(row <= 2, behind + self.got_ref[2].astype(F32), behind).astype(BF)
-        pl.when(row <= 2)(self.hop_right[2].start)
-        pl.when(row >= 1)(self.hop_left[2].start)
         for c in self.far:
             c.wait_recv()
         feat = self.send_ref.shape[2]
@@ -393,14 +400,12 @@
         self.own.wait()
         for c in self.diag + self.far + self.cores + self.sides:
             c.wait_send()
-        pl.when(row == 0)(self.hop_right[0].wait_send)
-        pl.when(row == 3)(self.hop_left[0].wait_send)
-        pl.when(row <= 1)(self.hop_right[1].wait_send)
-        pl.when(row >= 2)(self.hop_left[1].wait_send)
-        pl.when(row <= 2)(self.hop_right[2].wait_send)
-        pl.when(row >= 1)(self.hop_left[2].wait_send)
-        pl.when(row >= 1)(self.hop_right[2].wait_recv)
-        pl.when(row <= 2)(self.hop_left[2].wait_recv)
+        pl.when(row <= 1)(self.hop_right[0].wait_send)
+        pl.when(row >= 2)(self.hop_left[0].wait_send)
+        pl.when(row <= 2)(self.hop_right[1].wait_send)
+        pl.when(row >= 1)(self.hop_left[1].wait_send)
+        pl.when(row >= 1)(self.hop_right[1].wait_recv)
+        pl.when(row <= 2)(self.hop_left[1].wait_recv)
 
 
 def first_norm(x_ref, gain_ref, h_ref):
@@ -470,10 +475,27 @@
     make_queries(hf_ref, bq_ref, q_ref)
 
 
+def front(x_parts, gains, blocks, turn):
+    rows = x_parts.shape[1]
+    return call(
+        front_body,
+        (
+            jax.ShapeDtypeStruct((rows, D), BF),
+            jax.ShapeDtypeStruct((rows, HEAD_COLS), F32),
+            jax.ShapeDtypeStruct((rows, RQ * HD), F32),
+            jax.ShapeDtypeStruct((rows, 3 * LANES), BF),
+            jax.ShapeDtypeStruct((rows, D), BF),
+            jax.ShapeDtypeStruct((ALL_COLS, D), BF),
+        ),
+        cost=cost_of(2 * rows * D * 800 * 3, 6 << 20),
+    )(x_parts, gains, blocks, turn)
+
+
 def head_body(
-    tok_ref, w_own_ref, gain_ref, ffn_ref, mix_ref, turn_ref,
-    x_ref, gains_ref, parts_ref, mixes_ref, h_ref, hf_ref, bq_ref, q_ref, w_ref, win_ref,
-    blocks_ref, send_sem, recv_sem,
+    tok_ref, ranks_ref, heads_ref, gain_one_ref, gain_two_ref, gate_ref, up_ref, down_ref, mix_ref, seg_all_ref,
+    inverse_ref,
+    x_ref, gains_ref, parts_ref, mixes_ref, h_ref, hf_ref, bq_ref, q_ref, w_ref, win_ref, seg_ref, turn_ref, rows_ref,
+    w_own_ref, gain_ref, ffn_ref, blocks_ref, send_sem, recv_sem,
 ):
     row = lax.axis_index("row")
     col, core, across = neighbours()
@@ -481,7 +503,23 @@
     side = lax.rem(col, 2)
     rows = [lax.rem(row + k, 4) for k in range(4)]
     back = [lax.rem(row + 4 - k, 4) for k in range(4)]
-    greet([(None, {"col": c}) for c in (core, across, cross)] + [(None, {"row": r}) for r in rows[1:]])
+    dp = lax.axis_index("dp")
+
+    rank_rows = ranks_ref.shape[0]
+    place = lax.broadcasted_iota(jnp.int32, (GROUP_COLS, FAC * GROUP), 0)
+    lane = lax.broadcasted_iota(jnp.int32, (GROUP_COLS, FAC * GROUP), 1)
+    factor = lane % FAC
+    spot = jnp.where(factor < RQ, factor + 2 * RK, factor - RQ) * GROUP + lane // FAC
+    w_own_ref[:rank_rows] = ranks_ref[...]
+    w_own_ref[rank_rows:] = nn((place == spot).astype(F32).astype(BF), heads_ref[...]).astype(BF)
+    gain_ref[...] = jnp.zeros_like(gain_ref)
+    gain_ref[0:1] = gain_one_ref[...]
+    gain_ref[1:2] = gain_two_ref[...]
+    greet(
+        [(None, {"col": c}) for c in (core, across, cross)]
+        + [(None, {"row": r}) for r in rows[1:]]
+        + [(None, {"dp": 1 - dp})]
+    )
     mover = Mover(send_sem, recv_sem)
     started = []
 
@@ -499,7 +537,22 @@
     for c in (across, cross, core):
         toks.append(go(gain_ref, gains_ref.at[col], col=c))
         toks.append(go(tok_ref.at[c], x_ref.at[col], col=c))
-    mix_down = [None] + [go(mix_ref, mixes_ref.at[row, col], row=rows[k]) for k in range(1, 4)]
+    units = ffn_ref.shape[2]
+    hidden = gate_ref.shape[0]
+    unit = hidden // 8
+    place = lax.broadcasted_iota(jnp.int32, (4 * units, hidden), 0)
+    lane = lax.broadcasted_iota(jnp.int32, (4 * units, hidden), 1)
+    inside = place % units
+    taken = (inside < unit) & (lane == (dp * 4 + place // units) * unit + inside)
+    pick = taken.astype(F32).astype(BF)
+    for k, source in enumerate((gate_ref, up_ref, down_ref)):
+        chosen = nn(pick, source[...]).astype(BF)
+        for c in range(4):
+            ffn_ref[c, k] = chosen[c * units : (c + 1) * units]
+    ffn = [go(ffn_ref.at[c], parts_ref.at[col], col=c) for c in (across, cross, core)]
+    part = mix_ref.shape[0] // 2
+    half = pl.ds(pl.multiple_of(dp * part, part), part)
+    mix_down = [None] + [go(mix_ref.at[half], mixes_ref.at[row, col, half], row=rows[k]) for k in range(1, 4)]
     blocks_ref[row, col] = w_own_ref[...]
     gains_ref[col] = gain_ref[...]
     x_ref[col] = tok_ref[col]
@@ -520,16 +573,44 @@
         def _():
             win_ref[slot] = zero
 
+    keys = seg_ref.shape[1]
+    tokens = tok_ref.shape[1]
+    block_no = row * 2 + side
+    for slot in range(5):
+        index = block_no - 4 + slot
+        lanes = pl.ds(pl.multiple_of(jnp.maximum(index, 0) * tokens, tokens), tokens)
+        seg_ref[:, slot * tokens : (slot + 1) * tokens] = jnp.where(index >= 0, seg_all_ref[col // 2, :, lanes], -1)
+    seg_row = seg_ref[...].astype(F32)
+    column = jnp.broadcast_to(seg_row, (LANES, keys)).T
+    column = jnp.concatenate([column] * (tokens // LANES), axis=1)
+    key_idx = lax.broadcasted_iota(jnp.int32, (keys, tokens), 0)
+    query_idx = lax.broadcasted_iota(jnp.int32, (keys, tokens), 1) + (keys - tokens)
+    before = (column == seg_row[:, keys - tokens :]) & (key_idx < query_idx)
+    places = jnp.sum(jnp.where(before, 1.0, 0.0), axis=0, keepdims=True)
+    angles = jnp.broadcast_to(places, (LANES, tokens)).T * inverse_ref[...]
+    turn_ref[:, :LANES] = jnp.cos(angles)
+    sine = jnp.sin(angles)
+    turn_ref[:, LANES:] = jnp.where(lane_iota(sine.shape) % HD < HD // 2, -sine, sine)
+
     for k in range(1, 4):
         down[k].wait_recv()
         block = blocks_ref.at[back[k], col]
         sides.append(go(block, block, col=across))
         cores.append(go(block, block, col=core))
-    for c in (across, cross, core):
-        rest.append(go(ffn_ref.at[c], parts_ref.at[col], col=c))
     for c in toks:
         c.wait_recv()
     first_norm(x_ref, gains_ref, h_ref)
+    mix_side = []
+    for k in range(1, 4):
+        mix_down[k].wait_recv()
+        block = mixes_ref.at[back[k], col, half]
+        mix_side.append(go(block, block, dp=1 - dp))
+    for c in ffn:
+        c.wait_recv()
+    to_right = mover.copy(parts_ref, rows_ref.at[row], row=row + 1)
+    to_left = mover.copy(parts_ref, rows_ref.at[row], row=row - 1)
+    pl.when(row <= 2)(to_right.start)
+    pl.when(row >= 1)(to_left.start)
     passed = []
     for k in range(4):
         sides[k].wait_recv()
@@ -539,7 +620,7 @@
         c.wait_recv()
     for k in range(4):
         if k > 0:
-            mix_down[k].wait_recv()
+            mix_side[k - 1].wait_recv()
         block = mixes_ref.at[back[k], col]
         rest.append(go(block, block, col=across))
     place_factor_weights(blocks_ref, w_ref)
@@ -582,21 +663,28 @@
     pl.when(side == 0)(near.wait_send)
     pl.when(row <= 2)(one.wait_send)
     pl.when(hands_on)(two.wait_send)
+    pl.when(row <= 2)(to_right.wait_send)
+    pl.when(row >= 1)(to_left.wait_send)
+    pl.when(row >= 1)(to_right.wait_recv)
+    pl.when(row <= 2)(to_left.wait_recv)
     for c in rest:
         c.wait_recv()
     for c in started:
         c.wait_send()
 
 
-def head(tok, w_own, gains, ffn_own, w_out, turn):
+def head(tok, ranks_t, heads_t, gain_one, gain_two, gate_t, up_t, down, w_out, segments, inverse):
     rows, feat = tok.shape[1:]
-    count = 3 + 4 + 4 + 6 + 3 + 3 + 4 + 4 + 5
+    units = -(-gate_t.shape[0] // 8 // 16) * 16
+    block = (ranks_t.shape[0] + GROUP_COLS, feat)
+    ffn = (4, 3, units, feat)
+    count = 3 + 4 + 4 + 6 + 3 + 3 + 3 + 4 + 4 + 2 + 5
     return pl.pallas_call(
         head_body,
         out_shape=(
             jax.ShapeDtypeStruct(tok.shape, BF),
-            jax.ShapeDtypeStruct((4,) + gains.shape, F32),
-            jax.ShapeDtypeStruct(ffn_own.shape, BF),
+            jax.ShapeDtypeStruct((4, 8, feat), F32),
+            jax.ShapeDtypeStruct(ffn, BF),
             jax.ShapeDtypeStruct((4, 4) + w_out.shape, BF),
             jax.ShapeDtypeStruct((rows, D), BF),
             jax.ShapeDtypeStruct((rows, HEAD_COLS), F32),
@@ -604,33 +692,23 @@
             jax.ShapeDtypeStruct((rows, D), BF),
             jax.ShapeDtypeStruct((ALL_COLS, D), BF),
             jax.ShapeDtypeStruct((5, rows, 3 * LANES), BF),
+            jax.ShapeDtypeStruct((1, 5 * rows), jnp.int32),
+            jax.ShapeDtypeStruct((rows, 2 * LANES), F32),
+            jax.ShapeDtypeStruct((4,) + ffn, BF),
         ),
-        in_specs=[VMEM] * 6,
-        out_specs=(VMEM,) * 10,
+        in_specs=[VMEM] * 11,
+        out_specs=(VMEM,) * 12 + (ANY,),
         scratch_shapes=[
-            pltpu.VMEM((4, 4) + w_own.shape, BF),
+            pltpu.VMEM(block, BF),
+            pltpu.VMEM((8, feat), F32),
+            pltpu.VMEM(ffn, BF),
+            pltpu.VMEM((4, 4) + block, BF),
             pltpu.SemaphoreType.DMA((count,)),
             pltpu.SemaphoreType.DMA((count,)),
         ],
         compiler_params=comm_params(1),
         cost_estimate=cost_of(2 * rows * D * 800 * 3, 14 << 20),
-    )(tok, w_own, gains, ffn_own, w_out, turn)
-
-
-def front(x_parts, gains, blocks, turn):
-    rows = x_parts.shape[1]
-    return call(
-        front_body,
-        (
-            jax.ShapeDtypeStruct((rows, D), BF),
-            jax.ShapeDtypeStruct((rows, HEAD_COLS), F32),
-            jax.ShapeDtypeStruct((rows, RQ * HD), F32),
-            jax.ShapeDtypeStruct((rows, 3 * LANES), BF),
-            jax.ShapeDtypeStruct((rows, D), BF),
-            jax.ShapeDtypeStruct((ALL_COLS, D), BF),
-        ),
-        cost=cost_of(2 * rows * D * 800 * 3, 6 << 20),
-    )(x_parts, gains, blocks, turn)
+    )(tok, ranks_t, heads_t, gain_one, gain_two, gate_t, up_t, down, w_out, segments, inverse)
 
 
 def mask_bias(seg_ref, keys, rows):
@@ -646,9 +724,9 @@
 
 def attend_body(fast, q_ref, kf_ref, seg_ref, *refs):
     if fast:
-        w_ref, cot_ref, _, o_ref, lse_ref, k_ref, v_ref, w_rows_ref, cot_near_ref, mixes_ref = refs[:10]
+        _, cot_ref, _, o_ref, lse_ref, k_ref, v_ref, w_rows_ref, cot_near_ref, mixes_ref = refs[:10]
         bias_ref, dup_ref, send_sem, recv_sem = refs[10:]
-        side_work = AttendCopies(w_ref, cot_ref, w_rows_ref, cot_near_ref, mixes_ref, send_sem, recv_sem)
+        side_work = AttendCopies(cot_ref, w_rows_ref, cot_near_ref, mixes_ref, send_sem, recv_sem)
         side_work.first()
     else:
         o_ref, lse_ref, k_ref, v_ref, bias_ref, dup_ref = refs
@@ -661,6 +739,7 @@
 
     def pair(p, carried):
         if fast:
+            pl.when(p == 2)(lambda: side_work.hand_on(0))
             pl.when(p == 4)(side_work.second)
         lanes = pl.ds(pl.multiple_of(p * LANES, LANES), LANES)
         weights = kf_ref[:, 2 * LANES :]
@@ -696,10 +775,10 @@
         side_work.last()
 
 
-def attend(q, kf_window, seg_window, w_own=None, cot=None, mixes=None):
+def attend(q, kf_window, seg_window, w_rows=None, cot=None, mixes=None):
     rows = q.shape[0]
     keys = kf_window.shape[0]
-    fast = w_own is not None
+    fast = w_rows is not None
     outs = [
         jax.ShapeDtypeStruct((rows, D), BF),
         jax.ShapeDtypeStruct((H, 8, rows), F32),
@@ -710,16 +789,16 @@
     in_specs, out_specs, more = [VMEM] * 3, [VMEM] * 4, []
     if fast:
         outs += [
-            jax.ShapeDtypeStruct((4,) + w_own.shape, BF),
+            jax.ShapeDtypeStruct(w_rows.shape, BF),
             jax.ShapeDtypeStruct((4,) + cot.shape, BF),
             jax.ShapeDtypeStruct(mixes.shape, BF),
         ]
         in_specs += [ANY] * 3
         out_specs += [ANY] * 3
-        more = [w_own, cot, mixes]
+        more = [w_rows, cot, mixes]
         scratch += [
-            pltpu.SemaphoreType.DMA((18,)),
-            pltpu.SemaphoreType.DMA((18,)),
+            pltpu.SemaphoreType.DMA((22,)),
+            pltpu.SemaphoreType.DMA((22,)),
         ]
     return pl.pallas_call(
         functools.partial(attend_body, fast),
@@ -727,7 +806,7 @@
         in_specs=in_specs,
         out_specs=tuple(out_specs),
         scratch_shapes=scratch,
-        input_output_aliases={5: 6} if fast else {},
+        input_output_aliases={3: 4, 5: 6} if fast else {},
         compiler_params=comm_params(3) if fast else params(),
         cost_estimate=cost_of(2 * rows * keys * D * 16, 16 << 20),
     )(q, kf_window, seg_window, *more)
@@ -735,9 +814,9 @@
 
 def attend_back_body(fast, q_ref, k_ref, v_ref, do_ref, lse_ref, kf_ref, seg_ref, *refs):
     if fast:
-        dq_ref, dkf_ref = refs[4:6]
-        bias_ref, dup_ref, sum_ref, fac_ref = refs[9:13]
-        side_work = BackCopies(refs[:4] + refs[6:9] + refs[13:27], refs[27:])
+        dq_ref, dkf_ref = refs[5:7]
+        bias_ref, dup_ref, sum_ref, fac_ref = refs[10:14]
+        side_work = BackCopies(refs[:5] + refs[7:10] + refs[14:28], refs[28:])
         side_work.first()
     else:
         dq_ref, dkf_ref, bias_ref, dup_ref, sum_ref, fac_ref = refs
@@ -754,6 +833,7 @@
         if fast:
             pl.when(p == 1)(side_work.cross_x)
             pl.when(p == 3)(side_work.second)
+            pl.when(p == 4)(side_work.last_hop)
             pl.when(p == 6)(side_work.third)
         lanes = pl.ds(pl.multiple_of(p * LANES, LANES), LANES)
         k_tile = k_ref[:, lanes]
@@ -819,7 +899,7 @@
     ]
     in_specs, out_specs = [VMEM] * 7, [VMEM] * 2
     if fast:
-        in_specs += [ANY, VMEM, ANY, ANY]
+        in_specs += [ANY, VMEM, ANY, ANY, VMEM]
         grads, g_out = more[2], more[3]
         parts, feat = g_out.shape[1], g_out.shape[3]
         block, hop = g_out.shape[2:], grads.shape[1:]
@@ -836,7 +916,7 @@
             pltpu.VMEM((parts, rows, feat), BF),
             pltpu.VMEM((2,) + hop, BF),
             pltpu.VMEM((2,) + hop, BF),
-            pltpu.VMEM((3,) + hop, BF),
+            pltpu.VMEM((2,) + hop, BF),
             pltpu.VMEM((2, 4) + block, BF),
             pltpu.VMEM((4,) + block, BF),
             pltpu.VMEM((4,) + block, BF),
@@ -844,8 +924,8 @@
             pltpu.VMEM((rows, D), BF),
             pltpu.VMEM(grads.shape, BF),
             pltpu.VMEM((2, 4) + block, BF),
-            pltpu.SemaphoreType.DMA((27,)),
-            pltpu.SemaphoreType.DMA((27,)),
+            pltpu.SemaphoreType.DMA((25,)),
+            pltpu.SemaphoreType.DMA((25,)),
             pltpu.SemaphoreType.DMA((13,)),
         ]
     return pl.pallas_call(
@@ -982,7 +1062,7 @@
 
 def middle_body(
     x_ref, heads_ref, w_out_ref, gain_ref, cot_own_ref, cot_in_ref, w_own_ref, rows_ref,
-    mixed_ref, d_mixed_ref, d_heads_ref, g_out_ref, g_gain_ref, g_ref, out_pair_ref,
+    mixed_ref, d_mixed_ref, d_heads_ref, g_out_ref, g_gain_ref, g_ref, out_pair_ref, hop_ref,
     w_ref, h_ref, cot_ref, hid_ref, dg_ref, du_ref, back_ref, fwd_ref, back_got_ref, fwd_got_ref,
     pair_ref, diag_ref, far_ref, send_sem, recv_sem, w_sem, cot_sem,
 ):
@@ -1007,25 +1087,14 @@
     def w_place(r, c):
         return w_ref.at[:, pl.ds(pl.multiple_of(r * units, units), units), pl.ds(c * feat, feat)]
 
-    last = []
-    for c in range(4):
-        right = mover.copy(rows_ref.at[0, c], w_place(0, c), row=row + 1)
-        left = mover.copy(rows_ref.at[3, c], w_place(3, c), row=row - 1)
-        pl.when(row == 2)(right.start)
-        pl.when(row == 1)(left.start)
-        last.append((right, left))
     local = []
     for k in range(4):
         r = lax.rem(row + k, 4)
-        here = {1: row != 3, 3: row != 0}.get(k)
         for c in range(4):
             source = w_own_ref.at[c] if k == 0 else rows_ref.at[r, c]
             copy = pltpu.make_async_copy(source, w_place(r, c), w_sem.at[k, c])
-            if here is None:
-                copy.start()
-            else:
-                pl.when(here)(copy.start)
-            local.append((here, copy))
+            copy.start()
+            local.append(copy)
     cots = []
     for k in range(4):
         from_x = lax.rem(x + k % 2, 2)
@@ -1037,7 +1106,7 @@
             spot = from_dp * 2 + c // 2
             copy = pltpu.make_async_copy(source, cot_ref.at[lax.rem(mine + c, 2), spot, :, lanes], cot_sem.at[k, c])
             copy.start()
-            local.append((None, copy))
+            local.append(copy)
             sent = mover.copy(source, cot_ref.at[lax.rem(mine + c + 1, 2), spot, :, lanes], col=core)
             sent.start()
             cots.append(sent)
@@ -1100,16 +1169,10 @@
             c.wait_recv()
             pair_ref[s, p] = (back_ref[0, s, p].astype(F32) + back_got_ref[s, p].astype(F32)).astype(BF)
 
-    for here, copy in local:
-        if here is None:
-            copy.wait()
-        else:
-            pl.when(here)(copy.wait)
+    for copy in local:
+        copy.wait()
     for c in cots:
         c.wait_recv()
-    for right, left in last:
-        pl.when(row == 3)(right.wait_recv)
-        pl.when(row == 0)(left.wait_recv)
 
     def block(t, carried):
         @pl.when(t == 1)
@@ -1199,10 +1262,18 @@
     for c in diag:
         c.start()
 
+    hops = []
+    for place in range(3):
+        to_right = mover.copy(g_ref.at[3, place], hop_ref.at[place], row=row + 1)
+        to_left = mover.copy(g_ref.at[0, place], hop_ref.at[place], row=row - 1)
+        hops.append((to_right, to_left))
+
     def gradient(place, left, right):
         grad = tn(left[...], right[...].reshape(8 * rows, D))
         for r in range(4):
             g_ref[r, place] = grad[r * units : (r + 1) * units].astype(BF)
+        pl.when(row == 0)(hops[place][0].start)
+        pl.when(row == 3)(hops[place][1].start)
 
     gradient(0, dg_ref, h_ref)
     gradient(1, du_ref, h_ref)
@@ -1234,15 +1305,17 @@
             c.wait_send()
     for c in diag + far[2:]:
         c.wait_send()
-    for right, left in last:
-        pl.when(row == 2)(right.wait_send)
-        pl.when(row == 1)(left.wait_send)
+    for to_right, to_left in hops:
+        pl.when(row == 0)(to_right.wait_send)
+        pl.when(row == 3)(to_left.wait_send)
+        pl.when(row == 1)(to_right.wait_recv)
+        pl.when(row == 2)(to_left.wait_recv)
 
 
 def middle(x_parts, heads, w_out, gains, cot_own, cot_near, w_own, w_rows):
     parts, rows, feat = x_parts.shape
     units = w_rows.shape[3]
-    count = 8 + 16 + 12 + 16 + 6
+    count = 16 + 12 + 16 + 6 + 6
     square_of = pltpu.VMEM((2, 4, rows, D), BF)
     hidden_of = pltpu.VMEM((8 * rows, 4 * units), BF)
     quarter = pltpu.VMEM((4, rows, D), BF)
@@ -1256,9 +1329,10 @@
             jax.ShapeDtypeStruct((1, D), F32),
             jax.ShapeDtypeStruct((4, 3, units, D), BF),
             jax.ShapeDtypeStruct((4, rows, D), BF),
+            jax.ShapeDtypeStruct((3, units, D), BF),
         ),
         in_specs=[VMEM] * 4 + [ANY] * 4,
-        out_specs=(VMEM,) * 7,
+        out_specs=(VMEM,) * 7 + (ANY,),
         scratch_shapes=[pltpu.VMEM((3, 4 * units, D), BF), square_of, square_of]
         + [hidden_of] * 3
         + [square_of, square_of, quarter, quarter, quarter]
@@ -1567,6 +1641,55 @@
     )(win, dq, hf, bq, turn, w_rh, h, x_parts, gains, d_mixed, g_two, g_rows, ends, part)
 
 
+def layout_body(
+    grad_ref, gi_ref, cols_ref, other_ref, mix_ref, mix_other_ref,
+    gi_out_ref, gain_ref, gain_two_ref, heads_ref, ranks_ref, out_ref, gate_ref, up_ref, down_ref,
+):
+    first = lax.axis_index("dp") == 0
+    gi_out_ref[...] = gi_ref[...].astype(F32)
+    out_ref[...] = mix_ref[...].astype(F32) + mix_other_ref[...].astype(F32)
+    ranks = ranks_ref.shape[0]
+    used = heads_ref.shape[0]
+    gain_ref[...] = grad_ref[ranks + used : ranks + used + 1]
+    gain_two_ref[...] = grad_ref[ranks + used + 1 : ranks + used + 2]
+    ranks_ref[...] = grad_ref[:ranks]
+    lane = lax.broadcasted_iota(jnp.int32, (used, GROUP_COLS), 1)
+    place = lax.broadcasted_iota(jnp.int32, (used, GROUP_COLS), 0)
+    factor = place % FAC
+    spot = jnp.where(factor < RQ, factor + 2 * RK, factor - RQ) * GROUP + place // FAC
+    heads_ref[...] = jnp.dot(
+        (lane == spot).astype(F32), grad_ref[ranks:], precision=lax.Precision.HIGHEST, preferred_element_type=F32
+    )
+    part = down_ref.shape[0] // 8
+    for k, target in ((0, gate_ref), (1, up_ref), (2, down_ref)):
+        for c in range(4):
+            own = cols_ref[c, k].astype(F32)[:part]
+            other = other_ref[c, k].astype(F32)[:part]
+            target[c * part : (c + 1) * part] = jnp.where(first, own, other)
+            target[(4 + c) * part : (5 + c) * part] = jnp.where(first, other, own)
+
+
+def layout(grad, gi, cols, other, mix, mix_other, heads, ranks, hidden):
+    feat = grad.shape[1]
+    weight = jax.ShapeDtypeStruct((hidden, feat), F32)
+    gain = jax.ShapeDtypeStruct((1, feat), F32)
+    return call(
+        layout_body,
+        (
+            jax.ShapeDtypeStruct(gi.shape, F32),
+            gain,
+            gain,
+            jax.ShapeDtypeStruct((heads, feat), F32),
+            jax.ShapeDtypeStruct((ranks, feat), F32),
+            jax.ShapeDtypeStruct(mix.shape, F32),
+            weight,
+            weight,
+            weight,
+        ),
+        cost=cost_of(0, 8 << 20),
+    )(grad, gi, cols, other, mix, mix_other)
+
+
 def local(
     tokens_in, segments, gain_attn, gain_ffn, w_heads, w_ranks, w_out, w_gate, w_up, w_down, cotangent
 ):
@@ -1589,20 +1712,14 @@
     dp_count = lax.axis_size("dp")
     fast = n_col == 4 and n_row == 4 and dp_count == 2 and micro == 2 and past == 4
 
-    heads_t = jnp.transpose(w_heads.reshape(feat, head_local, FAC), (2, 1, 0))
-    heads_t = heads_t[jnp.array(FAC_ORDER)].reshape(FAC * head_local, feat)
-    pad = jnp.zeros((GROUP_COLS - FAC * head_local, feat), BF)
-    w_own = jnp.concatenate([w_ranks.T, heads_t, pad], axis=0)
-    gains_own = jnp.concatenate([gain_attn[None], gain_ffn[None], jnp.zeros((6, feat), F32)], axis=0)
     tokens = tokens_in.reshape(n_col, rows, feat)
-    if fast:
-        dp = lax.axis_index("dp")
-        part = ffn_local // (2 * n_col)
-        units = -(-part // 16) * 16
-        ffn_own = jnp.stack([w_gate.T, w_up.T, w_down]).reshape(3, 2, n_col, part, feat)
-        ffn_own = jnp.transpose(lax.dynamic_index_in_dim(ffn_own, dp, 1, False), (1, 0, 2, 3))
-        ffn_own = jnp.pad(ffn_own, ((0, 0), (0, 0), (0, units - part), (0, 0)))
-    else:
+    inverse = ROPE ** (-(jnp.arange(HD // 2, dtype=F32) * 2.0 / HD))
+    if not fast:
+        heads_t = jnp.transpose(w_heads.reshape(feat, head_local, FAC), (2, 1, 0))
+        heads_t = heads_t[jnp.array(FAC_ORDER)].reshape(FAC * head_local, feat)
+        pad = jnp.zeros((GROUP_COLS - FAC * head_local, feat), BF)
+        w_own = jnp.concatenate([w_ranks.T, heads_t, pad], axis=0)
+        gains_own = jnp.concatenate([gain_attn[None], gain_ffn[None], jnp.zeros((6, feat), F32)], axis=0)
         part = ffn_local // n_col
         units = part * n_row
         w_ffn = jnp.stack([w_gate.T, w_up.T, w_down]).reshape(3, n_col, part, feat)
@@ -1614,44 +1731,57 @@
         x_parts = lax.all_to_all(tokens, "col", 0, 0, tiled=True)
         w_out_all = lax.all_gather(w_out, ("row", "col"), axis=0).reshape((n_row, n_col) + w_out.shape)
 
-    seg_row = lax.dynamic_index_in_dim(segments, col // subs, 0, keepdims=False)
-    padded = jnp.concatenate([jnp.full((1, past * rows), -1, jnp.int32), seg_row], axis=1)
-    seg_window = lax.dynamic_slice_in_dim(padded, block * rows, keys, 1)
-    own_seg = seg_window[0, past * rows :]
-    key_idx = jnp.arange(keys, dtype=jnp.int32)
-    query_idx = jnp.arange(rows, dtype=jnp.int32) + past * rows
-    before = (own_seg[:, None] == seg_window) & (key_idx[None, :] < query_idx[:, None])
-    places = jnp.sum(before.astype(jnp.int32), axis=1)
-    inverse = ROPE ** (-(jnp.arange(HD // 2, dtype=F32) * 2.0 / HD))
-    angles = places.astype(F32)[:, None] * inverse[None, :]
-    cosine = jnp.cos(angles)
-    sine = jnp.sin(angles)
-    turn = jnp.concatenate([cosine] * 4 + [-sine, sine, -sine, sine], axis=1)
+        seg_row = lax.dynamic_index_in_dim(segments, col // subs, 0, keepdims=False)
+        padded = jnp.concatenate([jnp.full((1, past * rows), -1, jnp.int32), seg_row], axis=1)
+        seg_window = lax.dynamic_slice_in_dim(padded, block * rows, keys, 1)
+        own_seg = seg_window[0, past * rows :]
+        key_idx = jnp.arange(keys, dtype=jnp.int32)
+        query_idx = jnp.arange(rows, dtype=jnp.int32) + past * rows
+        before = (own_seg[:, None] == seg_window) & (key_idx[None, :] < query_idx[:, None])
+        places = jnp.sum(before.astype(jnp.int32), axis=1)
+        angles = places.astype(F32)[:, None] * inverse[None, :]
+        cosine = jnp.cos(angles)
+        sine = jnp.sin(angles)
+        turn = jnp.concatenate([cosine] * 4 + [-sine, sine, -sine, sine], axis=1)
 
     groups = [[m * subs + s for s in range(subs)] for m in range(micro)]
     if fast:
-        x_parts, gains, ffn_parts, mixes, h_one, head_fac, bq_rot, queries, w_rh, kf_window = head(
-            tokens, w_own, gains_own, ffn_own, w_out, turn
+        (
+            x_parts, gains, ffn_parts, mixes, h_one, head_fac, bq_rot, queries, w_rh, kf_window, seg_window, turn, w_rows
+        ) = head(
+            tokens, w_ranks.T, w_heads.T, gain_attn.reshape(1, feat), gain_ffn.reshape(1, feat), w_gate.T, w_up.T,
+            w_down, w_out, segments, jnp.concatenate([inverse] * 4).reshape(1, LANES),
         )
         kf_window = kf_window.reshape(keys, -1)
         cot_rows = cotangent.reshape(micro * row_tokens, feat)
         heads_out, lse, key_all, value_all, w_rows, cot_near, mixes = attend(
-            queries, kf_window, seg_window, ffn_parts, cot_rows, mixes
+            queries, kf_window, seg_window, w_rows, cot_rows, mixes
         )
-        mixed, d_mixed, d_heads, g_out, g_gain_two, g_rows, out_pair = middle(
+        mixed, d_mixed, d_heads, g_out, g_gain_two, g_rows, out_pair, hop = middle(
             x_parts, heads_out, mixes, gains, cot_rows, cot_near, ffn_parts, w_rows
         )
         d_q, d_kf, output, g_ends, g_part = attend_back(
-            queries, key_all, value_all, d_heads, lse, kf_window, seg_window, out_pair, mixed, g_rows, g_out
+            queries, key_all, value_all, d_heads, lse, kf_window, seg_window, out_pair, mixed, g_rows, g_out, hop
         )
         g_rh, grad_input, g_cols, cols_other, g_out, out_other = tail(
             d_kf.reshape(past + 1, rows, -1), d_q, head_fac, bq_rot, turn, w_rh, h_one, x_parts, gains, d_mixed,
             g_gain_two, g_rows, g_ends, g_part,
         )
-        grad_input = grad_input.astype(F32)
-        g_out = g_out.astype(F32) + out_other.astype(F32)
-        g_ffn = jnp.where(dp == 0, jnp.stack([g_cols, cols_other]), jnp.stack([cols_other, g_cols]))
-        g_ffn = jnp.transpose(g_ffn[:, :, :, :part], (2, 0, 1, 3, 4)).reshape(3, ffn_local, feat).astype(F32)
+        grad_input, g_one, g_two, own_heads, own_ranks, g_out, own_gate, own_up, own_down = layout(
+            g_rh, grad_input, g_cols, cols_other, g_out, out_other, w_heads.shape[1], w_ranks.shape[1], ffn_local
+        )
+        return (
+            output.reshape(tokens_in.shape),
+            grad_input.reshape(tokens_in.shape),
+            g_one.reshape(feat),
+            g_two.reshape(feat),
+            own_heads.T,
+            own_ranks.T,
+            g_out,
+            own_gate.T,
+            own_up.T,
+            own_down,
+        )
     else:
         h_one, head_fac, bq_rot, key_fac, queries, w_rh = front(x_parts, gains, w_blocks, turn)
         gathered = lax.all_gather(key_fac, "row", axis=0)

time: 255 us -> 237 us (0.929)
  local copies, waits for them, and re-layouts: 8.63 us -> 0.8 us
  Pallas kernels: 240 us -> 234 us
  other arithmetic: 5.98 us -> 0.6 us
    pallas_call x1, Pallas kernels: 63.2 us -> 54.2 us  [middle(): pl.pallas_call(middle_body, out_shape=(jax.ShapeDtypeStruct((rows, D), F3...]
    pallas_call x0 -> x1, Pallas kernels: none -> 3.5 us  [layout(): call(layout_body, (jax.ShapeDtypeStruct(gi.shape, F32), gain, gain, jax.S...]
where the time goes in v1:
time: 237 us; the launch traced here: 236 us
  Pallas kernels  234 us (99%)
    pallas_call x1, Pallas kernels, middle(): pl.pallas_call(middle_body, out_shape=(jax.ShapeDtypeStruct((rows, D), F3...  54.2 us
    pallas_call x1, Pallas kernels, attend_back(): pl.pallas_call(functools.partial(attend_back_body, fast), out_shape=tuple...  46.9 us
    pallas_call x1, Pallas kernels, head(): pl.pallas_call(head_body, out_shape=(jax.ShapeDtypeStruct(tok.shape, BF),...  46.7 us
    pallas_call x1, Pallas kernels, tail(): pl.pallas_call(tail_body, out_shape=(jax.ShapeDtypeStruct(block, F32), ja...  45.5 us
    pallas_call x1, Pallas kernels, attend(): pl.pallas_call(functools.partial(attend_body, fast), out_shape=tuple(outs...  37.6 us

profile of v1, /device:TPU:0, one launch (start us, length us, event | category | flops | bytes accessed | tf_op | source)
XLA Modules:
  0.0 236.5 jit_solution(11755617719706718002)
XLA Ops:
  0.7 0.6 maximum_bitcast_fusion.inverse_ref
  1.2 46.7 %shard_map.186 = (bf16[4,256,256]{2,1,0:T(8,128)(2,1)}, f32[4,8,256]{2,1,0:T(8,128)}, bf16[4,3,96,256]{3,2,1,0:T(8,128)(2,1)}, bf16[4,4,256,256]{3,2,1,0:T(8,128...) custom-call(bf16[4,256,256]{2,1,0:T(8,128)(2,1)} %bitcast.25, ...), custom_call_target="tpu_custom_call" | custom-call | flops 1258291200 | bytes 14680064 | tf_op jit(solution)/shard_map/pallas_call | solution.py:682
  47.9 37.6 %shard_map.187 = (bf16[256,1024]{1,0:T(8,128)(2,1)}, f32[16,8,256]{2,1,0:T(8,128)}, bf16[1280,1024]{1,0:T(8,128)(2,1)}, bf16[1280,1024]{1,0:T(8,128)(2,1)}, bf16...) custom-call(bf16[256,1024]{1,0:T(8,128)(2,1)} %get-tuple-element.58., ...), custom_call_target="tpu_custom_call", output_to_operand_aliasing={{4}: (3, {}), {6}: (5, {})} | custom-call | flops 10737418240 | bytes 16777216 | tf_op jit(solution)/shard_map/pallas_call | solution.py:803
  85.6 54.2 %shard_map.188 = (f32[256,1024]{1,0:T(8,128)}, f32[256,1024]{1,0:T(8,128)}, bf16[256,1024]{1,0:T(8,128)(2,1)}, bf16[4,4,256,256]{3,2,1,0:T(8,128)(2,1)}, f32[1,1...) custom-call(bf16[4,256,256]{2,1,0:T(8,128)(2,1)} %get-tuple-element., ...), custom_call_target="tpu_custom_call" | custom-call | flops 14495514624 | bytes 25165824 | tf_op jit(solution)/shard_map/pallas_call | solution.py:1322
  139.8 46.9 %shard_map.189 = (f32[256,1024]{1,0:T(8,128)}, bf16[1280,384]{1,0:T(8,128)(2,1)}, bf16[4,256,256]{2,1,0:T(8,128)(2,1)}, bf16[2,3,96,1024]{3,2,1,0:T(8,128)(2,1)}, bf16[4,256,256]{2,1,0:T(8,128)(2,1)}) custom-call(bf16[256,1024]{1,0:T(8,128)(2,1)} %get-tuple-element.58.q_ref, bf16[1280,1024]{1,0:T(8,128)(2,1)} %get-tuple-element.63.k_ref, ...), custom_call_target="tpu_custom_call" | custom-call | flops 26843545600 | bytes 16777216 | tf_op jit(solution)/shard_map/pallas_call | solution.py:931
  186.7 45.5 %shard_map.190 = (f32[208,256]{1,0:T(8,128)}, bf16[4,256,256]{2,1,0:T(8,128)(2,1)}, bf16[4,3,96,256]{3,2,1,0:T(8,128)(2,1)}, bf16[4,3,96,256]{3,2,1,0:T(8,128)(2...) custom-call(bf16[5,256,384]{2,1,0:T(8,128)(2,1)} %bitcast.20, f32[256,1024]{1,0:T(8,128)} %get-tuple-element.81.dq_ref, ...), custom_call_target="tpu_custom_call" | custom-call | flops 2516582400 | bytes 25165824 | tf_op jit(solution)/shard_map/pallas_call | solution.py:1606
  232.2 0.0 copy-start
  232.2 3.5 %shard_map.191 = (f32[4,256,256]{2,1,0:T(8,128)}, f32[1,256]{1,0:T(1,128)}, f32[1,256]{1,0:T(1,128)}, f32[40,256]{1,0:T(8,128)}, f32[160,256]{1,0:T(8,128)}, /*i...) custom-call(f32[208,256]{1,0:T(8,128)} %get-tuple-element.91.grad_ref, ...), custom_call_target="tpu_custom_call" | custom-call | bytes 8388608 | tf_op jit(solution)/shard_map/pallas_call | solution.py:1676
  235.7 0.0 copy-done
  235.7 0.8 copy.26
  (1 shorter events, 0.0 us)
Async XLA Ops:
  232.2 3.5 %copy-start = (bf16[4,256,256]{2,1,0:T(8,128)(2,1)S(1)}, bf16[4,256,256]{2,1,0:T(8,128)(2,1)}, u32[]{:S(2)}) copy-start(bf16[4,256,256]{2,1,0:T(8,128)(2,1)} %get-tuple-element.79) | copy-start | bytes 1572868

commit v2 on v1

--- a/solution.py
+++ b/solution.py
@@ -182,7 +182,8 @@
 
 
 class AttendCopies:
-    def __init__(self, cot_ref, rows_ref, near_ref, mixes_ref, send_sem, recv_sem):
+    def __init__(self, head_end, cot_ref, rows_ref, near_ref, mixes_ref, send_sem, recv_sem):
+        self.head_end = head_end
         row = lax.axis_index("row")
         col, core, across = neighbours()
         dp, (me, on_x, on_y, _) = square()
@@ -192,16 +193,9 @@
         self.both = jnp.logical_and(self.left, self.right)
         self.from_left = row >= 2
         self.from_right = row <= 1
-        self.partners = [
-            (self.right, {"row": row + 1}),
-            (self.left, {"row": row - 1}),
-            (None, {"col": across}),
-            (None, {"col": core}),
-            (None, {"dp": 1 - dp}),
-        ]
         self.row = row
         cuts = [pl.ds(0, 2), pl.ds(2, 2)]
-        lower, upper = rows_ref.at[row - 1], rows_ref.at[row + 1]
+        lower, upper = rows_ref.at[jnp.maximum(row - 1, 0)], rows_ref.at[jnp.minimum(row + 1, 3)]
         self.pass_right = [mover.copy(lower.at[c], lower.at[c], row=row + 1) for c in cuts]
         self.pass_left = [mover.copy(upper.at[c], upper.at[c], row=row - 1) for c in cuts]
         self.last_right = [mover.copy(rows_ref.at[0, c], rows_ref.at[0, c], row=row + 1) for c in cuts]
@@ -224,12 +218,17 @@
                 self.mixes.append(mover.copy(mixes_ref.at[r, c], mixes_ref.at[r, c], col=core))
 
     def first(self):
-        greet(self.partners)
         for k in range(2):
             pl.when(self.both)(self.pass_right[k].start)
             pl.when(self.both)(self.pass_left[k].start)
-        for c in self.cots + self.mixes:
+        for c in self.cots:
             c.start()
+
+    def early(self):
+        self.head_end()
+        for c in self.mixes:
+            c.start()
+        self.hand_on(0)
 
     def hand_on(self, k):
         pl.when(self.from_left)(self.pass_right[k].wait_recv)
@@ -276,7 +275,7 @@
         mover = Mover(send_sem, recv_sem)
         self.x, self.mine = x, mine = col // 2, lax.rem(col, 2)
         self.partners = [(None, {"col": c}) for c in (core, across, cross)]
-        self.partners += [(None, {"dp": 1 - dp}), (row <= 2, {"row": row + 1}), (row >= 1, {"row": row - 1})]
+        self.partners += [(None, {"dp": 1 - dp})] + [(None, {"row": lax.rem(row + k, 4)}) for k in range(1, 4)]
         half = self.pair_ref.shape[1] // 2
         top, low = pl.ds(0, half), pl.ds(half, half)
         y = 1 - dp
@@ -667,20 +666,37 @@
     pl.when(row >= 1)(to_left.wait_send)
     pl.when(row >= 1)(to_right.wait_recv)
     pl.when(row <= 2)(to_left.wait_recv)
-    for c in rest:
-        c.wait_recv()
-    for c in started:
-        c.wait_send()
-
-
-def head(tok, ranks_t, heads_t, gain_one, gain_two, gate_t, up_t, down, w_out, segments, inverse):
+
+    def end():
+        for c in rest:
+            c.wait_recv()
+        for c in started:
+            c.wait_send()
+
+    return end
+
+
+def head_attend_body(*refs):
+    head_in, cot_ref = refs[:11], refs[11]
+    outs, scratch = refs[12:30], refs[30:]
+    head_out = outs[:13]
+    o_ref, lse_ref, k_ref, v_ref, near_ref = outs[13:]
+    mixes_ref, q_ref, win_ref, seg_ref, rows_ref = (head_out[k] for k in (3, 7, 9, 10, 12))
+    end = head_body(*head_in, *head_out, *scratch[:6])
+    attend_body(
+        True, q_ref, win_ref, seg_ref, end, cot_ref, o_ref, lse_ref, k_ref, v_ref, rows_ref, near_ref, mixes_ref,
+        *scratch[6:],
+    )
+
+
+def head_attend(tok, ranks_t, heads_t, gain_one, gain_two, gate_t, up_t, down, w_out, segments, inverse, cot):
     rows, feat = tok.shape[1:]
     units = -(-gate_t.shape[0] // 8 // 16) * 16
     block = (ranks_t.shape[0] + GROUP_COLS, feat)
     ffn = (4, 3, units, feat)
     count = 3 + 4 + 4 + 6 + 3 + 3 + 3 + 4 + 4 + 2 + 5
     return pl.pallas_call(
-        head_body,
+        head_attend_body,
         out_shape=(
             jax.ShapeDtypeStruct(tok.shape, BF),
             jax.ShapeDtypeStruct((4, 8, feat), F32),
@@ -695,9 +711,11 @@
             jax.ShapeDtypeStruct((1, 5 * rows), jnp.int32),
             jax.ShapeDtypeStruct((rows, 2 * LANES), F32),
             jax.ShapeDtypeStruct((4,) + ffn, BF),
+            *attend_shapes(rows, 5 * rows),
+            jax.ShapeDtypeStruct((4,) + cot.shape, BF),
         ),
-        in_specs=[VMEM] * 11,
-        out_specs=(VMEM,) * 12 + (ANY,),
+        in_specs=[VMEM] * 11 + [ANY],
+        out_specs=(VMEM,) * 12 + (ANY,) + (VMEM,) * 4 + (ANY,),
         scratch_shapes=[
             pltpu.VMEM(block, BF),
             pltpu.VMEM((8, feat), F32),
@@ -705,10 +723,19 @@
             pltpu.VMEM((4, 4) + block, BF),
             pltpu.SemaphoreType.DMA((count,)),
             pltpu.SemaphoreType.DMA((count,)),
+            pltpu.VMEM((5 * rows, rows), F32),
+            pltpu.VMEM((2 * RK, 5 * rows, LANES), F32),
+            pltpu.SemaphoreType.DMA((22,)),
+            pltpu.SemaphoreType.DMA((22,)),
         ],
         compiler_params=comm_params(1),
-        cost_estimate=cost_of(2 * rows * D * 800 * 3, 14 << 20),
-    )(tok, ranks_t, heads_t, gain_one, gain_two, gate_t, up_t, down, w_out, segments, inverse)
+        cost_estimate=cost_of(2 * rows * D * (800 * 3 + 5 * rows * 16), 30 << 20),
+    )(tok, ranks_t, heads_t, gain_one, gain_two, gate_t, up_t, down, w_out, segments, inverse, cot)
+
+
+def window_lanes(ref, lanes):
+    value = ref[..., lanes]
+    return value.reshape(-1, value.shape[-1])
 
 
 def mask_bias(seg_ref, keys, rows):
@@ -724,25 +751,25 @@
 
 def attend_body(fast, q_ref, kf_ref, seg_ref, *refs):
     if fast:
-        _, cot_ref, _, o_ref, lse_ref, k_ref, v_ref, w_rows_ref, cot_near_ref, mixes_ref = refs[:10]
-        bias_ref, dup_ref, send_sem, recv_sem = refs[10:]
-        side_work = AttendCopies(cot_ref, w_rows_ref, cot_near_ref, mixes_ref, send_sem, recv_sem)
+        head_end, cot_ref, o_ref, lse_ref, k_ref, v_ref, w_rows_ref, cot_near_ref, mixes_ref = refs[:9]
+        bias_ref, dup_ref, send_sem, recv_sem = refs[9:]
+        side_work = AttendCopies(head_end, cot_ref, w_rows_ref, cot_near_ref, mixes_ref, send_sem, recv_sem)
         side_work.first()
     else:
         o_ref, lse_ref, k_ref, v_ref, bias_ref, dup_ref = refs
     rows = q_ref.shape[0]
-    keys = kf_ref.shape[0]
+    keys = seg_ref.shape[1]
     bias_ref[...] = mask_bias(seg_ref, keys, rows)
     for s in range(2 * RK):
-        tile = kf_ref[:, (s // 2) * LANES : (s // 2 + 1) * LANES].astype(F32)
+        tile = window_lanes(kf_ref, slice((s // 2) * LANES, (s // 2 + 1) * LANES)).astype(F32)
         dup_ref[s] = double_left(tile) if s % 2 == 0 else double_right(tile)
 
     def pair(p, carried):
         if fast:
-            pl.when(p == 2)(lambda: side_work.hand_on(0))
+            pl.when(p == 2)(side_work.early)
             pl.when(p == 4)(side_work.second)
         lanes = pl.ds(pl.multiple_of(p * LANES, LANES), LANES)
-        weights = kf_ref[:, 2 * LANES :]
+        weights = window_lanes(kf_ref, slice(2 * LANES, 3 * LANES))
         made = []
         for kind in range(2):
             acc = None
@@ -775,41 +802,24 @@
         side_work.last()
 
 
-def attend(q, kf_window, seg_window, w_rows=None, cot=None, mixes=None):
-    rows = q.shape[0]
-    keys = kf_window.shape[0]
-    fast = w_rows is not None
-    outs = [
+def attend_shapes(rows, keys):
+    return [
         jax.ShapeDtypeStruct((rows, D), BF),
         jax.ShapeDtypeStruct((H, 8, rows), F32),
         jax.ShapeDtypeStruct((keys, D), BF),
         jax.ShapeDtypeStruct((keys, D), BF),
     ]
-    scratch = [pltpu.VMEM((keys, rows), F32), pltpu.VMEM((2 * RK, keys, LANES), F32)]
-    in_specs, out_specs, more = [VMEM] * 3, [VMEM] * 4, []
-    if fast:
-        outs += [
-            jax.ShapeDtypeStruct(w_rows.shape, BF),
-            jax.ShapeDtypeStruct((4,) + cot.shape, BF),
-            jax.ShapeDtypeStruct(mixes.shape, BF),
-        ]
-        in_specs += [ANY] * 3
-        out_specs += [ANY] * 3
-        more = [w_rows, cot, mixes]
-        scratch += [
-            pltpu.SemaphoreType.DMA((22,)),
-            pltpu.SemaphoreType.DMA((22,)),
-        ]
-    return pl.pallas_call(
-        functools.partial(attend_body, fast),
-        out_shape=tuple(outs),
-        in_specs=in_specs,
-        out_specs=tuple(out_specs),
-        scratch_shapes=scratch,
-        input_output_aliases={3: 4, 5: 6} if fast else {},
-        compiler_params=comm_params(3) if fast else params(),
-        cost_estimate=cost_of(2 * rows * keys * D * 16, 16 << 20),
-    )(q, kf_window, seg_window, *more)
+
+
+def attend(q, kf_window, seg_window):
+    rows = q.shape[0]
+    keys = kf_window.shape[0]
+    return call(
+        functools.partial(attend_body, False),
+        tuple(attend_shapes(rows, keys)),
+        scratch=(pltpu.VMEM((keys, rows), F32), pltpu.VMEM((2 * RK, keys, LANES), F32)),
+        cost=cost_of(2 * rows * keys * D * 16, 16 << 20),
+    )(q, kf_window, seg_window)
 
 
 def attend_back_body(fast, q_ref, k_ref, v_ref, do_ref, lse_ref, kf_ref, seg_ref, *refs):
@@ -821,10 +831,10 @@
     else:
         dq_ref, dkf_ref, bias_ref, dup_ref, sum_ref, fac_ref = refs
     rows = q_ref.shape[0]
-    keys = kf_ref.shape[0]
+    keys = seg_ref.shape[1]
     bias_ref[...] = mask_bias(seg_ref, keys, rows)
     for s in range(2 * RK):
-        tile = kf_ref[:, (s // 2) * LANES : (s // 2 + 1) * LANES].astype(F32)
+        tile = window_lanes(kf_ref, slice((s // 2) * LANES, (s // 2 + 1) * LANES)).astype(F32)
         dup_ref[s] = double_left(tile) if s % 2 == 0 else double_right(tile)
     sum_ref[...] = jnp.zeros_like(sum_ref)
     fac_ref[...] = jnp.zeros_like(fac_ref)
@@ -864,7 +874,7 @@
             d_k = part_k if d_k is None else d_k + part_k
             d_v = part_v if d_v is None else d_v + part_v
         dq_ref[:, lanes] = jnp.concatenate(d_q, axis=0).T * HD**-0.5
-        weights = kf_ref[:, 2 * LANES :]
+        weights = window_lanes(kf_ref, slice(2 * LANES, 3 * LANES))
         for kind, grad in ((0, d_k), (1, d_v)):
             for s in range(RK):
                 slot = kind * RK + s
@@ -880,63 +890,31 @@
         first = first + pltpu.roll(first, HD, 1)
         second = second + pltpu.roll(second, HD, 1)
         merged = jnp.where(lane_iota(first.shape) < HD, first, second)
-        dkf_ref[:, tile * LANES : (tile + 1) * LANES] = (merged / RK).astype(BF)
-    dkf_ref[:, 2 * LANES :] = (fac_ref[...] / RK).astype(BF)
+        blocks = dkf_ref.shape[:-1] + (LANES,)
+        dkf_ref[..., tile * LANES : (tile + 1) * LANES] = (merged / RK).astype(BF).reshape(blocks)
+    dkf_ref[..., 2 * LANES :] = (fac_ref[...] / RK).astype(BF).reshape(blocks)
     if fast:
         side_work.last()
 
 
-def attend_back(q, k, v, d_heads, lse, kf_window, seg_window, *more):
-    rows = q.shape[0]
-    keys = kf_window.shape[0]
-    fast = len(more) > 0
-    outs = [jax.ShapeDtypeStruct((rows, D), F32), jax.ShapeDtypeStruct(kf_window.shape, BF)]
-    scratch = [
+def back_scratch(rows, keys):
+    return [
         pltpu.VMEM((keys, rows), F32),
         pltpu.VMEM((2 * RK, keys, LANES), F32),
         pltpu.VMEM((2 * RK, keys, LANES), F32),
         pltpu.VMEM((keys, LANES), F32),
     ]
-    in_specs, out_specs = [VMEM] * 7, [VMEM] * 2
-    if fast:
-        in_specs += [ANY, VMEM, ANY, ANY, VMEM]
-        grads, g_out = more[2], more[3]
-        parts, feat = g_out.shape[1], g_out.shape[3]
-        block, hop = g_out.shape[2:], grads.shape[1:]
-        outs += [
-            jax.ShapeDtypeStruct((parts, rows, feat), BF),
-            jax.ShapeDtypeStruct((2,) + hop, BF),
-            jax.ShapeDtypeStruct((4,) + block, BF),
-        ]
-        out_specs += [ANY, ANY, VMEM]
-        scratch += [
-            pltpu.VMEM((2, rows // 2, D), BF),
-            pltpu.VMEM((2, rows // 2, D), BF),
-            pltpu.VMEM((2, rows, D), BF),
-            pltpu.VMEM((parts, rows, feat), BF),
-            pltpu.VMEM((2,) + hop, BF),
-            pltpu.VMEM((2,) + hop, BF),
-            pltpu.VMEM((2,) + hop, BF),
-            pltpu.VMEM((2, 4) + block, BF),
-            pltpu.VMEM((4,) + block, BF),
-            pltpu.VMEM((4,) + block, BF),
-            pltpu.VMEM((2, rows // 2, D), BF),
-            pltpu.VMEM((rows, D), BF),
-            pltpu.VMEM(grads.shape, BF),
-            pltpu.VMEM((2, 4) + block, BF),
-            pltpu.SemaphoreType.DMA((25,)),
-            pltpu.SemaphoreType.DMA((25,)),
-            pltpu.SemaphoreType.DMA((13,)),
-        ]
-    return pl.pallas_call(
-        functools.partial(attend_back_body, fast),
-        out_shape=tuple(outs),
-        in_specs=in_specs,
-        out_specs=tuple(out_specs),
-        scratch_shapes=scratch,
-        compiler_params=comm_params(6) if fast else params(),
-        cost_estimate=cost_of(2 * rows * keys * D * 40, 16 << 20),
-    )(q, k, v, d_heads, lse, kf_window, seg_window, *more)
+
+
+def attend_back(q, k, v, d_heads, lse, kf_window, seg_window):
+    rows = q.shape[0]
+    keys = kf_window.shape[0]
+    return call(
+        functools.partial(attend_back_body, False),
+        (jax.ShapeDtypeStruct((rows, D), F32), jax.ShapeDtypeStruct(kf_window.shape, BF)),
+        scratch=back_scratch(rows, keys),
+        cost=cost_of(2 * rows * keys * D * 40, 16 << 20),
+    )(q, k, v, d_heads, lse, kf_window, seg_window)
 
 
 def mixing_body(x_ref, heads_ref, w_out_ref, gain_ref, mixed_ref, h_ref):
@@ -1479,11 +1457,6 @@
     x, mine = col // 2, lax.rem(col, 2)
     y = 1 - dp
     order = [lax.rem(row + k, 4) for k in (1, 2, 3, 0)]
-    greet(
-        [(None, {"col": c}) for c in (core, across, cross)]
-        + [(None, {"row": r}) for r in order[:3]]
-        + [(None, {"dp": y})]
-    )
     mover = Mover(send_sem, recv_sem)
     started = []
 
@@ -1593,19 +1566,36 @@
     own.wait()
 
 
-def tail(win, dq, hf, bq, turn, w_rh, h, x_parts, gains, d_mixed, g_two, g_rows, ends, part):
-    rows = dq.shape[0]
-    parts, _, feat = x_parts.shape
+def back_tail_body(*refs):
+    attend_in, side_in, tail_in = refs[:7], refs[7:12], refs[12:21]
+    out_ref, *tail_out = refs[21:28]
+    scratch = refs[28:]
+    dq_ref, dkf_ref, ends_ref, part_ref = scratch[:4]
+    hf_ref, bq_ref, turn_ref, w_ref, h_ref, x_ref, gain_ref, d_mixed_ref, g_two_ref = tail_in
+    attend_back_body(
+        True, *attend_in, *side_in, dq_ref, dkf_ref, out_ref, ends_ref, part_ref, *scratch[4:25]
+    )
+    tail_body(
+        dkf_ref, dq_ref, hf_ref, bq_ref, turn_ref, w_ref, h_ref, x_ref, gain_ref, d_mixed_ref, g_two_ref,
+        side_in[2], ends_ref, part_ref, *tail_out, *scratch[25:],
+    )
+
+
+def back_tail(attend_in, side_in, tail_in):
+    kf_window, g_rows, g_out = attend_in[5], side_in[2], side_in[3]
+    x_parts = tail_in[5]
+    parts, rows, feat = x_parts.shape
     units = g_rows.shape[2]
     block = (RANK_COLS // 4 + GROUP_COLS, feat)
     cols = (parts, 3, units, feat)
-    mix = part.shape[1:]
+    mix = g_out.shape[2:]
     wide = g_rows.shape[1:]
-    slot = win.shape[1:]
+    slot = kf_window.shape[1:]
     count = 2 + 2 + 3 + 8 + 4 + 3 + 1 + 1 + 3 + 3 + 3 + 1
     return pl.pallas_call(
-        tail_body,
+        back_tail_body,
         out_shape=(
+            jax.ShapeDtypeStruct(x_parts.shape, BF),
             jax.ShapeDtypeStruct(block, F32),
             jax.ShapeDtypeStruct(x_parts.shape, BF),
             jax.ShapeDtypeStruct(cols, BF),
@@ -1613,9 +1603,35 @@
             jax.ShapeDtypeStruct(mix, BF),
             jax.ShapeDtypeStruct(mix, BF),
         ),
-        in_specs=[VMEM] * 11 + [ANY, VMEM, VMEM],
-        out_specs=(VMEM, ANY, VMEM, ANY, VMEM, ANY),
+        in_specs=[VMEM] * 7 + [ANY, VMEM, ANY, ANY, VMEM] + [VMEM] * 9,
+        out_specs=(ANY, VMEM, ANY, VMEM, ANY, VMEM, ANY),
         scratch_shapes=[
+            pltpu.VMEM((rows, D), F32),
+            pltpu.VMEM(kf_window.shape, BF),
+            pltpu.VMEM((2,) + wide, BF),
+            pltpu.VMEM((4,) + mix, BF),
+        ]
+        + back_scratch(rows, 5 * rows)
+        + [
+            pltpu.VMEM((2, rows // 2, D), BF),
+            pltpu.VMEM((2, rows // 2, D), BF),
+            pltpu.VMEM((2, rows, D), BF),
+            pltpu.VMEM((parts, rows, feat), BF),
+            pltpu.VMEM((2,) + wide, BF),
+            pltpu.VMEM((2,) + wide, BF),
+            pltpu.VMEM((2,) + wide, BF),
+            pltpu.VMEM((2, 4) + mix, BF),
+            pltpu.VMEM((4,) + mix, BF),
+            pltpu.VMEM((4,) + mix, BF),
+            pltpu.VMEM((2, rows // 2, D), BF),
+            pltpu.VMEM((rows, D), BF),
+            pltpu.VMEM(g_rows.shape, BF),
+            pltpu.VMEM((2, 4) + mix, BF),
+            pltpu.SemaphoreType.DMA((25,)),
+            pltpu.SemaphoreType.DMA((25,)),
+            pltpu.SemaphoreType.DMA((13,)),
+        ]
+        + [
             pltpu.VMEM((rows, ALL_COLS), BF),
             pltpu.VMEM(x_parts.shape, BF),
             pltpu.VMEM((2,) + slot, BF),
@@ -1637,8 +1653,8 @@
             pltpu.SemaphoreType.DMA((2,)),
         ],
         compiler_params=comm_params(7),
-        cost_estimate=cost_of(2 * rows * D * 800 * 6, 24 << 20),
-    )(win, dq, hf, bq, turn, w_rh, h, x_parts, gains, d_mixed, g_two, g_rows, ends, part)
+        cost_estimate=cost_of(2 * rows * 5 * rows * D * 40, 40 << 20),
+    )(*attend_in, *side_in, *tail_in)
 
 
 def layout_body(
@@ -1746,26 +1762,21 @@
 
     groups = [[m * subs + s for s in range(subs)] for m in range(micro)]
     if fast:
+        cot_rows = cotangent.reshape(micro * row_tokens, feat)
         (
-            x_parts, gains, ffn_parts, mixes, h_one, head_fac, bq_rot, queries, w_rh, kf_window, seg_window, turn, w_rows
-        ) = head(
+            x_parts, gains, ffn_parts, mixes, h_one, head_fac, bq_rot, queries, w_rh, kf_window, seg_window, turn, w_rows,
+            heads_out, lse, key_all, value_all, cot_near,
+        ) = head_attend(
             tokens, w_ranks.T, w_heads.T, gain_attn.reshape(1, feat), gain_ffn.reshape(1, feat), w_gate.T, w_up.T,
-            w_down, w_out, segments, jnp.concatenate([inverse] * 4).reshape(1, LANES),
-        )
-        kf_window = kf_window.reshape(keys, -1)
-        cot_rows = cotangent.reshape(micro * row_tokens, feat)
-        heads_out, lse, key_all, value_all, w_rows, cot_near, mixes = attend(
-            queries, kf_window, seg_window, w_rows, cot_rows, mixes
+            w_down, w_out, segments, jnp.concatenate([inverse] * 4).reshape(1, LANES), cot_rows,
         )
         mixed, d_mixed, d_heads, g_out, g_gain_two, g_rows, out_pair, hop = middle(
             x_parts, heads_out, mixes, gains, cot_rows, cot_near, ffn_parts, w_rows
         )
-        d_q, d_kf, output, g_ends, g_part = attend_back(
-            queries, key_all, value_all, d_heads, lse, kf_window, seg_window, out_pair, mixed, g_rows, g_out, hop
-        )
-        g_rh, grad_input, g_cols, cols_other, g_out, out_other = tail(
-            d_kf.reshape(past + 1, rows, -1), d_q, head_fac, bq_rot, turn, w_rh, h_one, x_parts, gains, d_mixed,
-            g_gain_two, g_rows, g_ends, g_part,
+        output, g_rh, grad_input, g_cols, cols_other, g_out, out_other = back_tail(
+            (queries, key_all, value_all, d_heads, lse, kf_window, seg_window),
+            (out_pair, mixed, g_rows, g_out, hop),
+            (head_fac, bq_rot, turn, w_rh, h_one, x_parts, gains, d_mixed, g_gain_two),
         )
         grad_input, g_one, g_two, own_heads, own_ranks, g_out, own_gate, own_up, own_down = layout(
             g_rh, grad_input, g_cols, cols_other, g_out, out_other, w_heads.shape[1], w_ranks.shape[1], ffn_local

time: 237 us -> 229 us (0.966)
  Pallas kernels: 234 us -> 226 us
    pallas_call x4 -> x2, Pallas kernels: 177 us -> 168 us  [the longest x1 89.2 us: back_tail(): pl.pallas_call(back_tail_body, out_shape=(jax.ShapeDtypeStruct(x_parts.sh...]
where the time goes in v2:
time: 229 us; the launch traced here: 228 us
  Pallas kernels  226 us (99%)
    pallas_call x1, Pallas kernels, back_tail(): pl.pallas_call(back_tail_body, out_shape=(jax.ShapeDtypeStruct(x_parts.sh...  89.2 us
    pallas_call x1, Pallas kernels, head_attend(): pl.pallas_call(head_attend_body, out_shape=(jax.ShapeDtypeStruct(tok.shap...  78.9 us
    pallas_call x1, Pallas kernels, middle(): pl.pallas_call(middle_body, out_shape=(jax.ShapeDtypeStruct((rows, D), F3...  54.4 us

profile of v2, /device:TPU:0, one launch (start us, length us, event | category | flops | bytes accessed | tf_op | source)
XLA Modules:
  0.0 228.0 jit_solution(2577851404465310971)
XLA Ops:
  0.7 0.6 maximum_bitcast_fusion.refs_10_
  1.2 78.9 %shard_map.186 = (bf16[4,256,256]{2,1,0:T(8,128)(2,1)}, f32[4,8,256]{2,1,0:T(8,128)}, bf16[4,3,96,256]{3,2,1,0:T(8,128)(2,1)}, bf16[4,4,256,256]{3,2,1,0:T(8,128...) custom-call(bf16[4,256,256]{2,1,0:T(8,128)(2,1)} %bitcast.22, ...), custom_call_target="tpu_custom_call" | custom-call | flops 11995709440 | bytes 31457280 | tf_op jit(solution)/shard_map/pallas_call | solution.py:698
  80.1 54.4 %shard_map.187 = (f32[256,1024]{1,0:T(8,128)}, f32[256,1024]{1,0:T(8,128)}, bf16[256,1024]{1,0:T(8,128)(2,1)}, bf16[4,4,256,256]{3,2,1,0:T(8,128)(2,1)}, f32[1,1...) custom-call(bf16[4,256,256]{2,1,0:T(8,128)(2,1)} %get-tuple-element., ...), custom_call_target="tpu_custom_call" | custom-call | flops 14495514624 | bytes 25165824 | tf_op jit(solution)/shard_map/pallas_call | solution.py:1300
  134.5 89.2 %shard_map.188 = (bf16[4,256,256]{2,1,0:T(8,128)(2,1)}, f32[208,256]{1,0:T(8,128)}, bf16[4,256,256]{2,1,0:T(8,128)(2,1)}, bf16[4,3,96,256]{3,2,1,0:T(8,128)(2,1)...) custom-call(bf16[256,1024]{1,0:T(8,128)(2,1)} %get-tuple-element.52.refs_0_, ...), custom_call_target="tpu_custom_call" | custom-call | flops 26843545600 | bytes 41943040 | tf_op jit(solution)/shard_map/pallas_call | solution.py:1595
  223.7 0.0 copy-start
  223.7 3.5 %shard_map.189 = (f32[4,256,256]{2,1,0:T(8,128)}, f32[1,256]{1,0:T(1,128)}, f32[1,256]{1,0:T(1,128)}, f32[40,256]{1,0:T(8,128)}, f32[160,256]{1,0:T(8,128)}, /*i...) custom-call(f32[208,256]{1,0:T(8,128)} %get-tuple-element.79.grad_ref, ...), custom_call_target="tpu_custom_call" | custom-call | bytes 8388608 | tf_op jit(solution)/shard_map/pallas_call | solution.py:1692
  227.2 0.0 copy-done
  227.2 0.8 copy.22
  (1 shorter events, 0.0 us)
Async XLA Ops:
  223.7 3.5 %copy-start = (bf16[4,256,256]{2,1,0:T(8,128)(2,1)S(1)}, bf16[4,256,256]{2,1,0:T(8,128)(2,1)}, u32[]{:S(2)}) copy-start(bf16[4,256,256]{2,1,0:T(8,128)(2,1)} %get-tuple-element.78) | copy-start | bytes 1572868

commit v3 on v2

--- a/solution.py
+++ b/solution.py
@@ -2,6 +2,7 @@
 
 import jax
 import jax.numpy as jnp
+import numpy as np
 from jax import lax
 from jax.experimental import pallas as pl
 from jax.experimental.pallas import tpu as pltpu
@@ -676,17 +677,45 @@
     return end
 
 
+KEPT = (0, 2, 3, 4, 5, 6, 7, 8, 9, 11)
+
+
 def head_attend_body(*refs):
     head_in, cot_ref = refs[:11], refs[11]
     outs, scratch = refs[12:30], refs[30:]
-    head_out = outs[:13]
-    o_ref, lse_ref, k_ref, v_ref, near_ref = outs[13:]
+    kept = dict(zip(KEPT, scratch[10:20]))
+    tiles = scratch[20:23]
+    keep_sem, tile_sem = scratch[23:]
+    head_out = [kept.get(k, outs[k]) for k in range(13)]
+    o_out, lse_ref, k_out, v_out, near_ref = outs[13:]
     mixes_ref, q_ref, win_ref, seg_ref, rows_ref = (head_out[k] for k in (3, 7, 9, 10, 12))
     end = head_body(*head_in, *head_out, *scratch[:6])
+    copies = [pltpu.make_async_copy(kept[k], outs[k], keep_sem.at[n]) for n, k in enumerate(KEPT)]
+    for k, c in zip(KEPT, copies):
+        if k != 3:
+            c.start()
+
+    def tile_copies(p):
+        lanes = pl.ds(pl.multiple_of(p * LANES, LANES), LANES)
+        return [
+            pltpu.make_async_copy(source.at[:, lanes], target.at[:, lanes], tile_sem.at[n, p])
+            for n, (source, target) in enumerate(zip(tiles, (o_out, k_out, v_out)))
+        ]
+
+    def store(p):
+        for c in tile_copies(p):
+            c.start()
+
     attend_body(
-        True, q_ref, win_ref, seg_ref, end, cot_ref, o_ref, lse_ref, k_ref, v_ref, rows_ref, near_ref, mixes_ref,
-        *scratch[6:],
+        True, q_ref, win_ref, seg_ref, end, cot_ref, tiles[0], lse_ref, tiles[1], tiles[2], rows_ref, near_ref,
+        mixes_ref, *scratch[6:10], store=store,
     )
+    copies[KEPT.index(3)].start()
+    for p in range(PAIRS):
+        for c in tile_copies(p):
+            c.wait()
+    for c in copies:
+        c.wait()
 
 
 def head_attend(tok, ranks_t, heads_t, gain_one, gain_two, gate_t, up_t, down, w_out, segments, inverse, cot):
@@ -695,27 +724,31 @@
     block = (ranks_t.shape[0] + GROUP_COLS, feat)
     ffn = (4, 3, units, feat)
     count = 3 + 4 + 4 + 6 + 3 + 3 + 3 + 4 + 4 + 2 + 5
+    outs = (
+        jax.ShapeDtypeStruct(tok.shape, BF),
+        jax.ShapeDtypeStruct((4, 8, feat), F32),
+        jax.ShapeDtypeStruct(ffn, BF),
+        jax.ShapeDtypeStruct((4, 4) + w_out.shape, BF),
+        jax.ShapeDtypeStruct((rows, D), BF),
+        jax.ShapeDtypeStruct((rows, HEAD_COLS), F32),
+        jax.ShapeDtypeStruct((rows, RQ * HD), F32),
+        jax.ShapeDtypeStruct((rows, D), BF),
+        jax.ShapeDtypeStruct((ALL_COLS, D), BF),
+        jax.ShapeDtypeStruct((5, rows, 3 * LANES), BF),
+        jax.ShapeDtypeStruct((1, 5 * rows), jnp.int32),
+        jax.ShapeDtypeStruct((rows, 2 * LANES), F32),
+        jax.ShapeDtypeStruct((4,) + ffn, BF),
+        *attend_shapes(rows, 5 * rows),
+        jax.ShapeDtypeStruct((4,) + cot.shape, BF),
+    )
+    out_specs = [VMEM] * 12 + [ANY] + [ANY, VMEM, ANY, ANY] + [ANY]
+    for k in KEPT:
+        out_specs[k] = ANY
     return pl.pallas_call(
         head_attend_body,
-        out_shape=(
-            jax.ShapeDtypeStruct(tok.shape, BF),
-            jax.ShapeDtypeStruct((4, 8, feat), F32),
-            jax.ShapeDtypeStruct(ffn, BF),
-            jax.ShapeDtypeStruct((4, 4) + w_out.shape, BF),
-            jax.ShapeDtypeStruct((rows, D), BF),
-            jax.ShapeDtypeStruct((rows, HEAD_COLS), F32),
-            jax.ShapeDtypeStruct((rows, RQ * HD), F32),
-            jax.ShapeDtypeStruct((rows, D), BF),
-            jax.ShapeDtypeStruct((ALL_COLS, D), BF),
-            jax.ShapeDtypeStruct((5, rows, 3 * LANES), BF),
-            jax.ShapeDtypeStruct((1, 5 * rows), jnp.int32),
-            jax.ShapeDtypeStruct((rows, 2 * LANES), F32),
-            jax.ShapeDtypeStruct((4,) + ffn, BF),
-            *attend_shapes(rows, 5 * rows),
-            jax.ShapeDtypeStruct((4,) + cot.shape, BF),
-        ),
+        out_shape=outs,
         in_specs=[VMEM] * 11 + [ANY],
-        out_specs=(VMEM,) * 12 + (ANY,) + (VMEM,) * 4 + (ANY,),
+        out_specs=tuple(out_specs),
         scratch_shapes=[
             pltpu.VMEM(block, BF),
             pltpu.VMEM((8, feat), F32),
@@ -727,7 +760,9 @@
             pltpu.VMEM((2 * RK, 5 * rows, LANES), F32),
             pltpu.SemaphoreType.DMA((22,)),
             pltpu.SemaphoreType.DMA((22,)),
-        ],
+        ]
+        + [pltpu.VMEM(outs[k].shape, outs[k].dtype) for k in KEPT + (13, 15, 16)]
+        + [pltpu.SemaphoreType.DMA((len(KEPT),)), pltpu.SemaphoreType.DMA((3, PAIRS))],
         compiler_params=comm_params(1),
         cost_estimate=cost_of(2 * rows * D * (800 * 3 + 5 * rows * 16), 30 << 20),
     )(tok, ranks_t, heads_t, gain_one, gain_two, gate_t, up_t, down, w_out, segments, inverse, cot)
@@ -749,7 +784,7 @@
     return jnp.where(same & (key_idx <= query_idx), 0.0, NEG)
 
 
-def attend_body(fast, q_ref, kf_ref, seg_ref, *refs):
+def attend_body(fast, q_ref, kf_ref, seg_ref, *refs, store=None):
     if fast:
         head_end, cot_ref, o_ref, lse_ref, k_ref, v_ref, w_rows_ref, cot_near_ref, mixes_ref = refs[:9]
         bias_ref, dup_ref, send_sem, recv_sem = refs[9:]
@@ -795,6 +830,8 @@
             outs.append(nn(v_turned[side * HD : (side + 1) * HD], probs))
             lse_ref[2 * p + side] = jnp.broadcast_to(peak + jnp.log(total), (8, rows))
         o_ref[:, lanes] = jnp.concatenate(outs, axis=0).T.astype(BF)
+        if fast:
+            store(p)
         return carried
 
     lax.fori_loop(0, PAIRS, pair, 0)
@@ -822,7 +859,7 @@
     )(q, kf_window, seg_window)
 
 
-def attend_back_body(fast, q_ref, k_ref, v_ref, do_ref, lse_ref, kf_ref, seg_ref, *refs):
+def attend_back_body(fast, q_ref, k_ref, v_ref, do_ref, lse_ref, kf_ref, seg_ref, *refs, load=None):
     if fast:
         dq_ref, dkf_ref = refs[5:7]
         bias_ref, dup_ref, sum_ref, fac_ref = refs[10:14]
@@ -845,6 +882,7 @@
             pl.when(p == 3)(side_work.second)
             pl.when(p == 4)(side_work.last_hop)
             pl.when(p == 6)(side_work.third)
+            load(p)
         lanes = pl.ds(pl.multiple_of(p * LANES, LANES), LANES)
         k_tile = k_ref[:, lanes]
         v_tile = v_ref[:, lanes]
@@ -880,7 +918,8 @@
                 slot = kind * RK + s
                 pick = spread(LANES, slot * H + 2 * p, LANES)
                 sum_ref[slot] += nn(weights, pick) * grad
-                fac_ref[...] += two_pass(grad * dup_ref[slot], collect(LANES, LANES, slot * H + 2 * p))
+                product = (grad * dup_ref[slot]).astype(BF)
+                fac_ref[...] += nn(product, collect(LANES, LANES, slot * H + 2 * p))
         return carried
 
     lax.fori_loop(0, PAIRS, pair, 0)
@@ -1040,9 +1079,10 @@
 
 def middle_body(
     x_ref, heads_ref, w_out_ref, gain_ref, cot_own_ref, cot_in_ref, w_own_ref, rows_ref,
-    mixed_ref, d_mixed_ref, d_heads_ref, g_out_ref, g_gain_ref, g_ref, out_pair_ref, hop_ref,
+    mixed_out, d_mixed_ref, d_heads_ref, g_out_ref, g_gain_ref, g_hbm, out_pair_hbm, hop_ref,
     w_ref, h_ref, cot_ref, hid_ref, dg_ref, du_ref, back_ref, fwd_ref, back_got_ref, fwd_got_ref,
     pair_ref, diag_ref, far_ref, send_sem, recv_sem, w_sem, cot_sem,
+    mixed_ref, g_ref, out_pair_ref, leave_sem,
 ):
     row = lax.axis_index("row")
     col, core, across = neighbours()
@@ -1103,6 +1143,14 @@
         lanes = slice(c * feat, (c + 1) * feat)
         h_ref[0, me, :, lanes] = (mixed_ref[:, lanes] * scale * gain_ref[c, 1:2]).astype(BF)
 
+    leave = [
+        pltpu.make_async_copy(source, target, leave_sem.at[n])
+        for n, (source, target) in enumerate(
+            ((mixed_ref, mixed_out), (g_ref, g_hbm), (out_pair_ref, out_pair_hbm))
+        )
+    ]
+    leave[0].start()
+
     half = rows // 2
     top, low = pl.ds(0, half), pl.ds(half, half)
 
@@ -1132,14 +1180,14 @@
     back_near = [[mover.copy(back_ref.at[1, s, p], back_got_ref.at[s, p], col=core) for s, p in two] for two in steps]
     fwd_near = [[mover.copy(fwd_ref.at[1, s, p], fwd_got_ref.at[s, p], col=core) for s, p in two] for two in steps]
     diag = [
-        mover.copy(pair_ref.at[on_both, top], diag_ref.at[0], col=across),
-        mover.copy(pair_ref.at[on_both, low], diag_ref.at[1], dp=y),
+        mover.copy(pair_ref.at[on_both, low], diag_ref.at[0], col=across),
+        mover.copy(pair_ref.at[on_both, top], diag_ref.at[1], dp=y),
     ]
     far = [
+        mover.copy(pair_ref.at[on_x, low], far_ref.at[0, low], col=across),
+        mover.copy(pair_ref.at[on_y, top], far_ref.at[1, top], dp=y),
+        mover.copy(pair_ref.at[on_y, low], far_ref.at[1, low], dp=y),
         mover.copy(pair_ref.at[on_x, top], far_ref.at[0, top], col=across),
-        mover.copy(pair_ref.at[on_y, low], far_ref.at[1, low], dp=y),
-        mover.copy(pair_ref.at[on_y, top], far_ref.at[1, top], dp=y),
-        mover.copy(pair_ref.at[on_x, low], far_ref.at[0, low], col=across),
     ]
 
     def add_pair(k):
@@ -1183,6 +1231,8 @@
             for c in near_second:
                 c.wait_recv()
             add_pair(1)
+            far[0].start()
+            far[1].start()
 
         @pl.when(t == 6)
         def _():
@@ -1194,8 +1244,6 @@
         def _():
             near_both.wait_recv()
             add_pair(2)
-            far[0].start()
-            far[1].start()
 
         name, side = t // 2, lax.rem(t, 2)
         first_dp = lax.rem(dp + jnp.where(name == 3, 1, 0), 2)
@@ -1255,19 +1303,17 @@
 
     gradient(0, dg_ref, h_ref)
     gradient(1, du_ref, h_ref)
-    for k, (s, part) in enumerate(((on_y, top), (on_x, low))):
-        if k == 1:
-            far[0].wait_send()
-        else:
-            far[1].wait_send()
+    for k, (s, part) in enumerate(((on_y, low), (on_x, top))):
         diag[k].wait_recv()
         pair_ref[s, part] = (pair_ref[s, part].astype(F32) + diag_ref[k].astype(F32)).astype(BF)
         far[2 + k].start()
     gradient(2, hid_ref, cot_ref)
+    leave[1].start()
     for two, copies in zip(steps, fwd_near):
         for (s, p), c in zip(two, copies):
             c.wait_recv()
             out_pair_ref[s, p] = (fwd_ref[0, s, p].astype(F32) + fwd_got_ref[s, p].astype(F32)).astype(BF)
+    leave[2].start()
     add_pair(0)
     for c in far:
         c.wait_recv()
@@ -1281,8 +1327,10 @@
     for two in back_near + fwd_near:
         for c in two:
             c.wait_send()
-    for c in diag + far[2:]:
+    for c in diag + far:
         c.wait_send()
+    for c in leave:
+        c.wait()
     for to_right, to_left in hops:
         pl.when(row == 0)(to_right.wait_send)
         pl.when(row == 3)(to_left.wait_send)
@@ -1310,7 +1358,7 @@
             jax.ShapeDtypeStruct((3, units, D), BF),
         ),
         in_specs=[VMEM] * 4 + [ANY] * 4,
-        out_specs=(VMEM,) * 7 + (ANY,),
+        out_specs=(ANY,) + (VMEM,) * 4 + (ANY,) * 3,
         scratch_shapes=[pltpu.VMEM((3, 4 * units, D), BF), square_of, square_of]
         + [hidden_of] * 3
         + [square_of, square_of, quarter, quarter, quarter]
@@ -1321,6 +1369,10 @@
             pltpu.SemaphoreType.DMA((count,)),
             pltpu.SemaphoreType.DMA((4, 4)),
             pltpu.SemaphoreType.DMA((4, 4)),
+            pltpu.VMEM((rows, D), F32),
+            pltpu.VMEM((4, 3, units, D), BF),
+            quarter,
+            pltpu.SemaphoreType.DMA((3,)),
         ],
         compiler_params=comm_params(4),
         cost_estimate=cost_of(2 * 8 * rows * 9 * D * 4 * units, 24 << 20),
@@ -1571,10 +1623,39 @@
     out_ref, *tail_out = refs[21:28]
     scratch = refs[28:]
     dq_ref, dkf_ref, ends_ref, part_ref = scratch[:4]
-    hf_ref, bq_ref, turn_ref, w_ref, h_ref, x_ref, gain_ref, d_mixed_ref, g_two_ref = tail_in
+    gain_ref, g_two_ref = tail_in[6], tail_in[8]
+    q_ref, k_hbm, v_hbm, *attend_rest = attend_in
+    pair_in, mixed_hbm, *side_rest = side_in
+    *scratch, k_ref, v_ref, mixed_ref, hf_ref, bq_ref, turn_ref, w_ref, h_ref, x_ref, d_mixed_ref = scratch[:-2]
+    tile_sem, load_sem = refs[-2:]
+
+    def tile_copies(p):
+        lanes = pl.ds(pl.multiple_of(p * LANES, LANES), LANES)
+        return [
+            pltpu.make_async_copy(source.at[:, lanes], target.at[:, lanes], tile_sem.at[n, p])
+            for n, (source, target) in enumerate(((k_hbm, k_ref), (v_hbm, v_ref)))
+        ]
+
+    for p in range(PAIRS):
+        for c in tile_copies(p):
+            c.start()
+    sources = (mixed_hbm, *(tail_in[k] for k in (0, 1, 2, 3, 4, 5, 7)))
+    targets = (mixed_ref, hf_ref, bq_ref, turn_ref, w_ref, h_ref, x_ref, d_mixed_ref)
+    loads = [pltpu.make_async_copy(a, b, load_sem.at[n]) for n, (a, b) in enumerate(zip(sources, targets))]
+    for c in loads:
+        c.start()
+
+    def load(p):
+        for c in tile_copies(p):
+            c.wait()
+        pl.when(p == 5)(loads[0].wait)
+
     attend_back_body(
-        True, *attend_in, *side_in, dq_ref, dkf_ref, out_ref, ends_ref, part_ref, *scratch[4:25]
+        True, q_ref, k_ref, v_ref, *attend_rest, pair_in, mixed_ref, *side_rest, dq_ref, dkf_ref, out_ref, ends_ref,
+        part_ref, *scratch[4:25], load=load,
     )
+    for c in loads[1:]:
+        c.wait()
     tail_body(
         dkf_ref, dq_ref, hf_ref, bq_ref, turn_ref, w_ref, h_ref, x_ref, gain_ref, d_mixed_ref, g_two_ref,
         side_in[2], ends_ref, part_ref, *tail_out, *scratch[25:],
@@ -1603,7 +1684,7 @@
             jax.ShapeDtypeStruct(mix, BF),
             jax.ShapeDtypeStruct(mix, BF),
         ),
-        in_specs=[VMEM] * 7 + [ANY, VMEM, ANY, ANY, VMEM] + [VMEM] * 9,
+        in_specs=[VMEM, ANY, ANY] + [VMEM] * 4 + [ANY] * 4 + [VMEM] + [ANY] * 6 + [VMEM, ANY, VMEM],
         out_specs=(ANY, VMEM, ANY, VMEM, ANY, VMEM, ANY),
         scratch_shapes=[
             pltpu.VMEM((rows, D), F32),
@@ -1651,17 +1732,23 @@
             pltpu.SemaphoreType.DMA((count,)),
             pltpu.SemaphoreType.DMA((count,)),
             pltpu.SemaphoreType.DMA((2,)),
-        ],
+        ]
+        + [
+            pltpu.VMEM(a.shape, a.dtype)
+            for a in (attend_in[1], attend_in[2], side_in[1], *(tail_in[k] for k in (0, 1, 2, 3, 4, 5, 7)))
+        ]
+        + [pltpu.SemaphoreType.DMA((2, PAIRS)), pltpu.SemaphoreType.DMA((8,))],
         compiler_params=comm_params(7),
         cost_estimate=cost_of(2 * rows * 5 * rows * D * 40, 40 << 20),
     )(*attend_in, *side_in, *tail_in)
 
 
 def layout_body(
-    grad_ref, gi_ref, cols_ref, other_ref, mix_ref, mix_other_ref,
-    gi_out_ref, gain_ref, gain_two_ref, heads_ref, ranks_ref, out_ref, gate_ref, up_ref, down_ref,
+    grad_ref, gi_ref, cols_ref, other_ref, mix_ref, mix_other_ref, y_ref,
+    y_out_ref, gi_out_ref, gain_ref, gain_two_ref, heads_ref, ranks_ref, out_ref, gate_ref, up_ref, down_ref,
 ):
     first = lax.axis_index("dp") == 0
+    y_out_ref[...] = y_ref[...]
     gi_out_ref[...] = gi_ref[...].astype(F32)
     out_ref[...] = mix_ref[...].astype(F32) + mix_other_ref[...].astype(F32)
     ranks = ranks_ref.shape[0]
@@ -1685,13 +1772,14 @@
             target[(4 + c) * part : (5 + c) * part] = jnp.where(first, other, own)
 
 
-def layout(grad, gi, cols, other, mix, mix_other, heads, ranks, hidden):
+def layout(grad, gi, cols, other, mix, mix_other, y, heads, ranks, hidden):
     feat = grad.shape[1]
     weight = jax.ShapeDtypeStruct((hidden, feat), F32)
     gain = jax.ShapeDtypeStruct((1, feat), F32)
     return call(
         layout_body,
         (
+            jax.ShapeDtypeStruct(y.shape, y.dtype),
             jax.ShapeDtypeStruct(gi.shape, F32),
             gain,
             gain,
@@ -1703,7 +1791,7 @@
             weight,
         ),
         cost=cost_of(0, 8 << 20),
-    )(grad, gi, cols, other, mix, mix_other)
+    )(grad, gi, cols, other, mix, mix_other, y)
 
 
 def local(
@@ -1729,8 +1817,9 @@
     fast = n_col == 4 and n_row == 4 and dp_count == 2 and micro == 2 and past == 4
 
     tokens = tokens_in.reshape(n_col, rows, feat)
-    inverse = ROPE ** (-(jnp.arange(HD // 2, dtype=F32) * 2.0 / HD))
+    turns = (ROPE ** (-(np.arange(HD // 2) * 2.0 / HD))).astype(np.float32)
     if not fast:
+        inverse = ROPE ** (-(jnp.arange(HD // 2, dtype=F32) * 2.0 / HD))
         heads_t = jnp.transpose(w_heads.reshape(feat, head_local, FAC), (2, 1, 0))
         heads_t = heads_t[jnp.array(FAC_ORDER)].reshape(FAC * head_local, feat)
         pad = jnp.zeros((GROUP_COLS - FAC * head_local, feat), BF)
@@ -1768,7 +1857,7 @@
             heads_out, lse, key_all, value_all, cot_near,
         ) = head_attend(
             tokens, w_ranks.T, w_heads.T, gain_attn.reshape(1, feat), gain_ffn.reshape(1, feat), w_gate.T, w_up.T,
-            w_down, w_out, segments, jnp.concatenate([inverse] * 4).reshape(1, LANES), cot_rows,
+            w_down, w_out, segments, np.tile(turns, 4).reshape(1, LANES), cot_rows,
         )
         mixed, d_mixed, d_heads, g_out, g_gain_two, g_rows, out_pair, hop = middle(
             x_parts, heads_out, mixes, gains, cot_rows, cot_near, ffn_parts, w_rows
@@ -1778,8 +1867,8 @@
             (out_pair, mixed, g_rows, g_out, hop),
             (head_fac, bq_rot, turn, w_rh, h_one, x_parts, gains, d_mixed, g_gain_two),
         )
-        grad_input, g_one, g_two, own_heads, own_ranks, g_out, own_gate, own_up, own_down = layout(
-            g_rh, grad_input, g_cols, cols_other, g_out, out_other, w_heads.shape[1], w_ranks.shape[1], ffn_local
+        output, grad_input, g_one, g_two, own_heads, own_ranks, g_out, own_gate, own_up, own_down = layout(
+            g_rh, grad_input, g_cols, cols_other, g_out, out_other, output, w_heads.shape[1], w_ranks.shape[1], ffn_local
         )
         return (
             output.reshape(tokens_in.shape),

time: 229 us -> 218 us (0.952)
  Pallas kernels: 226 us -> 216 us
    pallas_call x1, Pallas kernels: 89.2 us -> 84.3 us  [back_tail(): pl.pallas_call(back_tail_body, out_shape=(jax.ShapeDtypeStruct(x_parts.sh...]
    pallas_call x1, Pallas kernels: 54.4 us -> 51.3 us  [middle(): pl.pallas_call(middle_body, out_shape=(jax.ShapeDtypeStruct((rows, D), F3...]
where the time goes in v3:
time: 218 us; the launch traced here: 216 us
  Pallas kernels  216 us (99%)
    pallas_call x1, Pallas kernels, back_tail(): pl.pallas_call(back_tail_body, out_shape=(jax.ShapeDtypeStruct(x_parts.sh...  84.3 us
    pallas_call x1, Pallas kernels, head_attend(): pl.pallas_call(head_attend_body, out_shape=outs, in_specs=[VMEM] * 11 + [...  76.4 us
    pallas_call x1, Pallas kernels, middle(): pl.pallas_call(middle_body, out_shape=(jax.ShapeDtypeStruct((rows, D), F3...  51.3 us

profile of v3, /device:TPU:0, one launch (start us, length us, event | category | flops | bytes accessed | tf_op | source)
XLA Modules:
  0.0 216.4 jit_solution(7202806324714586671)
XLA Ops:
  0.6 76.4 %shard_map.195 = (bf16[4,256,256]{2,1,0:T(8,128)(2,1)}, f32[4,8,256]{2,1,0:T(8,128)}, bf16[4,3,96,256]{3,2,1,0:T(8,128)(2,1)}, bf16[4,4,256,256]{3,2,1,0:T(8,128...) custom-call(bf16[4,256,256]{2,1,0:T(8,128)(2,1)} %bitcast.19, ...), custom_call_target="tpu_custom_call" | custom-call | flops 11995709440 | bytes 31457280 | tf_op jit(solution)/shard_map/pallas_call | solution.py:747
  77.0 51.3 %shard_map.196 = (f32[256,1024]{1,0:T(8,128)}, f32[256,1024]{1,0:T(8,128)}, bf16[256,1024]{1,0:T(8,128)(2,1)}, bf16[4,4,256,256]{3,2,1,0:T(8,128)(2,1)}, f32[1,1...) custom-call(bf16[4,256,256]{2,1,0:T(8,128)(2,1)} %get-tuple-element., ...), custom_call_target="tpu_custom_call" | custom-call | flops 14495514624 | bytes 25165824 | tf_op jit(solution)/shard_map/pallas_call | solution.py:1348
  128.3 84.3 %shard_map.197 = (bf16[4,256,256]{2,1,0:T(8,128)(2,1)}, f32[208,256]{1,0:T(8,128)}, bf16[4,256,256]{2,1,0:T(8,128)(2,1)}, bf16[4,3,96,256]{3,2,1,0:T(8,128)(2,1)...) custom-call(bf16[256,1024]{1,0:T(8,128)(2,1)} %get-tuple-element.53.refs_0_, ...), custom_call_target="tpu_custom_call" | custom-call | flops 26843545600 | bytes 41943040 | tf_op jit(solution)/shard_map/pallas_call | solution.py:1676
  212.6 3.8 %shard_map.198 = (bf16[4,256,256]{2,1,0:T(8,128)(2,1)}, f32[4,256,256]{2,1,0:T(8,128)}, f32[1,256]{1,0:T(1,128)}, f32[1,256]{1,0:T(1,128)}, f32[40,256]{1,0:T(8,...) custom-call(f32[208,256]{1,0:T(8,128)} %get-tuple-element.79.grad_re, ...), custom_call_target="tpu_custom_call" | custom-call | bytes 8388608 | tf_op jit(solution)/shard_map/pallas_call | solution.py:1779

commit v4 on v3

--- a/solution.py
+++ b/solution.py
@@ -183,8 +183,7 @@
 
 
 class AttendCopies:
-    def __init__(self, head_end, cot_ref, rows_ref, near_ref, mixes_ref, send_sem, recv_sem):
-        self.head_end = head_end
+    def __init__(self, cot_ref, rows_ref, near_ref, mixes_ref, send_sem, recv_sem):
         row = lax.axis_index("row")
         col, core, across = neighbours()
         dp, (me, on_x, on_y, _) = square()
@@ -495,7 +494,7 @@
     tok_ref, ranks_ref, heads_ref, gain_one_ref, gain_two_ref, gate_ref, up_ref, down_ref, mix_ref, seg_all_ref,
     inverse_ref,
     x_ref, gains_ref, parts_ref, mixes_ref, h_ref, hf_ref, bq_ref, q_ref, w_ref, win_ref, seg_ref, turn_ref, rows_ref,
-    w_own_ref, gain_ref, ffn_ref, blocks_ref, send_sem, recv_sem,
+    w_own_ref, gain_ref, ffn_ref, blocks_ref, send_sem, recv_sem, next_copies,
 ):
     row = lax.axis_index("row")
     col, core, across = neighbours()
@@ -644,6 +643,9 @@
         pass_one.start()
 
     pl.when(hands_on)(two.start)
+    pl.when(row >= 1)(to_right.wait_recv)
+    pl.when(row <= 2)(to_left.wait_recv)
+    next_copies()
     make_queries(hf_ref, bq_ref, q_ref)
 
     @pl.when(has_two)
@@ -665,8 +667,6 @@
     pl.when(hands_on)(two.wait_send)
     pl.when(row <= 2)(to_right.wait_send)
     pl.when(row >= 1)(to_left.wait_send)
-    pl.when(row >= 1)(to_right.wait_recv)
-    pl.when(row <= 2)(to_left.wait_recv)
 
     def end():
         for c in rest:
@@ -689,7 +689,8 @@
     head_out = [kept.get(k, outs[k]) for k in range(13)]
     o_out, lse_ref, k_out, v_out, near_ref = outs[13:]
     mixes_ref, q_ref, win_ref, seg_ref, rows_ref = (head_out[k] for k in (3, 7, 9, 10, 12))
-    end = head_body(*head_in, *head_out, *scratch[:6])
+    side_work = AttendCopies(cot_ref, rows_ref, near_ref, mixes_ref, *scratch[8:10])
+    side_work.head_end = head_body(*head_in, *head_out, *scratch[:6], side_work.first)
     copies = [pltpu.make_async_copy(kept[k], outs[k], keep_sem.at[n]) for n, k in enumerate(KEPT)]
     for k, c in zip(KEPT, copies):
         if k != 3:
@@ -707,8 +708,8 @@
             c.start()
 
     attend_body(
-        True, q_ref, win_ref, seg_ref, end, cot_ref, tiles[0], lse_ref, tiles[1], tiles[2], rows_ref, near_ref,
-        mixes_ref, *scratch[6:10], store=store,
+        True, q_ref, win_ref, seg_ref, tiles[0], lse_ref, tiles[1], tiles[2], *scratch[6:8],
+        store=store, side_work=side_work,
     )
     copies[KEPT.index(3)].start()
     for p in range(PAIRS):
@@ -784,14 +785,8 @@
     return jnp.where(same & (key_idx <= query_idx), 0.0, NEG)
 
 
-def attend_body(fast, q_ref, kf_ref, seg_ref, *refs, store=None):
-    if fast:
-        head_end, cot_ref, o_ref, lse_ref, k_ref, v_ref, w_rows_ref, cot_near_ref, mixes_ref = refs[:9]
-        bias_ref, dup_ref, send_sem, recv_sem = refs[9:]
-        side_work = AttendCopies(head_end, cot_ref, w_rows_ref, cot_near_ref, mixes_ref, send_sem, recv_sem)
-        side_work.first()
-    else:
-        o_ref, lse_ref, k_ref, v_ref, bias_ref, dup_ref = refs
+def attend_body(fast, q_ref, kf_ref, seg_ref, *refs, store=None, side_work=None):
+    o_ref, lse_ref, k_ref, v_ref, bias_ref, dup_ref = refs
     rows = q_ref.shape[0]
     keys = seg_ref.shape[1]
     bias_ref[...] = mask_bias(seg_ref, keys, rows)
@@ -801,8 +796,8 @@
 
     def pair(p, carried):
         if fast:
-            pl.when(p == 2)(side_work.early)
-            pl.when(p == 4)(side_work.second)
+            pl.when(p == 1)(side_work.early)
+            pl.when(p == 3)(side_work.second)
         lanes = pl.ds(pl.multiple_of(p * LANES, LANES), LANES)
         weights = window_lanes(kf_ref, slice(2 * LANES, 3 * LANES))
         made = []
@@ -878,8 +873,8 @@
 
     def pair(p, carried):
         if fast:
-            pl.when(p == 1)(side_work.cross_x)
             pl.when(p == 3)(side_work.second)
+            pl.when(p == 3)(side_work.cross_x)
             pl.when(p == 4)(side_work.last_hop)
             pl.when(p == 6)(side_work.third)
             load(p)

time: 218 us -> 214 us (0.982)
  Pallas kernels: 216 us -> 213 us
    pallas_call x1, Pallas kernels: 76.4 us -> 71.4 us  [head_attend(): pl.pallas_call(head_attend_body, out_shape=outs, in_specs=[VMEM] * 11 + [...]
where the time goes in v4:
time: 214 us
  Pallas kernels  213 us (100%)
    pallas_call x1, Pallas kernels, back_tail(): pl.pallas_call(back_tail_body, out_shape=(jax.ShapeDtypeStruct(x_parts.sh...  85.9 us
    pallas_call x1, Pallas kernels, head_attend(): pl.pallas_call(head_attend_body, out_shape=outs, in_specs=[VMEM] * 11 + [...  71.4 us
    pallas_call x1, Pallas kernels, middle(): pl.pallas_call(middle_body, out_shape=(jax.ShapeDtypeStruct((rows, D), F3...  51.7 us

profile of v4, /device:TPU:0, one launch (start us, length us, event | category | flops | bytes accessed | tf_op | source)
XLA Modules:
  0.0 213.5 jit_solution(6488702657689691780)
XLA Ops:
  0.6 71.4 %shard_map.195 = (bf16[4,256,256]{2,1,0:T(8,128)(2,1)}, f32[4,8,256]{2,1,0:T(8,128)}, bf16[4,3,96,256]{3,2,1,0:T(8,128)(2,1)}, bf16[4,4,256,256]{3,2,1,0:T(8,128...) custom-call(bf16[4,256,256]{2,1,0:T(8,128)(2,1)} %bitcast.19, ...), custom_call_target="tpu_custom_call" | custom-call | flops 11995709440 | bytes 31457280 | tf_op jit(solution)/shard_map/pallas_call | solution.py:748
  72.1 51.7 %shard_map.196 = (f32[256,1024]{1,0:T(8,128)}, f32[256,1024]{1,0:T(8,128)}, bf16[256,1024]{1,0:T(8,128)(2,1)}, bf16[4,4,256,256]{3,2,1,0:T(8,128)(2,1)}, f32[1,1...) custom-call(bf16[4,256,256]{2,1,0:T(8,128)(2,1)} %get-tuple-element., ...), custom_call_target="tpu_custom_call" | custom-call | flops 14495514624 | bytes 25165824 | tf_op jit(solution)/shard_map/pallas_call | solution.py:1343
  123.8 85.9 %shard_map.197 = (bf16[4,256,256]{2,1,0:T(8,128)(2,1)}, f32[208,256]{1,0:T(8,128)}, bf16[4,256,256]{2,1,0:T(8,128)(2,1)}, bf16[4,3,96,256]{3,2,1,0:T(8,128)(2,1)...) custom-call(bf16[256,1024]{1,0:T(8,128)(2,1)} %get-tuple-element.53.refs_0_, ...), custom_call_target="tpu_custom_call" | custom-call | flops 26843545600 | bytes 41943040 | tf_op jit(solution)/shard_map/pallas_call | solution.py:1671
  209.7 3.8 %shard_map.198 = (bf16[4,256,256]{2,1,0:T(8,128)(2,1)}, f32[4,256,256]{2,1,0:T(8,128)}, f32[1,256]{1,0:T(1,128)}, f32[1,256]{1,0:T(1,128)}, f32[40,256]{1,0:T(8,...) custom-call(f32[208,256]{1,0:T(8,128)} %get-tuple-element.79.grad_re, ...), custom_call_target="tpu_custom_call" | custom-call | bytes 8388608 | tf_op jit(solution)/shard_map/pallas_call | solution.py:1774

commit v5 on v4

--- a/solution.py
+++ b/solution.py
@@ -1495,7 +1495,7 @@
     grad_ref, gi_all_ref, cols_ref, cols_other_ref, mix_ref, mix_other_ref,
     d_ref, gi_ref, wnear_ref, wsend_ref, wfar_ref, rows_own_ref, cols_send_ref, mix_got_ref,
     g_ref, near_ref, pair_ref, far_ref, side_ref, down_ref, last_ref, end_ref,
-    send_sem, recv_sem, local_sem,
+    send_sem, recv_sem, local_sem, tail_ref,
 ):
     row = lax.axis_index("row")
     col, core, across = neighbours()
@@ -1553,28 +1553,53 @@
     wsend_ref[0] = jnp.where(hands_on, sent_on + wfar_ref[1].astype(F32), sent_on).astype(BF)
     pl.when(row >= 1)(one.start)
 
-    mixes = [go(part_ref.at[order[k]], mix_got_ref.at[k], row=order[k]) for k in range(3)]
-
     fac_more, folded = query_grads(range(4, RQ), dq, high, low, bq_ref)
     put_query_grads(folded, 4, turn_ref, d_ref)
     for c, source in zip(columns, (across, cross, core)):
         c.wait_recv()
         rest.append(go(cols_ref.at[source], cols_other_ref.at[source], dp=y))
+    split = RQ * HD
+    ranks_each = RANK_COLS // 4
+    d_h = nn(d_ref[:, :split], w_ref[:split])
+    early = tn(d_ref[:, :split], h_ref[...])
+    for r in range(2):
+        for c in range(4):
+            g_ref[r, c, :ranks_each] = early[r * ranks_each : (r + 1) * ranks_each, c * width : (c + 1) * width].astype(BF)
     d_kf = win_ref[4].astype(F32) + jnp.where(left, from_high, zero)
     pl.when(row <= 2)(one.wait_recv)
     d_kf = jnp.where(row <= 2, d_kf + wfar_ref[0].astype(F32), d_kf)
     put_key_grads(d_kf, fac + fac_more, turn_ref, d_ref)
-    d_h = nn(d_ref[...], w_ref[...])
+    mixes = [go(part_ref.at[order[k]], mix_got_ref.at[k], row=order[k]) for k in range(3)]
+    d_h = d_h + nn(d_ref[:, split:], w_ref[split:])
     gains = first_norm_back(d_h, x_ref, gain_ref, d_mixed_ref, gi_ref)
-    factor_weight_grads(d_ref, h_ref, gains, g_two_ref, g_ref)
-
+    for c in range(4):
+        tail_ref[0:1, c * width : (c + 1) * width] = gains[c]
+    tail_ref[1:2] = g_two_ref[...]
+    tail_ref[2:8] = jnp.zeros((6, D), F32)
+    start = 2 * LANES
+    d_late = d_ref[:, start:]
+    used = FAC * GROUP
+
+    def column(c):
+        lanes = pl.ds(pl.multiple_of(c * width, width), width)
+        grad = tn(d_late, h_ref[:, lanes])
+        for r in range(4):
+            at = RANK_COLS + r * GROUP_COLS - start
+            if r >= 2:
+                g_ref[r, c, :ranks_each] = grad[r * ranks_each - start : (r + 1) * ranks_each - start].astype(BF)
+            g_ref[r, c, ranks_each:] = jnp.concatenate([grad[at : at + used], tail_ref[:, lanes]], axis=0).astype(BF)
+
+    column((1 - x) * 2 + 1 - mine)
     first = [go(g_ref.at[r, (1 - x) * 2 + 1 - mine], near_ref.at[0, k], col=core) for k, r in enumerate(order)]
+    column((1 - x) * 2 + mine)
+    column(x * 2 + 1 - mine)
     second = [go(g_ref.at[r, x * 2 + 1 - mine], near_ref.at[1, k], col=core) for k, r in enumerate(order)]
     sides = []
     for k, r in enumerate(order):
         first[k].wait_recv()
         pair_ref[k] = (g_ref[r, (1 - x) * 2 + mine].astype(F32) + near_ref[0, k].astype(F32)).astype(BF)
         sides.append(go(pair_ref.at[k], side_ref.at[k], col=across))
+    column(x * 2 + mine)
 
     total = part_ref[row].astype(F32)
     for k, c in enumerate(mixes):
@@ -1727,6 +1752,7 @@
             pltpu.SemaphoreType.DMA((count,)),
             pltpu.SemaphoreType.DMA((count,)),
             pltpu.SemaphoreType.DMA((2,)),
+            pltpu.VMEM((8, D), F32),
         ]
         + [
             pltpu.VMEM(a.shape, a.dtype)

time: 214 us -> 212 us (level)
  no operation moved by 1% of the time
where the time goes in v5:
time: 212 us
  Pallas kernels  211 us (100%)
    pallas_call x1, Pallas kernels, back_tail(): pl.pallas_call(back_tail_body, out_shape=(jax.ShapeDtypeStruct(x_parts.sh...  84.4 us
    pallas_call x1, Pallas kernels, head_attend(): pl.pallas_call(head_attend_body, out_shape=outs, in_specs=[VMEM] * 11 + [...  71.4 us
    pallas_call x1, Pallas kernels, middle(): pl.pallas_call(middle_body, out_shape=(jax.ShapeDtypeStruct((rows, D), F3...  51.7 us

profile of v5, /device:TPU:0, one launch (start us, length us, event | category | flops | bytes accessed | tf_op | source)
XLA Modules:
  0.0 212.1 jit_solution(6206689686115775484)
XLA Ops:
  0.6 71.4 %shard_map.195 = (bf16[4,256,256]{2,1,0:T(8,128)(2,1)}, f32[4,8,256]{2,1,0:T(8,128)}, bf16[4,3,96,256]{3,2,1,0:T(8,128)(2,1)}, bf16[4,4,256,256]{3,2,1,0:T(8,128...) custom-call(bf16[4,256,256]{2,1,0:T(8,128)(2,1)} %bitcast.19, ...), custom_call_target="tpu_custom_call" | custom-call | flops 11995709440 | bytes 31457280 | tf_op jit(solution)/shard_map/pallas_call | solution.py:748
  72.1 51.7 %shard_map.196 = (f32[256,1024]{1,0:T(8,128)}, f32[256,1024]{1,0:T(8,128)}, bf16[256,1024]{1,0:T(8,128)(2,1)}, bf16[4,4,256,256]{3,2,1,0:T(8,128)(2,1)}, f32[1,1...) custom-call(bf16[4,256,256]{2,1,0:T(8,128)(2,1)} %get-tuple-element., ...), custom_call_target="tpu_custom_call" | custom-call | flops 14495514624 | bytes 25165824 | tf_op jit(solution)/shard_map/pallas_call | solution.py:1343
  123.8 84.4 %shard_map.197 = (bf16[4,256,256]{2,1,0:T(8,128)(2,1)}, f32[208,256]{1,0:T(8,128)}, bf16[4,256,256]{2,1,0:T(8,128)(2,1)}, bf16[4,3,96,256]{3,2,1,0:T(8,128)(2,1)...) custom-call(bf16[256,1024]{1,0:T(8,128)(2,1)} %get-tuple-element.53.refs_0_, ...), custom_call_target="tpu_custom_call" | custom-call | flops 26843545600 | bytes 41943040 | tf_op jit(solution)/shard_map/pallas_call | solution.py:1696
  208.2 3.8 %shard_map.198 = (bf16[4,256,256]{2,1,0:T(8,128)(2,1)}, f32[4,256,256]{2,1,0:T(8,128)}, f32[1,256]{1,0:T(1,128)}, f32[1,256]{1,0:T(1,128)}, f32[40,256]{1,0:T(8,...) custom-call(f32[208,256]{1,0:T(8,128)} %get-tuple-element.79.grad_re, ...), custom_call_target="tpu_custom_call" | custom-call | bytes 8388608 | tf_op jit(solution)/shard_map/pallas_call | solution.py:1800
